TPU v7x, 32 devices: a whole 2x2x4 slice. The times are simulated.
32 devices in a mesh: row: 4 (over z), col: 8 (over y, x, core).
Axes of the slice: x: 2, y: 2, z: 4, core: 2. Of those that a mesh axis runs over, the one named last changes fastest.
Arguments:
- a_vals: bfloat16 [4, 8, 4, 8, 128, 128], P('row', 'col'), may hold values from -0.5 to 0.5
- a_rows: int32 [4, 8, 4, 8], P('row', 'col'), may hold values from 0 to 15
- a_cols: int32 [4, 8, 4, 8], P('row', 'col'), may hold values from 0 to 1
- a_live: int32 [4, 8, 4], P('row', 'col'), may hold values from 1 to 8, as said below
- p_vals: bfloat16 [64, 3, 128, 128], P(('row', 'col')), may hold values from -1 to 1
- p_cols: int32 [64, 3], replicated, may hold values from 0 to 15, as said below
Outputs:
- coarse_op: float32 [16, 16, 128, 128], P('col', 'row')
Inputs may be any that keep to these rules, and one draw needn't show every extreme that they name: Only slots t < a_live[r, c, s] carry blocks of A; the values in the other slots are not part of A. In every draw some grid position has all its sections full. `p_cols`: the 3 coarse block columns of a fine block row i are distinct and lie in the 4 coarse blocks from (i // 16) * 4 on.
All inputs are finite; a program needn't handle non-finite values.
Results may differ from a plain program's by a relative error of at most 0.0029.
Values may be sent and summed in bfloat16 or wider, within the bound.
No kernel may reach another device: no remote copies, remote signals or barrier semaphores. Data moves between devices by JAX's collectives and lax.ppermute only.
A program may use at most 128 MiB of HBM per device.

v0:
```python
import jax
import jax.numpy as jnp
from jax import lax
from jax.sharding import PartitionSpec as P

CROW = 4


def local(a_vals, a_rows, a_cols, a_live, p_vals, p_cols):
    row_count = lax.axis_size("row")
    col_count = lax.axis_size("col")
    grid_row = lax.axis_index("row")
    grid_col = lax.axis_index("col")
    segment = p_vals.shape[0]
    per_row = p_vals.shape[1]
    block_size = p_vals.shape[2]
    slot_count = a_vals.shape[3]
    section_vals = a_vals.reshape(row_count, slot_count, block_size, block_size)
    section_rows = a_rows.reshape(row_count, slot_count)
    section_cols = a_cols.reshape(row_count, slot_count)
    section_live = a_live.reshape(row_count)
    fine_span = segment * col_count
    coarse_total = CROW * row_count
    left_all = lax.all_gather(p_vals, "col", axis=0, tiled=True)
    left_coarse = (
        lax.dynamic_slice_in_dim(p_cols, grid_row * fine_span, fine_span, 0) - grid_row * CROW
    )
    right_coarse = lax.dynamic_index_in_dim(
        p_cols.reshape(row_count, col_count, segment, per_row), grid_col, 1, keepdims=False
    ).reshape(row_count * segment, per_row)
    initial = jnp.zeros((coarse_total, CROW, block_size, block_size), jnp.float32)
    row_labels = lax.iota(jnp.int32, CROW)
    col_labels = lax.iota(jnp.int32, coarse_total)

    def add_slots(partial_value, values, fine_rows, source_index, usable, source, source_coarse):
        right_blocks = jnp.take(source, source_index, axis=0)
        products = jnp.einsum(
            "sij,spjk->spik", values, right_blocks, preferred_element_type=jnp.float32
        )
        products = jnp.where(usable[:, None, None, None], products, 0.0).astype(jnp.bfloat16)
        left_blocks = jnp.take(left_all, fine_rows, axis=0)
        coarse_row = jnp.take(left_coarse, fine_rows, axis=0)
        row_pick = (coarse_row[:, :, None] == row_labels[None, None, :]).astype(jnp.bfloat16)
        folded = jnp.einsum(
            "saq,saji->sqji", row_pick, left_blocks, preferred_element_type=jnp.float32
        ).astype(jnp.bfloat16)
        triple = jnp.einsum(
            "sqji,spjk->spqik", folded, products, preferred_element_type=jnp.float32
        )
        coarse_col = jnp.take(source_coarse, source_index, axis=0)
        col_pick = (coarse_col[:, :, None] == col_labels[None, None, :]).astype(jnp.float32)
        flat_terms = triple.reshape(-1, CROW * block_size * block_size)
        flat_pick = col_pick.reshape(-1, coarse_total)
        added = jnp.einsum("sj,sx->jx", flat_pick, flat_terms, precision=lax.Precision.HIGHEST)
        return partial_value + added.reshape(coarse_total, CROW, block_size, block_size)

    def add_section(partial_value, section_at, source, source_coarse, source_start, piece_len):
        values = lax.dynamic_index_in_dim(section_vals, section_at, 0, keepdims=False)
        fine_rows = lax.dynamic_index_in_dim(section_rows, section_at, 0, keepdims=False)
        fine_cols = lax.dynamic_index_in_dim(section_cols, section_at, 0, keepdims=False)
        live_count = lax.dynamic_index_in_dim(section_live, section_at, 0, keepdims=False)
        target = section_at * segment + fine_cols
        inside = (target >= source_start) & (target < source_start + piece_len)
        source_index = jnp.clip(target - source_start, 0, piece_len - 1)
        position = lax.iota(jnp.int32, slot_count)
        usable = inside & (position < live_count)
        return add_slots(
            partial_value, values, fine_rows, source_index, usable, source, source_coarse
        )

    right_all = lax.all_gather(p_vals, "row", axis=0, tiled=True)

    def whole_section(section_at, running):
        return add_section(running, section_at, right_all, right_coarse, 0, row_count * segment)

    partial_value = lax.fori_loop(0, row_count, whole_section, initial)
    return lax.psum_scatter(partial_value, "col", scatter_dimension=0, tiled=True)


def solution(mesh):
    return jax.shard_map(
        local,
        mesh=mesh,
        in_specs=(
            P("row", "col", None, None, None, None),
            P("row", "col", None, None),
            P("row", "col", None, None),
            P("row", "col", None),
            P(("row", "col"), None, None, None),
            P(),
        ),
        out_specs=P("col", "row", None, None),
        check_vma=False,
    )
```

profile of v0, /device:TPU:0, one launch (start us, length us, event | category | flops | bytes accessed | tf_op | source)
XLA Modules:
  0.0 262.2 jit_solution(9492211815750386809)
XLA Ops:
  6.5 0.7 all-gather.2.cloned.1.call-update
  7.3 0.8 reshape.178
  8.1 0.8 constant_dynamic-slice_fusion.2
  9.1 21.5 %all_gather.6 = bf16[8,3,128,128]{3,2,1,0:T(8,128)(2,1)S(1)} all-gather(bf16[2,3,128,128]{3,2,1,0:T(8,128)(2,1)} %param.12), channel_id=1, replica_groups=mesh['row'=4,'col'=8] {'row'}, dimensions={0}, use_global_device_ids=true | all-gather | bytes 983040 | tf_op jit(solution)/shard_map/all_gather | solution.py:71
  30.6 7.1 %all-gather.2.cloned.1.call-done = bf16[16,3,128,128]{3,2,1,0:T(8,128)(2,1)} async-done(((bf16[2,3,128,128]{3,2,1,0:T(8,128)(2,1)}), bf16[16,3,128,128]{3,2,1,0:T(8,128)(2,1)}) %all-gather.2.cloned.1.call-update) | async-done | bytes 1572880 | tf_op jit(solution)/shard_map/all_gather | solution.py:24
  37.7 160.7 %while.14 = (s32[]{:T(128)}, f32[16,4,128,128]{3,0,2,1:T(8,128)}, s32[4,8]{1,0:T(4,128)}, s32[8,3]{1,0:T(8,128)S(1)}, s32[4]{0:T(128)}, /*index=5*/bf16[8,3,128,...) while((s32[]{:T(128)}, f32[16,4,128,128]{3,0,2,1:T(8,128)}, ...), condition=%wide.region_1.2_spmd.clone, body=%wide.region_0.1_spmd.clone.sunk | while | flops 812649216 | bytes 100935528 | solution.py:76
  37.7 1.2 dynamic_slice.65
  39.6 1.3 bitcast_and_fusion.2
  43.0 2.1 gather_fusion
  45.2 0.8 fusion.57
  46.0 5.0 %convolution_bitcast_fusion.2 = f32[8,3,4,128,128]{3,4,2,1,0:T(8,128)} fusion(bf16[8,4,128,128,1]{3,1,2,0,4:T(4,128)(2,1)S(1)} %fusion.57, bf16[8,3,128,128]{3,2,1,0:T(8,128)(2,1)S(1)} %gather_fusion.2, pred[8]{0:T(512)(128)(4,1)S(1)} %compare_and_fusion.3, pred[8]{0:T(512)(128)(4,1)S(1)} %get-tuple-element.331, ...), kind=kOutput, calls=%fused_computation.9.clone.1 | convolution fusion | flops 504496128 | bytes 8388628 | tf_op jit(solution)/shard_map/while/body/eval_jaxpr/sqji,spjk->spqik/dot_general | solution.py:47
  51.0 6.6 %copy.49 = f32[8,3,4,128,128]{4,3,2,1,0:T(8,128)} copy(f32[8,3,4,128,128]{3,4,2,1,0:T(8,128)} %convolution_bitcast_fusion.2) | data formatting | bytes 12582912 | tf_op jit(solution)/shard_map/while/body/eval_jaxpr/sqji,spjk->spqik/transpose | solution.py:47
  57.6 6.8 %reshape.248 = f32[24,65536]{1,0:T(8,128)} reshape(f32[8,3,4,128,128]{4,3,2,1,0:T(8,128)} %copy.49) | data formatting | bytes 12582912 | tf_op jit(solution)/shard_map/while/body/eval_jaxpr/reshape | solution.py:52
  64.4 4.0 %copy.50 = f32[3,8,512,128]{3,2,1,0:T(8,128)S(1)} copy(f32[3,8,512,128]{3,1,2,0:T(8,128)} %bitcast.89) | data formatting | bytes 12582912 | tf_op jit(solution)/shard_map/while
  68.4 7.4 %select_add_fusion.2 = f32[16,4,128,128]{3,0,2,1:T(8,128)S(1)} fusion(f32[16,4,128,128]{3,0,2,1:T(8,128)S(1)} %copy-done, f32[4,128,128,24]{2,1,0,3:T(8,128)S(1)} %bitcast.90, pred[]{:T(512)S(6)} %compare.3, s32[24]{0:T(128)S(1)} %select_n.169), kind=kOutput, calls=%fused_computation.8.clone.1 | convolution fusion | flops 304087424 | bytes 14680161 | tf_op jit(solution)/shard_map/while/body/eval_jaxpr/sj,sx->jx/dot_general | solution.py:54
  75.9 1.9 copy-done.1
  77.8 1.2 dynamic_slice.65
  79.8 1.3 bitcast_and_fusion.2
  83.1 2.1 gather_fusion
  85.4 0.8 fusion.57
  86.2 5.0 %convolution_bitcast_fusion.2 = f32[8,3,4,128,128]{3,4,2,1,0:T(8,128)} fusion(bf16[8,4,128,128,1]{3,1,2,0,4:T(4,128)(2,1)S(1)} %fusion.57, bf16[8,3,128,128]{3,2,1,0:T(8,128)(2,1)S(1)} %gather_fusion.2, pred[8]{0:T(512)(128)(4,1)S(1)} %compare_and_fusion.3, pred[8]{0:T(512)(128)(4,1)S(1)} %get-tuple-element.331, ...), kind=kOutput, calls=%fused_computation.9.clone.1 | convolution fusion | flops 504496128 | bytes 8388628 | tf_op jit(solution)/shard_map/while/body/eval_jaxpr/sqji,spjk->spqik/dot_general | solution.py:47
  91.2 6.6 %copy.49 = f32[8,3,4,128,128]{4,3,2,1,0:T(8,128)} copy(f32[8,3,4,128,128]{3,4,2,1,0:T(8,128)} %convolution_bitcast_fusion.2) | data formatting | bytes 12582912 | tf_op jit(solution)/shard_map/while/body/eval_jaxpr/sqji,spjk->spqik/transpose | solution.py:47
  97.7 6.8 %reshape.248 = f32[24,65536]{1,0:T(8,128)} reshape(f32[8,3,4,128,128]{4,3,2,1,0:T(8,128)} %copy.49) | data formatting | bytes 12582912 | tf_op jit(solution)/shard_map/while/body/eval_jaxpr/reshape | solution.py:52
  104.6 4.0 %copy.50 = f32[3,8,512,128]{3,2,1,0:T(8,128)S(1)} copy(f32[3,8,512,128]{3,1,2,0:T(8,128)} %bitcast.89) | data formatting | bytes 12582912 | tf_op jit(solution)/shard_map/while
  108.6 7.4 %select_add_fusion.2 = f32[16,4,128,128]{3,0,2,1:T(8,128)S(1)} fusion(f32[16,4,128,128]{3,0,2,1:T(8,128)S(1)} %copy-done, f32[4,128,128,24]{2,1,0,3:T(8,128)S(1)} %bitcast.90, pred[]{:T(512)S(6)} %compare.3, s32[24]{0:T(128)S(1)} %select_n.169), kind=kOutput, calls=%fused_computation.8.clone.1 | convolution fusion | flops 304087424 | bytes 14680161 | tf_op jit(solution)/shard_map/while/body/eval_jaxpr/sj,sx->jx/dot_general | solution.py:54
  116.1 1.9 copy-done.1
  118.0 1.2 dynamic_slice.65
  119.9 1.3 bitcast_and_fusion.2
  123.3 2.1 gather_fusion
  125.6 0.8 fusion.57
  126.4 5.0 %convolution_bitcast_fusion.2 = f32[8,3,4,128,128]{3,4,2,1,0:T(8,128)} fusion(bf16[8,4,128,128,1]{3,1,2,0,4:T(4,128)(2,1)S(1)} %fusion.57, bf16[8,3,128,128]{3,2,1,0:T(8,128)(2,1)S(1)} %gather_fusion.2, pred[8]{0:T(512)(128)(4,1)S(1)} %compare_and_fusion.3, pred[8]{0:T(512)(128)(4,1)S(1)} %get-tuple-element.331, ...), kind=kOutput, calls=%fused_computation.9.clone.1 | convolution fusion | flops 504496128 | bytes 8388628 | tf_op jit(solution)/shard_map/while/body/eval_jaxpr/sqji,spjk->spqik/dot_general | solution.py:47
  131.3 6.6 %copy.49 = f32[8,3,4,128,128]{4,3,2,1,0:T(8,128)} copy(f32[8,3,4,128,128]{3,4,2,1,0:T(8,128)} %convolution_bitcast_fusion.2) | data formatting | bytes 12582912 | tf_op jit(solution)/shard_map/while/body/eval_jaxpr/sqji,spjk->spqik/transpose | solution.py:47
  137.9 6.8 %reshape.248 = f32[24,65536]{1,0:T(8,128)} reshape(f32[8,3,4,128,128]{4,3,2,1,0:T(8,128)} %copy.49) | data formatting | bytes 12582912 | tf_op jit(solution)/shard_map/while/body/eval_jaxpr/reshape | solution.py:52
  144.8 4.0 %copy.50 = f32[3,8,512,128]{3,2,1,0:T(8,128)S(1)} copy(f32[3,8,512,128]{3,1,2,0:T(8,128)} %bitcast.89) | data formatting | bytes 12582912 | tf_op jit(solution)/shard_map/while
  148.8 7.4 %select_add_fusion.2 = f32[16,4,128,128]{3,0,2,1:T(8,128)S(1)} fusion(f32[16,4,128,128]{3,0,2,1:T(8,128)S(1)} %copy-done, f32[4,128,128,24]{2,1,0,3:T(8,128)S(1)} %bitcast.90, pred[]{:T(512)S(6)} %compare.3, s32[24]{0:T(128)S(1)} %select_n.169), kind=kOutput, calls=%fused_computation.8.clone.1 | convolution fusion | flops 304087424 | bytes 14680161 | tf_op jit(solution)/shard_map/while/body/eval_jaxpr/sj,sx->jx/dot_general | solution.py:54
  156.3 1.9 copy-done.1
  158.2 1.2 dynamic_slice.65
  160.1 1.3 bitcast_and_fusion.2
  163.5 2.1 gather_fusion
  165.7 0.8 fusion.57
  166.5 5.0 %convolution_bitcast_fusion.2 = f32[8,3,4,128,128]{3,4,2,1,0:T(8,128)} fusion(bf16[8,4,128,128,1]{3,1,2,0,4:T(4,128)(2,1)S(1)} %fusion.57, bf16[8,3,128,128]{3,2,1,0:T(8,128)(2,1)S(1)} %gather_fusion.2, pred[8]{0:T(512)(128)(4,1)S(1)} %compare_and_fusion.3, pred[8]{0:T(512)(128)(4,1)S(1)} %get-tuple-element.331, ...), kind=kOutput, calls=%fused_computation.9.clone.1 | convolution fusion | flops 504496128 | bytes 8388628 | tf_op jit(solution)/shard_map/while/body/eval_jaxpr/sqji,spjk->spqik/dot_general | solution.py:47
  171.5 6.6 %copy.49 = f32[8,3,4,128,128]{4,3,2,1,0:T(8,128)} copy(f32[8,3,4,128,128]{3,4,2,1,0:T(8,128)} %convolution_bitcast_fusion.2) | data formatting | bytes 12582912 | tf_op jit(solution)/shard_map/while/body/eval_jaxpr/sqji,spjk->spqik/transpose | solution.py:47
  178.1 6.8 %reshape.248 = f32[24,65536]{1,0:T(8,128)} reshape(f32[8,3,4,128,128]{4,3,2,1,0:T(8,128)} %copy.49) | data formatting | bytes 12582912 | tf_op jit(solution)/shard_map/while/body/eval_jaxpr/reshape | solution.py:52
  184.9 4.0 %copy.50 = f32[3,8,512,128]{3,2,1,0:T(8,128)S(1)} copy(f32[3,8,512,128]{3,1,2,0:T(8,128)} %bitcast.89) | data formatting | bytes 12582912 | tf_op jit(solution)/shard_map/while
  189.0 7.4 %select_add_fusion.2 = f32[16,4,128,128]{3,0,2,1:T(8,128)S(1)} fusion(f32[16,4,128,128]{3,0,2,1:T(8,128)S(1)} %copy-done, f32[4,128,128,24]{2,1,0,3:T(8,128)S(1)} %bitcast.90, pred[]{:T(512)S(6)} %compare.3, s32[24]{0:T(128)S(1)} %select_n.169), kind=kOutput, calls=%fused_computation.8.clone.1 | convolution fusion | flops 304087424 | bytes 14680161 | tf_op jit(solution)/shard_map/while/body/eval_jaxpr/sj,sx->jx/dot_general | solution.py:54
  196.4 1.9 copy-done.1
  198.3 5.5 %copy.22 = f32[16,4,128,128]{3,2,1,0:T(8,128)} copy(f32[16,4,128,128]{3,0,2,1:T(8,128)} %get-tuple-element.204) | data formatting | bytes 8388608 | tf_op jit(solution)/shard_map/while | solution.py:76
  203.9 51.5 %reduce-scatter.2.cloned.1.call-done = f32[2,4,128,128]{3,2,1,0:T(8,128)} async-done(((f32[16,4,128,128]{3,2,1,0:T(8,128)}), f32[2,4,128,128]{3,2,1,0:T(8,128)}) %reduce-scatter.2.cloned.1.call-update) | async-done | bytes 524304 | tf_op jit(solution)/shard_map/reduce_scatter | solution.py:77
  (68 shorter events, 11.9 us)
Async XLA Ops:
  6.5 31.1 %all-gather.2.cloned.1.call-start = ((), (), s32[]{:S(2)}) async-start(), calls=%async_computation.1 | async-start | bytes 1769472 | tf_op jit(solution)/shard_map/all_gather | solution.py:24
  7.3 248.1 %reduce-scatter.2.cloned.1.call-start = ((), (), s32[]{:S(2)}) async-start(), calls=%async_computation.2 | async-start | bytes 4718592 | tf_op jit(solution)/shard_map/reduce_scatter | solution.py:77
  64.4 4.0 %copy-start = (f32[16,4,128,128]{3,0,2,1:T(8,128)S(1)}, f32[16,4,128,128]{3,0,2,1:T(8,128)}, u32[]{:S(2)}) copy-start(f32[16,4,128,128]{3,0,2,1:T(8,128)} %get-tuple-element.346) | copy-start | bytes 12582916 | tf_op jit(solution)/shard_map/while
  75.9 1.9 copy-start.1
  104.6 4.0 %copy-start = (f32[16,4,128,128]{3,0,2,1:T(8,128)S(1)}, f32[16,4,128,128]{3,0,2,1:T(8,128)}, u32[]{:S(2)}) copy-start(f32[16,4,128,128]{3,0,2,1:T(8,128)} %get-tuple-element.346) | copy-start | bytes 12582916 | tf_op jit(solution)/shard_map/while
  116.1 1.9 copy-start.1
  144.8 4.0 %copy-start = (f32[16,4,128,128]{3,0,2,1:T(8,128)S(1)}, f32[16,4,128,128]{3,0,2,1:T(8,128)}, u32[]{:S(2)}) copy-start(f32[16,4,128,128]{3,0,2,1:T(8,128)} %get-tuple-element.346) | copy-start | bytes 12582916 | tf_op jit(solution)/shard_map/while
  156.2 1.9 copy-start.1
  184.9 4.0 %copy-start = (f32[16,4,128,128]{3,0,2,1:T(8,128)S(1)}, f32[16,4,128,128]{3,0,2,1:T(8,128)}, u32[]{:S(2)}) copy-start(f32[16,4,128,128]{3,0,2,1:T(8,128)} %get-tuple-element.346) | copy-start | bytes 12582916 | tf_op jit(solution)/shard_map/while
  196.4 1.9 copy-start.1
Sparse Core Ops, SparseCore 0:
  9.2 28.3 all-gather.1
  204.0 51.3 reduce-scatter.1
where the time goes:
time: 263 us; the launch traced here: 262 us
  local copies, waits for them, and re-layouts  106 us (40%)
  waiting for transfers between devices  59.3 us (23%)
  matrix products  52.8 us (20%)
  blocking collectives  21.5 us (8%)
  between operations  13.4 us (5%)
  other arithmetic  9.08 us (3%)
    reduce_scatter x1, waiting for transfers between devices, local(): lax.psum_scatter(partial_value, 'col', scatter_dimension=0, tiled=True)  51.5 us
    dot_general x4, matrix products, add_slots(): jnp.einsum('sj,sx->jx', flat_pick, flat_terms, precision=lax.Precision.HI...  29.8 us
    reshape x4, local copies, waits for them, and re-layouts, add_slots(): flat_terms = triple.reshape(-1, CROW * block_size * block_size)  27.4 us
    transpose x4, local copies, waits for them, and re-layouts, add_slots(): jnp.einsum('sqji,spjk->spqik', folded, products, preferred_element_type=j...  26.3 us
    while x20, local copies, waits for them, and re-layouts  23.8 us
    all_gather x1, blocking collectives, local(): right_all = lax.all_gather(p_vals, 'row', axis=0, tiled=True)  21.5 us
    dot_general x4, matrix products, add_slots(): jnp.einsum('sqji,spjk->spqik', folded, products, preferred_element_type=j...  19.9 us
    gather x4, local copies, waits for them, and re-layouts, add_slots(): left_blocks = jnp.take(left_all, fine_rows, axis=0)  8.43 us
  transfers between devices with their start and end apart: 2, of which 2 were waited for; matrix products, arithmetic and copies ran while one was open for 1% of the time, Pallas kernels for 0%

commit v1 on v0

v1 whole, which is shorter than its diff:
```python
import functools

import jax
import jax.numpy as jnp
from jax import lax
from jax.experimental import pallas as pl
from jax.experimental.pallas import tpu as pltpu
from jax.sharding import PartitionSpec as P

CROW = 4
HALF = 2


def fold_left(sizes, info, pcols, *refs):
    pieces, out = refs[:-1], refs[-1]
    _, segment, per_row, block = sizes
    grid_row, grid_col = info[0], info[1]
    fine_span = segment * len(pieces)
    for b, piece in enumerate(pieces):
        for seg in range(segment):
            i = lax.bitwise_xor(grid_col, b) * segment + seg
            base = (grid_row * fine_span + i) * per_row
            used = 0
            for q in range(per_row):
                coarse = pcols[base + q] - grid_row * CROW
                used = used + coarse
                out[i, coarse] = jnp.transpose(piece[seg, q])
            out[i, CROW * (CROW - 1) // 2 - used] = jnp.zeros((block, block), out.dtype)


def section(sizes, hop, info, pcols, own_a, other_a, left, *refs):
    slots, segment, per_row, block = sizes
    pieces, (out, a_buf, r_buf, folded, lhs, rhs, sems) = refs[:-7], refs[-7:]
    row_count = len(pieces) // 2
    grid_row, grid_col = info[0], info[1]
    chip, core = grid_col // 2, grid_col % 2
    sec = lax.bitwise_xor(chip, hop)
    dist = lax.bitwise_xor(sec, grid_row)
    copies = [
        pltpu.make_async_copy(own_a.at[sec], a_buf.at[0], sems.at[0]),
        pltpu.make_async_copy(other_a.at[sec], a_buf.at[1], sems.at[1]),
    ]
    for copy in copies:
        copy.start()
    for d in range(row_count):

        @pl.when(dist == d)
        def _():
            two = [
                pltpu.make_async_copy(pieces[2 * d + u], r_buf.at[u], sems.at[2 + u])
                for u in range(2)
            ]
            for copy in two:
                copy.start()
            for copy in two:
                copy.wait()

    for u in range(2):
        col = lax.bitwise_xor(grid_col, u)
        for seg in range(segment):
            k = (sec * 2 * row_count + col) * segment + seg
            cols = [pcols[k * per_row + p] for p in range(per_row)]
            for jj in range(HALF):
                want = sec * CROW + core * HALF + jj
                at = jnp.int32(0)
                found = cols[0] == want
                for p in range(1, per_row):
                    at = jnp.where(cols[p] == want, p, at)
                    found = found | (cols[p] == want)
                blk = r_buf[u, seg, at]
                folded[u * segment + seg, :, jj * block : (jj + 1) * block] = jnp.where(
                    found, blk, jnp.zeros_like(blk)
                )
    for copy in copies:
        copy.wait()
    for u in range(2):
        for t in range(slots):
            code = info[2 + (u * row_count + sec) * slots + t]
            live = code >= 0
            code = jnp.maximum(code, 0)
            n = u * slots + t
            product = jnp.dot(
                a_buf[u, t],
                folded[u * segment + code % segment],
                preferred_element_type=jnp.float32,
            )
            rhs[n * block : (n + 1) * block, :] = jnp.where(live, product, 0.0).astype(rhs.dtype)
            lhs[:, n * block : (n + 1) * block] = left[code // segment].reshape(CROW * block, block)
    acc = jnp.dot(lhs[...], rhs[...], preferred_element_type=jnp.float32)
    for jj in range(HALF):
        for i in range(CROW):
            out[jj, i] = acc[
                i * block : (i + 1) * block, jj * block : (jj + 1) * block
            ].astype(out.dtype)


def local(a_vals, a_rows, a_cols, a_live, p_vals, p_cols):
    row_count = lax.axis_size("row")
    col_count = lax.axis_size("col")
    assert col_count == 2 * row_count
    grid_row = lax.axis_index("row")
    grid_col = lax.axis_index("col")
    segment, per_row, block = p_vals.shape[0], p_vals.shape[1], p_vals.shape[2]
    slots = a_vals.shape[3]
    sizes = (slots, segment, per_row, block)

    def col_xor(x, b):
        return lax.ppermute(x, "col", [(c, c ^ b) for c in range(col_count)])

    def row_xor(x, b):
        return lax.ppermute(x, "row", [(r, r ^ b) for r in range(row_count)])

    own_a = a_vals.reshape(row_count, slots, block, block)
    position = lax.iota(jnp.int32, slots)[None, :]
    codes = jnp.where(
        position < a_live.reshape(row_count, 1),
        a_rows.reshape(row_count, slots) * segment + a_cols.reshape(row_count, slots),
        -1,
    )
    right_far = [row_xor(p_vals, d) for d in range(1, row_count)]
    left_far = [col_xor(p_vals, 2 * e) for e in range(1, row_count)]
    other_p = col_xor(p_vals, 1)
    other_a = col_xor(own_a, 1)
    other_codes = col_xor(codes, 1)
    left = [p_vals, other_p]
    for piece in left_far:
        left += [piece, col_xor(piece, 1)]
    right = [p_vals, other_p]
    for piece in right_far:
        right += [piece, col_xor(piece, 1)]
    info = jnp.concatenate(
        [jnp.stack([grid_row, grid_col]), codes.reshape(-1), other_codes.reshape(-1)]
    )
    pcols = p_cols.reshape(-1)
    smem = pl.BlockSpec(memory_space=pltpu.SMEM)
    vmem = pl.BlockSpec(memory_space=pltpu.VMEM)
    hbm = pl.BlockSpec(memory_space=pl.ANY)
    fine = segment * col_count
    folded_left = pl.pallas_call(
        functools.partial(fold_left, sizes),
        out_shape=jax.ShapeDtypeStruct((fine, CROW, block, block), jnp.bfloat16),
        in_specs=[smem, smem] + [vmem] * col_count,
        out_specs=vmem,
        compiler_params=pltpu.CompilerParams(vmem_limit_bytes=16 << 20),
        cost_estimate=pl.CostEstimate(flops=0, bytes_accessed=4 << 20, transcendentals=0),
        name="fold_left",
    )(info, pcols, *left)
    depth = 2 * slots * block

    def partial_of(hop, dtype):
        return pl.pallas_call(
            functools.partial(section, sizes, hop),
            out_shape=jax.ShapeDtypeStruct((HALF, CROW, block, block), dtype),
            in_specs=[smem, smem, hbm, hbm, vmem] + [hbm] * len(right),
            out_specs=vmem,
            scratch_shapes=[
                pltpu.VMEM((2, slots, block, block), jnp.bfloat16),
                pltpu.VMEM((2, segment, per_row, block, block), jnp.bfloat16),
                pltpu.VMEM((2 * segment, block, HALF * block), jnp.bfloat16),
                pltpu.VMEM((CROW * block, depth), jnp.bfloat16),
                pltpu.VMEM((depth, HALF * block), jnp.bfloat16),
                pltpu.SemaphoreType.DMA((4,)),
            ],
            compiler_params=pltpu.CompilerParams(vmem_limit_bytes=24 << 20),
            cost_estimate=pl.CostEstimate(
                flops=2 * CROW * block * depth * HALF * block,
                bytes_accessed=4 << 20,
                transcendentals=0,
            ),
            name="section",
        )(info, pcols, own_a, other_a, folded_left, *right)

    arrived = []
    for hop in range(row_count - 1, 0, -1):
        arrived.append(col_xor(partial_of(hop, jnp.bfloat16), 2 * hop))
    total = partial_of(0, jnp.float32)
    for piece in arrived:
        total = total + piece.astype(jnp.float32)
    return total


def solution(mesh):
    return jax.shard_map(
        local,
        mesh=mesh,
        in_specs=(
            P("row", "col", None, None, None, None),
            P("row", "col", None, None),
            P("row", "col", None, None),
            P("row", "col", None),
            P(("row", "col"), None, None, None),
            P(),
        ),
        out_specs=P("col", "row", None, None),
        check_vma=False,
    )
```

time: 263 us -> 54.9 us (0.21)
  local copies, waits for them, and re-layouts: 106 us -> 3.69 us
  matrix products: 52.8 us -> 0 us
  waiting for transfers between devices: 59.3 us -> 20.6 us
  blocking collectives: 21.5 us -> 0 us
  starting transfers between devices: 0.04 us -> 16.7 us
  between operations: 13.4 us -> 0.13 us
  Pallas kernels: 0 us -> 11.1 us
  other arithmetic: 9.08 us -> 2.49 us
    dot_general x12 -> x0, matrix products: 52.8 us -> none  [the longest x4 29.8 us: add_slots(): jnp.einsum('sj,sx->jx', flat_pick, flat_terms, precision=lax.Precision.HI...]
    reduce_scatter x1 -> x0, waiting for transfers between devices: 51.5 us -> none  [local(): lax.psum_scatter(partial_value, 'col', scatter_dimension=0, tiled=True)]
    while x21 -> x0, local copies, waits for them, and re-layouts: 29.3 us -> none
    reshape x5 -> x2, local copies, waits for them, and re-layouts: 28.2 us -> 0.22 us  [the longest x1 0.13 us: local(): pcols = p_cols.reshape(-1)]
    transpose x4 -> x0, local copies, waits for them, and re-layouts: 26.3 us -> none  [add_slots(): jnp.einsum('sqji,spjk->spqik', folded, products, preferred_element_type=j...]
    all_gather x1 -> x0, blocking collectives: 21.5 us -> none  [local(): right_all = lax.all_gather(p_vals, 'row', axis=0, tiled=True)]
    ppermute x0 -> x18, waiting for transfers between devices: none -> 20.6 us  [the longest x3 11.5 us: row_xor(): return lax.ppermute(x, 'row', [(r, r ^ b) for r in range(row_count)])]
    ppermute x0 -> x18, starting transfers between devices: none -> 16.7 us  [the longest x15 11.5 us: col_xor(): return lax.ppermute(x, 'col', [(c, c ^ b) for c in range(col_count)])]
  transfers between devices with their start and end apart: 2 -> 18, of which waited for: 2 -> 7; matrix products, arithmetic and copies ran while one was open for 1% -> 5% of each run, Pallas kernels for 0% -> 16%
where the time goes in v1:
time: 54.9 us; the launch traced here: 54.7 us
  waiting for transfers between devices  20.6 us (38%)
  starting transfers between devices  16.7 us (30%)
  Pallas kernels  11.1 us (20%)
  local copies, waits for them, and re-layouts  3.69 us (7%)
  other arithmetic  2.49 us (5%)
    ppermute x15, starting transfers between devices, col_xor(): return lax.ppermute(x, 'col', [(c, c ^ b) for c in range(col_count)])  11.5 us
    ppermute x3, waiting for transfers between devices, row_xor(): return lax.ppermute(x, 'row', [(r, r ^ b) for r in range(row_count)])  11.5 us
    pallas_call x4, Pallas kernels, partial_of(): pl.pallas_call(functools.partial(section, sizes, hop), out_shape=jax.Shap...  9.31 us
    ppermute x15, waiting for transfers between devices, col_xor(): return lax.ppermute(x, 'col', [(c, c ^ b) for c in range(col_count)])  9.1 us
    ppermute x3, starting transfers between devices, row_xor(): return lax.ppermute(x, 'row', [(r, r ^ b) for r in range(row_count)])  5.23 us
    unnamed x11, local copies, waits for them, and re-layouts  3.31 us
    pallas_call x1, Pallas kernels, local(): pl.pallas_call(functools.partial(fold_left, sizes), out_shape=jax.ShapeDt...  1.78 us
  transfers between devices with their start and end apart: 18, of which 7 were waited for; matrix products, arithmetic and copies ran while one was open for 5% of the time, Pallas kernels for 16%

profile of v1, /device:TPU:0, one launch (start us, length us, event | category | flops | bytes accessed | tf_op | source)
XLA Modules:
  0.0 54.7 jit_solution(9827763116374845102)
XLA Ops:
  0.0 0.5 collective-permute-start.1
  0.5 4.7 %collective-permute-start.13 = (bf16[2,3,128,128]{3,2,1,0:T(8,128)(2,1)}, bf16[2,3,128,128]{3,2,1,0:T(8,128)(2,1)S(1)}, u32[]{:S(2)}, u32[]{:S(2)}) collective-permute-start(bf16[2,3,128,128]{3,2,1,0:T(8,128)(2,1)} %refs_0_.9), channel_id=1, source_target_pairs={{0,24},{8,16},{16,8},{24,0},{1,25},{9,17},{17,9},{25,1},{2,26},{10... | collective-permute-start | bytes 589832 | tf_op jit(solution)/shard_map/ppermute | solution.py:111
  5.1 0.0 collective-permute-start.11
  5.1 0.8 %bitcast_select_fusion = (s32[4,8]{1,0:T(4,128)S(1)}, s32[1,1,4,8]{3,2,1,0:T(4,128)S(1)}) fusion(s32[4]{0:T(128)} %bitcast.11, s32[1,1,4,8]{3,2,1,0:T(4,128)} %param.8, s32[1,1,4,8]{3,2,1,0:T(4,128)} %param.7), kind=kLoop, calls=%fused_computation.1 | loop fusion | flops 128 | bytes 528 | tf_op jit(solution)/shard_map/jit(_where)/select_n | solution.py:115
  5.9 0.2 collective-permute-start
  6.1 0.6 %collective-permute-start.9 = (bf16[2,3,128,128]{3,2,1,0:T(8,128)(2,1)}, bf16[2,3,128,128]{3,2,1,0:T(8,128)(2,1)S(1)}, u32[]{:S(2)}, u32[]{:S(2)}) collective-permute-start(bf16[2,3,128,128]{3,2,1,0:T(8,128)(2,1)} %refs_0_.9), channel_id=1, source_target_pairs={{0,8},{8,0},{16,24},{24,16},{1,9},{9,1},{17,25},{25,17},{2,10},{10... | collective-permute-start | bytes 589832 | tf_op jit(solution)/shard_map/ppermute | solution.py:111
  6.6 0.4 collective-permute-done
  7.1 2.4 %collective-permute-start.7 = (bf16[2,3,128,128]{3,2,1,0:T(8,128)(2,1)}, bf16[2,3,128,128]{3,2,1,0:T(8,128)(2,1)S(1)}, u32[]{:S(2)}, u32[]{:S(2)}) collective-permute-start(bf16[2,3,128,128]{3,2,1,0:T(8,128)(2,1)} %refs_0_.9), channel_id=1, source_target_pairs={{0,6},{1,7},{2,4},{3,5},{4,2},{5,3},{6,0},{7,1},{8,14},{9,15},{10,... | collective-permute-start | bytes 589832 | tf_op jit(solution)/shard_map/ppermute | solution.py:108
  9.5 1.7 %collective-permute-done.13.refs_6_ = bf16[2,3,128,128]{3,2,1,0:T(8,128)(2,1)S(1)} collective-permute-done((bf16[2,3,128,128]{3,2,1,0:T(8,128)(2,1)}, bf16[2,3,128,128]{3,2,1,0:T(8,128)(2,1)S(1)}, u32[]{:S(2)}, u32[]{:S(2)}) %collective-permute-start.13) | collective-permute-done | bytes 196640 | tf_op jit(solution)/shard_map/ppermute | solution.py:111
  11.2 1.7 %collective-permute-start.5 = (bf16[2,3,128,128]{3,2,1,0:T(8,128)(2,1)}, bf16[2,3,128,128]{3,2,1,0:T(8,128)(2,1)}, u32[]{:S(2)}, u32[]{:S(2)}) collective-permute-start(bf16[2,3,128,128]{3,2,1,0:T(8,128)(2,1)} %refs_0_.9), channel_id=1, source_target_pairs={{0,4},{1,5},{2,6},{3,7},{4,0},{5,1},{6,2},{7,3},{8,12},{9,13},{10,... | collective-permute-start | bytes 589832 | tf_op jit(solution)/shard_map/ppermute | solution.py:108
  12.8 9.8 %collective-permute-done.11.refs_4_ = bf16[2,3,128,128]{3,2,1,0:T(8,128)(2,1)S(1)} collective-permute-done((bf16[2,3,128,128]{3,2,1,0:T(8,128)(2,1)}, bf16[2,3,128,128]{3,2,1,0:T(8,128)(2,1)S(1)}, u32[]{:S(2)}, u32[]{:S(2)}) %collective-permute-start.11) | collective-permute-done | bytes 196640 | tf_op jit(solution)/shard_map/ppermute | solution.py:111
  22.6 1.5 %collective-permute-start.3 = (bf16[2,3,128,128]{3,2,1,0:T(8,128)(2,1)}, bf16[2,3,128,128]{3,2,1,0:T(8,128)(2,1)}, u32[]{:S(2)}, u32[]{:S(2)}) collective-permute-start(bf16[2,3,128,128]{3,2,1,0:T(8,128)(2,1)} %refs_0_.9), channel_id=1, source_target_pairs={{0,2},{1,3},{2,0},{3,1},{4,6},{5,7},{6,4},{7,5},{8,10},{9,11},{10,... | collective-permute-start | bytes 589832 | tf_op jit(solution)/shard_map/ppermute | solution.py:108
  24.1 0.0 collective-permute-done.9.refs_2_
  24.1 0.0 collective-permute-start.2
  24.1 0.0 collective-permute-done.7.refs_6_
  24.1 0.5 collective-permute-start.8
  24.6 0.7 %copy-done.3 = bf16[2,3,128,128]{3,2,1,0:T(8,128)(2,1)} copy-done((bf16[2,3,128,128]{3,2,1,0:T(8,128)(2,1)}, bf16[2,3,128,128]{3,2,1,0:T(8,128)(2,1)S(1)}, u32[]{:S(2)}) %copy-start.3) | copy-done | bytes 196632
  25.3 0.0 collective-permute-done.5.refs_4_
  25.3 0.1 collective-permute-start.6
  25.4 0.7 %iota_compare_fusion = pred[4,8]{1,0:T(4,128)(4,1)S(1)} fusion(s32[4]{0:T(128)} %bitcast.12), kind=kLoop, calls=%fused_computation.3 | loop fusion | flops 32 | bytes 48 | tf_op jit(solution)/shard_map/lt | solution.py:116
  26.1 0.1 lt.23
  26.2 0.1 add.20
  26.3 3.1 %collective-permute-done.3.refs_2_ = bf16[2,3,128,128]{3,2,1,0:T(8,128)(2,1)} collective-permute-done((bf16[2,3,128,128]{3,2,1,0:T(8,128)(2,1)}, bf16[2,3,128,128]{3,2,1,0:T(8,128)(2,1)}, u32[]{:S(2)}, u32[]{:S(2)}) %collective-permute-start.3) | collective-permute-done | bytes 196640 | tf_op jit(solution)/shard_map/ppermute | solution.py:108
  29.4 0.0 collective-permute-start.14
  29.4 0.0 collective-permute-done.2.refs_1_
  29.4 0.5 collective-permute-start.12
  29.9 0.0 collective-permute-done.8.refs_7_
  29.9 0.1 collective-permute-start.10
  30.0 0.0 collective-permute-done.6.refs_5_
  30.0 0.4 collective-permute-start.4
  30.5 0.8 %copy.7 = s32[64,3]{1,0:T(8,128)S(1)} copy(s32[64,3]{0,1:T(4,128)} %param.11) | data formatting | bytes 1536 | tf_op args[5]
  31.2 0.1 reshape.26.pcols
  31.4 0.1 reshape.25
  31.4 0.1 pad_add_fusion.info
  31.5 0.5 collective-permute-done.4.refs_3_
  32.0 0.9 %copy-done.1 = bf16[2,3,128,128]{3,2,1,0:T(8,128)(2,1)S(1)} copy-done((bf16[2,3,128,128]{3,2,1,0:T(8,128)(2,1)S(1)}, bf16[2,3,128,128]{3,2,1,0:T(8,128)(2,1)}, u32[]{:S(2)}) %copy-start.1) | copy-done | bytes 196632
  33.0 0.9 %copy-done.4 = bf16[2,3,128,128]{3,2,1,0:T(8,128)(2,1)S(1)} copy-done((bf16[2,3,128,128]{3,2,1,0:T(8,128)(2,1)S(1)}, bf16[2,3,128,128]{3,2,1,0:T(8,128)(2,1)}, u32[]{:S(2)}) %copy-start.4) | copy-done | bytes 196632
  33.9 1.8 %fold_left.1.left = bf16[16,4,128,128]{3,2,1,0:T(8,128)(2,1)S(1)} custom-call(s32[66]{0:T(128)S(1)} %pad_add_fusion.info, s32[192]{0:T(256)S(1)} %reshape.26.pcols, bf16[2,3,128,128]{3,2,1,0:T(8,128)(2,1)S(1)} %copy-done.1, bf16[2,3,128,128]{3,2,1,0:T(8,128)(2,1)S(1)} %collective-permute-done.2.refs_1_, ...), custom_call_target="tpu_custom_call" | custom-call | bytes 4194304 | tf_op jit(solution)/shard_map/fold_left/pallas_call | solution.py:139
  35.7 2.3 %section.5 = bf16[2,4,128,128]{3,2,1,0:T(8,128)(2,1)S(1)} custom-call(s32[66]{0:T(128)S(1)} %pad_add_fusion.info, s32[192]{0:T(256)S(1)} %reshape.26.pcols, bf16[4,8,128,128]{3,2,1,0:T(8,128)(2,1)S(1)} %bitcast.7, bf16[4,8,128,128]{3,2,1,0:T(8,128)(2,1)S(1)} %collective-permute-done.1.other_a, bf16[16,4,128,128]{3,2,1,0:T(8,128)(2,1)S(1)} %fold_left.1.left, ...), custom_call_target="tpu_custom_call" | custom-call | flops 536870912 | bytes 4194304 | tf_op jit(solution)/shard_map/section/pallas_call | solution.py:151
  38.1 2.5 %collective-permute-start.15 = (bf16[2,4,128,128]{3,2,1,0:T(8,128)(2,1)S(1)}, bf16[2,4,128,128]{3,2,1,0:T(8,128)(2,1)S(1)}, u32[]{:S(2)}, u32[]{:S(2)}) collective-permute-start(bf16[2,4,128,128]{3,2,1,0:T(8,128)(2,1)S(1)} %section.5), channel_id=1, source_target_pairs={{0,6},{1,7},{2,4},{3,5},{4,2},{5,3},{6,0},{7,1},{8,14},{9,15},{10,... | collective-permute-start | bytes 786440 | tf_op jit(solution)/shard_map/ppermute | solution.py:108
  40.6 2.3 %section.6 = bf16[2,4,128,128]{3,2,1,0:T(8,128)(2,1)S(1)} custom-call(s32[66]{0:T(128)S(1)} %pad_add_fusion.info, s32[192]{0:T(256)S(1)} %reshape.26.pcols, bf16[4,8,128,128]{3,2,1,0:T(8,128)(2,1)S(1)} %bitcast.8, bf16[4,8,128,128]{3,2,1,0:T(8,128)(2,1)S(1)} %collective-permute-done.1.other_a, bf16[16,4,128,128]{3,2,1,0:T(8,128)(2,1)S(1)} %fold_left.1.left, ...), custom_call_target="tpu_custom_call" | custom-call | flops 536870912 | bytes 4194304 | tf_op jit(solution)/shard_map/section/pallas_call | solution.py:151
  42.9 0.6 %collective-permute-start.16 = (bf16[2,4,128,128]{3,2,1,0:T(8,128)(2,1)S(1)}, bf16[2,4,128,128]{3,2,1,0:T(8,128)(2,1)S(1)}, u32[]{:S(2)}, u32[]{:S(2)}) collective-permute-start(bf16[2,4,128,128]{3,2,1,0:T(8,128)(2,1)S(1)} %section.6), channel_id=1, source_target_pairs={{0,4},{1,5},{2,6},{3,7},{4,0},{5,1},{6,2},{7,3},{8,12},{9,13},{10,... | collective-permute-start | bytes 786440 | tf_op jit(solution)/shard_map/ppermute | solution.py:108
  43.5 2.3 %section.7 = bf16[2,4,128,128]{3,2,1,0:T(8,128)(2,1)S(1)} custom-call(s32[66]{0:T(128)S(1)} %pad_add_fusion.info, s32[192]{0:T(256)S(1)} %reshape.26.pcols, bf16[4,8,128,128]{3,2,1,0:T(8,128)(2,1)S(1)} %bitcast.9, bf16[4,8,128,128]{3,2,1,0:T(8,128)(2,1)S(1)} %collective-permute-done.1.other_a, bf16[16,4,128,128]{3,2,1,0:T(8,128)(2,1)S(1)} %fold_left.1.left, ...), custom_call_target="tpu_custom_call" | custom-call | flops 536870912 | bytes 4194304 | tf_op jit(solution)/shard_map/section/pallas_call | solution.py:151
  45.8 0.6 %collective-permute-start.17 = (bf16[2,4,128,128]{3,2,1,0:T(8,128)(2,1)S(1)}, bf16[2,4,128,128]{3,2,1,0:T(8,128)(2,1)S(1)}, u32[]{:S(2)}, u32[]{:S(2)}) collective-permute-start(bf16[2,4,128,128]{3,2,1,0:T(8,128)(2,1)S(1)} %section.7), channel_id=1, source_target_pairs={{0,2},{1,3},{2,0},{3,1},{4,6},{5,7},{6,4},{7,5},{8,10},{9,11},{10,... | collective-permute-start | bytes 786440 | tf_op jit(solution)/shard_map/ppermute | solution.py:108
  46.4 2.3 %section.4 = f32[2,4,128,128]{3,2,1,0:T(8,128)S(1)} custom-call(s32[66]{0:T(128)S(1)} %pad_add_fusion.info, s32[192]{0:T(256)S(1)} %reshape.26.pcols, bf16[4,8,128,128]{3,2,1,0:T(8,128)(2,1)S(1)} %bitcast.10, bf16[4,8,128,128]{3,2,1,0:T(8,128)(2,1)S(1)} %collective-permute-done.1.other_a, bf16[16,4,128,128]{3,2,1,0:T(8,128)(2,1)S(1)} %fold_left.1.left, ...), custom_call_target="tpu_custom_call" | custom-call | flops 536870912 | bytes 4194304 | tf_op jit(solution)/shard_map/section/pallas_call | solution.py:151
  48.8 4.3 %collective-permute-done.16 = bf16[2,4,128,128]{3,2,1,0:T(8,128)(2,1)S(1)} collective-permute-done((bf16[2,4,128,128]{3,2,1,0:T(8,128)(2,1)S(1)}, bf16[2,4,128,128]{3,2,1,0:T(8,128)(2,1)S(1)}, u32[]{:S(2)}, u32[]{:S(2)}) %collective-permute-start.16) | collective-permute-done | bytes 262176 | tf_op jit(solution)/shard_map/ppermute | solution.py:108
  53.1 0.7 %collective-permute-done.17 = bf16[2,4,128,128]{3,2,1,0:T(8,128)(2,1)S(1)} collective-permute-done((bf16[2,4,128,128]{3,2,1,0:T(8,128)(2,1)S(1)}, bf16[2,4,128,128]{3,2,1,0:T(8,128)(2,1)S(1)}, u32[]{:S(2)}, u32[]{:S(2)}) %collective-permute-start.17) | collective-permute-done | bytes 262176 | tf_op jit(solution)/shard_map/ppermute | solution.py:108
  53.8 0.9 %convert_add_fusion = f32[2,4,128,128]{3,2,1,0:T(8,128)} fusion(bf16[2,4,128,128]{3,2,1,0:T(8,128)(2,1)S(1)} %collective-permute-done.17, bf16[2,4,128,128]{3,2,1,0:T(8,128)(2,1)S(1)} %collective-permute-done.16, f32[2,4,128,128]{3,2,1,0:T(8,128)S(1)} %section.4, bf16[2,4,128,128]{3,2,1,0:T(8,128)(2,1)S(1)} %collective-permute-done.15), kind=kLoop, calls=%fused_computation | loop fusion | flops 786432 | bytes 1835008 | tf_op jit(solution)/shard_map/add | solution.py:178
  (13 shorter events, 0.0 us)
Async XLA Ops:
  0.0 35.7 %copy-start = (bf16[1,1,4,8,128,128]{5,4,3,2,1,0:T(8,128)(2,1)S(1)}, bf16[1,1,4,8,128,128]{5,4,3,2,1,0:T(8,128)(2,1)}, u32[]{:S(2)}) copy-start(bf16[1,1,4,8,128,128]{5,4,3,2,1,0:T(8,128)(2,1)} %param.6) | copy-start | bytes 3145732
  0.0 35.7 %collective-permute-start.1 = (bf16[4,8,128,128]{3,2,1,0:T(8,128)(2,1)}, bf16[4,8,128,128]{3,2,1,0:T(8,128)(2,1)S(1)}, u32[]{:S(2)}, u32[]{:S(2)}) collective-permute-start(bf16[4,8,128,128]{3,2,1,0:T(8,128)(2,1)} %bitcast.6), channel_id=1, source_target_pairs={{0,1},{1,0},{2,3},{3,2},{4,5},{5,4},{6,7},{7,6},{8,9},{9,8},{10,11... | collective-permute-start | bytes 3145736 | tf_op jit(solution)/shard_map/ppermute | solution.py:108
  0.5 10.7 %collective-permute-start.13 = (bf16[2,3,128,128]{3,2,1,0:T(8,128)(2,1)}, bf16[2,3,128,128]{3,2,1,0:T(8,128)(2,1)S(1)}, u32[]{:S(2)}, u32[]{:S(2)}) collective-permute-start(bf16[2,3,128,128]{3,2,1,0:T(8,128)(2,1)} %refs_0_.9), channel_id=1, source_target_pairs={{0,24},{8,16},{16,8},{24,0},{1,25},{9,17},{17,9},{25,1},{2,26},{10... | collective-permute-start | bytes 589832 | tf_op jit(solution)/shard_map/ppermute | solution.py:111
  5.1 17.5 %collective-permute-start.11 = (bf16[2,3,128,128]{3,2,1,0:T(8,128)(2,1)}, bf16[2,3,128,128]{3,2,1,0:T(8,128)(2,1)S(1)}, u32[]{:S(2)}, u32[]{:S(2)}) collective-permute-start(bf16[2,3,128,128]{3,2,1,0:T(8,128)(2,1)} %refs_0_.9), channel_id=1, source_target_pairs={{0,16},{8,24},{16,0},{24,8},{1,17},{9,25},{17,1},{25,9},{2,18},{10... | collective-permute-start | bytes 589832 | tf_op jit(solution)/shard_map/ppermute | solution.py:111
  5.9 1.2 %collective-permute-start = (s32[4,8]{1,0:T(4,128)S(1)}, s32[4,8]{1,0:T(4,128)S(1)}, u32[]{:S(2)}, u32[]{:S(2)}) collective-permute-start(s32[4,8]{1,0:T(4,128)S(1)} %get-tuple-element.5), channel_id=1, source_target_pairs={{0,1},{1,0},{2,3},{3,2},{4,5},{5,4},{6,7},{7,6},{8,9},{9,8},{10,11... | collective-permute-start | bytes 392 | tf_op jit(solution)/shard_map/ppermute | solution.py:108
  6.1 18.1 %collective-permute-start.9 = (bf16[2,3,128,128]{3,2,1,0:T(8,128)(2,1)}, bf16[2,3,128,128]{3,2,1,0:T(8,128)(2,1)S(1)}, u32[]{:S(2)}, u32[]{:S(2)}) collective-permute-start(bf16[2,3,128,128]{3,2,1,0:T(8,128)(2,1)} %refs_0_.9), channel_id=1, source_target_pairs={{0,8},{8,0},{16,24},{24,16},{1,9},{9,1},{17,25},{25,17},{2,10},{10... | collective-permute-start | bytes 589832 | tf_op jit(solution)/shard_map/ppermute | solution.py:111
  7.1 17.1 %collective-permute-start.7 = (bf16[2,3,128,128]{3,2,1,0:T(8,128)(2,1)}, bf16[2,3,128,128]{3,2,1,0:T(8,128)(2,1)S(1)}, u32[]{:S(2)}, u32[]{:S(2)}) collective-permute-start(bf16[2,3,128,128]{3,2,1,0:T(8,128)(2,1)} %refs_0_.9), channel_id=1, source_target_pairs={{0,6},{1,7},{2,4},{3,5},{4,2},{5,3},{6,0},{7,1},{8,14},{9,15},{10,... | collective-permute-start | bytes 589832 | tf_op jit(solution)/shard_map/ppermute | solution.py:108
  11.2 14.1 %collective-permute-start.5 = (bf16[2,3,128,128]{3,2,1,0:T(8,128)(2,1)}, bf16[2,3,128,128]{3,2,1,0:T(8,128)(2,1)}, u32[]{:S(2)}, u32[]{:S(2)}) collective-permute-start(bf16[2,3,128,128]{3,2,1,0:T(8,128)(2,1)} %refs_0_.9), channel_id=1, source_target_pairs={{0,4},{1,5},{2,6},{3,7},{4,0},{5,1},{6,2},{7,3},{8,12},{9,13},{10,... | collective-permute-start | bytes 589832 | tf_op jit(solution)/shard_map/ppermute | solution.py:108
  22.6 6.8 %collective-permute-start.3 = (bf16[2,3,128,128]{3,2,1,0:T(8,128)(2,1)}, bf16[2,3,128,128]{3,2,1,0:T(8,128)(2,1)}, u32[]{:S(2)}, u32[]{:S(2)}) collective-permute-start(bf16[2,3,128,128]{3,2,1,0:T(8,128)(2,1)} %refs_0_.9), channel_id=1, source_target_pairs={{0,2},{1,3},{2,0},{3,1},{4,6},{5,7},{6,4},{7,5},{8,10},{9,11},{10,... | collective-permute-start | bytes 589832 | tf_op jit(solution)/shard_map/ppermute | solution.py:108
  24.1 5.3 %collective-permute-start.2 = (bf16[2,3,128,128]{3,2,1,0:T(8,128)(2,1)}, bf16[2,3,128,128]{3,2,1,0:T(8,128)(2,1)S(1)}, u32[]{:S(2)}, u32[]{:S(2)}) collective-permute-start(bf16[2,3,128,128]{3,2,1,0:T(8,128)(2,1)} %refs_0_.9), channel_id=1, source_target_pairs={{0,1},{1,0},{2,3},{3,2},{4,5},{5,4},{6,7},{7,6},{8,9},{9,8},{10,11... | collective-permute-start | bytes 589832 | tf_op jit(solution)/shard_map/ppermute | solution.py:108
  24.1 5.8 %collective-permute-start.8 = (bf16[2,3,128,128]{3,2,1,0:T(8,128)(2,1)S(1)}, bf16[2,3,128,128]{3,2,1,0:T(8,128)(2,1)}, u32[]{:S(2)}, u32[]{:S(2)}) collective-permute-start(bf16[2,3,128,128]{3,2,1,0:T(8,128)(2,1)S(1)} %collective-permute-done.7.refs_6_), channel_id=1, source_target_pairs={{0,1},{1,0},{2,3},{3,2},{4,5},{5,4},{6,7},{7,6},{8,9},{9,8},{10,11... | collective-permute-start | bytes 589832 | tf_op jit(solution)/shard_map/ppermute | solution.py:108
  24.6 0.7 %copy-start.3 = (bf16[2,3,128,128]{3,2,1,0:T(8,128)(2,1)}, bf16[2,3,128,128]{3,2,1,0:T(8,128)(2,1)S(1)}, u32[]{:S(2)}) copy-start(bf16[2,3,128,128]{3,2,1,0:T(8,128)(2,1)S(1)} %collective-permute-done.7.refs_6_) | copy-start | bytes 589828
  25.3 4.7 %collective-permute-start.6 = (bf16[2,3,128,128]{3,2,1,0:T(8,128)(2,1)}, bf16[2,3,128,128]{3,2,1,0:T(8,128)(2,1)}, u32[]{:S(2)}, u32[]{:S(2)}) collective-permute-start(bf16[2,3,128,128]{3,2,1,0:T(8,128)(2,1)} %collective-permute-done.5.refs_4_), channel_id=1, source_target_pairs={{0,1},{1,0},{2,3},{3,2},{4,5},{5,4},{6,7},{7,6},{8,9},{9,8},{10,11... | collective-permute-start | bytes 589832 | tf_op jit(solution)/shard_map/ppermute | solution.py:108
  29.4 6.3 %collective-permute-start.14 = (bf16[2,3,128,128]{3,2,1,0:T(8,128)(2,1)S(1)}, bf16[2,3,128,128]{3,2,1,0:T(8,128)(2,1)S(1)}, u32[]{:S(2)}, u32[]{:S(2)}) collective-permute-start(bf16[2,3,128,128]{3,2,1,0:T(8,128)(2,1)S(1)} %collective-permute-done.13.refs_6_), channel_id=1, source_target_pairs={{0,1},{1,0},{2,3},{3,2},{4,5},{5,4},{6,7},{7,6},{8,9},{9,8},{10,11... | collective-permute-start | bytes 589832 | tf_op jit(solution)/shard_map/ppermute | solution.py:108
  29.4 6.3 %collective-permute-start.12 = (bf16[2,3,128,128]{3,2,1,0:T(8,128)(2,1)S(1)}, bf16[2,3,128,128]{3,2,1,0:T(8,128)(2,1)S(1)}, u32[]{:S(2)}, u32[]{:S(2)}) collective-permute-start(bf16[2,3,128,128]{3,2,1,0:T(8,128)(2,1)S(1)} %collective-permute-done.11.refs_4_), channel_id=1, source_target_pairs={{0,1},{1,0},{2,3},{3,2},{4,5},{5,4},{6,7},{7,6},{8,9},{9,8},{10,11... | collective-permute-start | bytes 589832 | tf_op jit(solution)/shard_map/ppermute | solution.py:108
  29.9 5.8 %collective-permute-start.10 = (bf16[2,3,128,128]{3,2,1,0:T(8,128)(2,1)S(1)}, bf16[2,3,128,128]{3,2,1,0:T(8,128)(2,1)S(1)}, u32[]{:S(2)}, u32[]{:S(2)}) collective-permute-start(bf16[2,3,128,128]{3,2,1,0:T(8,128)(2,1)S(1)} %collective-permute-done.9.refs_2_), channel_id=1, source_target_pairs={{0,1},{1,0},{2,3},{3,2},{4,5},{5,4},{6,7},{7,6},{8,9},{9,8},{10,11... | collective-permute-start | bytes 589832 | tf_op jit(solution)/shard_map/ppermute | solution.py:108
  30.0 2.0 %collective-permute-start.4 = (bf16[2,3,128,128]{3,2,1,0:T(8,128)(2,1)}, bf16[2,3,128,128]{3,2,1,0:T(8,128)(2,1)}, u32[]{:S(2)}, u32[]{:S(2)}) collective-permute-start(bf16[2,3,128,128]{3,2,1,0:T(8,128)(2,1)} %collective-permute-done.3.refs_2_), channel_id=1, source_target_pairs={{0,1},{1,0},{2,3},{3,2},{4,5},{5,4},{6,7},{7,6},{8,9},{9,8},{10,11... | collective-permute-start | bytes 589832 | tf_op jit(solution)/shard_map/ppermute | solution.py:108
  32.0 0.9 %copy-start.1 = (bf16[2,3,128,128]{3,2,1,0:T(8,128)(2,1)S(1)}, bf16[2,3,128,128]{3,2,1,0:T(8,128)(2,1)}, u32[]{:S(2)}) copy-start(bf16[2,3,128,128]{3,2,1,0:T(8,128)(2,1)} %refs_0_.9) | copy-start | bytes 589828
  33.0 0.9 %copy-start.4 = (bf16[2,3,128,128]{3,2,1,0:T(8,128)(2,1)S(1)}, bf16[2,3,128,128]{3,2,1,0:T(8,128)(2,1)}, u32[]{:S(2)}) copy-start(bf16[2,3,128,128]{3,2,1,0:T(8,128)(2,1)} %copy-done.3) | copy-start | bytes 589828
  33.9 1.8 %copy-start.2 = (bf16[2,3,128,128]{3,2,1,0:T(8,128)(2,1)S(1)}, bf16[2,3,128,128]{3,2,1,0:T(8,128)(2,1)}, u32[]{:S(2)}) copy-start(bf16[2,3,128,128]{3,2,1,0:T(8,128)(2,1)} %refs_0_.9) | copy-start | bytes 589828
  38.1 10.7 %collective-permute-start.15 = (bf16[2,4,128,128]{3,2,1,0:T(8,128)(2,1)S(1)}, bf16[2,4,128,128]{3,2,1,0:T(8,128)(2,1)S(1)}, u32[]{:S(2)}, u32[]{:S(2)}) collective-permute-start(bf16[2,4,128,128]{3,2,1,0:T(8,128)(2,1)S(1)} %section.5), channel_id=1, source_target_pairs={{0,6},{1,7},{2,4},{3,5},{4,2},{5,3},{6,0},{7,1},{8,14},{9,15},{10,... | collective-permute-start | bytes 786440 | tf_op jit(solution)/shard_map/ppermute | solution.py:108
  42.9 10.2 %collective-permute-start.16 = (bf16[2,4,128,128]{3,2,1,0:T(8,128)(2,1)S(1)}, bf16[2,4,128,128]{3,2,1,0:T(8,128)(2,1)S(1)}, u32[]{:S(2)}, u32[]{:S(2)}) collective-permute-start(bf16[2,4,128,128]{3,2,1,0:T(8,128)(2,1)S(1)} %section.6), channel_id=1, source_target_pairs={{0,4},{1,5},{2,6},{3,7},{4,0},{5,1},{6,2},{7,3},{8,12},{9,13},{10,... | collective-permute-start | bytes 786440 | tf_op jit(solution)/shard_map/ppermute | solution.py:108
  45.8 7.9 %collective-permute-start.17 = (bf16[2,4,128,128]{3,2,1,0:T(8,128)(2,1)S(1)}, bf16[2,4,128,128]{3,2,1,0:T(8,128)(2,1)S(1)}, u32[]{:S(2)}, u32[]{:S(2)}) collective-permute-start(bf16[2,4,128,128]{3,2,1,0:T(8,128)(2,1)S(1)} %section.7), channel_id=1, source_target_pairs={{0,2},{1,3},{2,0},{3,1},{4,6},{5,7},{6,4},{7,5},{8,10},{9,11},{10,... | collective-permute-start | bytes 786440 | tf_op jit(solution)/shard_map/ppermute | solution.py:108

commit v2 on v1

v2 whole, which is shorter than its diff:
```python
import functools

import jax
import jax.numpy as jnp
from jax import lax
from jax.experimental import pallas as pl
from jax.experimental.pallas import tpu as pltpu
from jax.sharding import PartitionSpec as P

CROW = 4
HALF = 2


def fold_left(sizes, hop, info, *refs):
    pieces, out = refs[:2], refs[-1]
    slots, segment, per_row, block = sizes
    table = 2 + slots * out.shape[0] // segment
    grid_row, grid_col = info[0], info[1]
    for u, piece in enumerate(pieces):
        for seg in range(segment):
            i = lax.bitwise_xor(grid_col, 2 * hop + u) * segment + seg
            base = table + (grid_row * out.shape[0] + i) * per_row
            used = 0
            for q in range(per_row):
                coarse = info[base + q] - grid_row * CROW
                used = used + coarse
                out[i, coarse] = jnp.transpose(piece[seg, q])
            out[i, CROW * (CROW - 1) // 2 - used] = jnp.zeros((block, block), out.dtype)


def section(sizes, hop, info, own_a, other_a, left, *refs):
    slots, segment, per_row, block = sizes
    pieces, (out, folded, lhs, rhs) = refs[:-4], refs[-4:]
    row_count = len(pieces) // 2
    table = 2 + slots * len(pieces)
    grid_row, grid_col = info[0], info[1]
    chip, core = grid_col // 2, grid_col % 2
    sec = lax.bitwise_xor(chip, hop)
    dist = lax.bitwise_xor(sec, grid_row)
    for d in range(row_count):

        @pl.when(dist == d)
        def _():
            for u in range(2):
                col = lax.bitwise_xor(grid_col, u)
                for seg in range(segment):
                    k = (sec * 2 * row_count + col) * segment + seg
                    cols = [info[table + k * per_row + p] for p in range(per_row)]
                    for jj in range(HALF):
                        want = sec * CROW + core * HALF + jj
                        at = jnp.int32(0)
                        found = cols[0] == want
                        for p in range(1, per_row):
                            at = jnp.where(cols[p] == want, p, at)
                            found = found | (cols[p] == want)
                        blk = pieces[2 * d + u][seg, at]
                        folded[u * segment + seg, :, jj * block : (jj + 1) * block] = jnp.where(
                            found, blk, jnp.zeros_like(blk)
                        )

    for u in range(2):
        for t in range(slots):
            code = info[2 + (u * row_count + sec) * slots + t]
            live = code >= 0
            code = jnp.maximum(code, 0)
            n = u * slots + t
            product = jnp.dot(
                (own_a, other_a)[u][sec, t],
                folded[u * segment + code % segment],
                preferred_element_type=jnp.float32,
            )
            rhs[n * block : (n + 1) * block, :] = jnp.where(live, product, 0.0).astype(rhs.dtype)
            lhs[:, n * block : (n + 1) * block] = left[code // segment].reshape(CROW * block, block)
    acc = jnp.dot(lhs[...], rhs[...], preferred_element_type=jnp.float32)
    for jj in range(HALF):
        for i in range(CROW):
            out[jj, i] = acc[
                i * block : (i + 1) * block, jj * block : (jj + 1) * block
            ].astype(out.dtype)


def local(a_vals, a_rows, a_cols, a_live, p_vals, p_cols):
    row_count = lax.axis_size("row")
    col_count = lax.axis_size("col")
    assert col_count == 2 * row_count
    grid_row = lax.axis_index("row")
    grid_col = lax.axis_index("col")
    segment, per_row, block = p_vals.shape[0], p_vals.shape[1], p_vals.shape[2]
    slots = a_vals.shape[3]
    sizes = (slots, segment, per_row, block)

    def col_xor(x, b):
        return lax.ppermute(x, "col", [(c, c ^ b) for c in range(col_count)])

    def row_xor(x, b):
        return lax.ppermute(x, "row", [(r, r ^ b) for r in range(row_count)])

    own_a = a_vals.reshape(row_count, slots, block, block)
    position = lax.iota(jnp.int32, slots)[None, :]
    codes = jnp.where(
        position < a_live.reshape(row_count, 1),
        a_rows.reshape(row_count, slots) * segment + a_cols.reshape(row_count, slots),
        -1,
    )
    right = [p_vals] + [None] * (row_count - 1)
    for d in sorted(range(1, row_count), key=lambda d: (d.bit_count(), -d)):
        right[d] = row_xor(right[d & (d - 1)], d & -d)
    other_codes = col_xor(codes, 1)
    info = jnp.concatenate(
        [
            jnp.stack([grid_row, grid_col]),
            codes.reshape(-1),
            other_codes.reshape(-1),
            p_cols.reshape(-1),
        ]
    )
    near_p, info, other_p, other_a = lax.optimization_barrier(
        (p_vals, info, col_xor(p_vals, 1), col_xor(own_a, 1))
    )
    left = [p_vals] + [col_xor(near_p, 2 * e) for e in range(1, row_count)]
    right = [half for piece in right[1:] for half in (piece, col_xor(piece, 1))]
    right = [p_vals, other_p] + right
    smem = pl.BlockSpec(memory_space=pltpu.SMEM)
    vmem = pl.BlockSpec(memory_space=pltpu.VMEM)
    hbm = pl.BlockSpec(memory_space=pl.ANY)
    folded_left = ()
    for hop in [*range(1, row_count), 0]:
        pair = (left[hop], col_xor(left[hop], 1) if hop else other_p)
        folded_left = (
            pl.pallas_call(
                functools.partial(fold_left, sizes, hop),
                out_shape=jax.ShapeDtypeStruct(
                    (segment * col_count, CROW, block, block), jnp.bfloat16
                ),
                in_specs=[smem, vmem, vmem] + [hbm] * len(folded_left),
                out_specs=vmem,
                input_output_aliases={3: 0} if folded_left else {},
                compiler_params=pltpu.CompilerParams(vmem_limit_bytes=8 << 20),
                cost_estimate=pl.CostEstimate(
                    flops=0, bytes_accessed=1 << 20, transcendentals=0
                ),
                name="fold_left",
            )(info, *pair, *folded_left),
        )
    (folded_left,) = folded_left
    depth = 2 * slots * block

    def partial_of(hop, dtype):
        return pl.pallas_call(
            functools.partial(section, sizes, hop),
            out_shape=jax.ShapeDtypeStruct((HALF, CROW, block, block), dtype),
            in_specs=[smem] + [vmem] * (3 + len(right)),
            out_specs=vmem,
            scratch_shapes=[
                pltpu.VMEM((2 * segment, block, HALF * block), jnp.bfloat16),
                pltpu.VMEM((CROW * block, depth), jnp.bfloat16),
                pltpu.VMEM((depth, HALF * block), jnp.bfloat16),
            ],
            compiler_params=pltpu.CompilerParams(vmem_limit_bytes=16 << 20),
            cost_estimate=pl.CostEstimate(
                flops=2 * CROW * block * depth * HALF * block,
                bytes_accessed=4 << 20,
                transcendentals=0,
            ),
            name="section",
        )(info, own_a, other_a, folded_left, *right)

    arrived = []
    for hop in range(row_count - 1, 0, -1):
        arrived.append(col_xor(partial_of(hop, jnp.bfloat16), 2 * hop))
    total = partial_of(0, jnp.float32)
    for piece in arrived:
        total = total + piece.astype(jnp.float32)
    return total


def solution(mesh):
    return jax.shard_map(
        local,
        mesh=mesh,
        in_specs=(
            P("row", "col", None, None, None, None),
            P("row", "col", None, None),
            P("row", "col", None, None),
            P("row", "col", None),
            P(("row", "col"), None, None, None),
            P(),
        ),
        out_specs=P("col", "row", None, None),
        check_vma=False,
    )
```

time: 54.9 us -> 44.4 us (0.81)
  waiting for transfers between devices: 20.6 us -> 14.6 us
  local copies, waits for them, and re-layouts: 3.69 us -> 1.89 us
  starting transfers between devices: 16.7 us -> 15.3 us
  Pallas kernels: 11.1 us -> 9.91 us
    ppermute x3, waiting for transfers between devices: 11.5 us -> 3.17 us  [row_xor(): return lax.ppermute(x, 'row', [(r, r ^ b) for r in range(row_count)])]
    ppermute x15, starting transfers between devices: 11.5 us -> 8.84 us  [col_xor(): return lax.ppermute(x, 'col', [(c, c ^ b) for c in range(col_count)])]
    ppermute x15, waiting for transfers between devices: 9.1 us -> 11.4 us  [col_xor(): return lax.ppermute(x, 'col', [(c, c ^ b) for c in range(col_count)])]
    pallas_call x4, Pallas kernels: 9.31 us -> 7.04 us  [partial_of(): pl.pallas_call(functools.partial(section, sizes, hop), out_shape=jax.Shap...]
    unnamed x11 -> x5, local copies, waits for them, and re-layouts: 3.31 us -> 1.43 us
    ppermute x3, starting transfers between devices: 5.23 us -> 6.41 us  [row_xor(): return lax.ppermute(x, 'row', [(r, r ^ b) for r in range(row_count)])]
    pallas_call x1 -> x4, Pallas kernels: 1.78 us -> 2.87 us  [local(): pl.pallas_call(functools.partial(fold_left, sizes, hop), out_shape=jax.Sh...]
  transfers between devices with their start and end apart: 18 -> 18, of which waited for: 7 -> 7; matrix products, arithmetic and copies ran while one was open for 5% -> 6% of each run, Pallas kernels for 16% -> 18%
where the time goes in v2:
time: 44.4 us; the launch traced here: 44.2 us
  starting transfers between devices  15.3 us (34%)
  waiting for transfers between devices  14.6 us (33%)
  Pallas kernels  9.91 us (22%)
  other arithmetic  2.42 us (5%)
  local copies, waits for them, and re-layouts  1.89 us (4%)
    ppermute x15, waiting for transfers between devices, col_xor(): return lax.ppermute(x, 'col', [(c, c ^ b) for c in range(col_count)])  11.4 us
    ppermute x15, starting transfers between devices, col_xor(): return lax.ppermute(x, 'col', [(c, c ^ b) for c in range(col_count)])  8.84 us
    pallas_call x4, Pallas kernels, partial_of(): pl.pallas_call(functools.partial(section, sizes, hop), out_shape=jax.Shap...  7.04 us
    ppermute x3, starting transfers between devices, row_xor(): return lax.ppermute(x, 'row', [(r, r ^ b) for r in range(row_count)])  6.41 us
    ppermute x3, waiting for transfers between devices, row_xor(): return lax.ppermute(x, 'row', [(r, r ^ b) for r in range(row_count)])  3.17 us
    pallas_call x4, Pallas kernels, local(): pl.pallas_call(functools.partial(fold_left, sizes, hop), out_shape=jax.Sh...  2.87 us
    unnamed x5, local copies, waits for them, and re-layouts  1.43 us
    add x1, other arithmetic, local(): total = total + piece.astype(jnp.float32)  0.9 us
  transfers between devices with their start and end apart: 18, of which 7 were waited for; matrix products, arithmetic and copies ran while one was open for 6% of the time, Pallas kernels for 18%

profile of v2, /device:TPU:0, one launch (start us, length us, event | category | flops | bytes accessed | tf_op | source)
XLA Modules:
  0.0 44.2 jit_solution(1703469160734462124)
XLA Ops:
  0.0 0.5 %collective-permute-start.2 = (bf16[4,8,128,128]{3,2,1,0:T(8,128)(2,1)}, bf16[4,8,128,128]{3,2,1,0:T(8,128)(2,1)S(1)}, u32[]{:S(2)}, u32[]{:S(2)}) collective-permute-start(bf16[4,8,128,128]{3,2,1,0:T(8,128)(2,1)} %bitcast.6), channel_id=1, source_target_pairs={{0,1},{1,0},{2,3},{3,2},{4,5},{5,4},{6,7},{7,6},{8,9},{9,8},{10,11... | collective-permute-start | bytes 3145736 | tf_op jit(solution)/shard_map/ppermute | solution.py:93
  0.5 0.1 collective-permute-start.1
  0.5 4.0 %collective-permute-start.11 = (bf16[2,3,128,128]{3,2,1,0:T(8,128)(2,1)}, bf16[2,3,128,128]{3,2,1,0:T(8,128)(2,1)S(1)}, u32[]{:S(2)}, u32[]{:S(2)}) collective-permute-start(bf16[2,3,128,128]{3,2,1,0:T(8,128)(2,1)} %refs_0_.9), channel_id=1, source_target_pairs={{0,16},{8,24},{16,0},{24,8},{1,17},{9,25},{17,1},{25,9},{2,18},{10... | collective-permute-start | bytes 589832 | tf_op jit(solution)/shard_map/ppermute | solution.py:96
  4.5 0.8 %bitcast_select_fusion = (s32[4,8]{1,0:T(4,128)S(1)}, s32[1,1,4,8]{3,2,1,0:T(4,128)S(1)}) fusion(s32[4]{0:T(128)} %bitcast.11, s32[1,1,4,8]{3,2,1,0:T(4,128)} %param.8, s32[1,1,4,8]{3,2,1,0:T(4,128)} %param.7), kind=kLoop, calls=%fused_computation.1 | loop fusion | flops 128 | bytes 528 | tf_op jit(solution)/shard_map/jit(_where)/select_n | solution.py:100
  5.3 0.0 collective-permute-start
  5.3 0.1 add.20
  5.4 0.7 %iota_compare_fusion = pred[4,8]{1,0:T(4,128)(4,1)S(1)} fusion(s32[4]{0:T(128)} %bitcast.12), kind=kLoop, calls=%fused_computation.3 | loop fusion | flops 32 | bytes 48 | tf_op jit(solution)/shard_map/lt | solution.py:101
  6.1 0.1 lt.23
  6.2 0.8 %copy.10 = s32[64,3]{1,0:T(8,128)S(1)} copy(s32[64,3]{0,1:T(4,128)} %param.11) | data formatting | bytes 1536 | tf_op args[5]
  7.0 0.1 reshape.26
  7.2 0.0 collective-permute-done
  7.2 0.1 reshape.25
  7.2 0.1 concatenate.3.info
  7.3 0.0 collective-permute-done.1.refs_1_
  7.3 0.0 collective-permute-done.2.other_a
  7.3 1.6 %collective-permute-start.7 = (bf16[2,3,128,128]{3,2,1,0:T(8,128)(2,1)}, bf16[2,3,128,128]{3,2,1,0:T(8,128)(2,1)S(1)}, u32[]{:S(2)}, u32[]{:S(2)}) collective-permute-start(bf16[2,3,128,128]{3,2,1,0:T(8,128)(2,1)} %refs_0_.9), channel_id=1, source_target_pairs={{0,2},{1,3},{2,0},{3,1},{4,6},{5,7},{6,4},{7,5},{8,10},{9,11},{10,... | collective-permute-start | bytes 589832 | tf_op jit(solution)/shard_map/ppermute | solution.py:93
  8.9 1.5 %collective-permute-start.5 = (bf16[2,3,128,128]{3,2,1,0:T(8,128)(2,1)}, bf16[2,3,128,128]{3,2,1,0:T(8,128)(2,1)S(1)}, u32[]{:S(2)}, u32[]{:S(2)}) collective-permute-start(bf16[2,3,128,128]{3,2,1,0:T(8,128)(2,1)} %refs_0_.9), channel_id=1, source_target_pairs={{0,4},{1,5},{2,6},{3,7},{4,0},{5,1},{6,2},{7,3},{8,12},{9,13},{10,... | collective-permute-start | bytes 589832 | tf_op jit(solution)/shard_map/ppermute | solution.py:93
  10.4 0.5 %collective-permute-start.3 = (bf16[2,3,128,128]{3,2,1,0:T(8,128)(2,1)}, bf16[2,3,128,128]{3,2,1,0:T(8,128)(2,1)S(1)}, u32[]{:S(2)}, u32[]{:S(2)}) collective-permute-start(bf16[2,3,128,128]{3,2,1,0:T(8,128)(2,1)} %refs_0_.9), channel_id=1, source_target_pairs={{0,6},{1,7},{2,4},{3,5},{4,2},{5,3},{6,0},{7,1},{8,14},{9,15},{10,... | collective-permute-start | bytes 589832 | tf_op jit(solution)/shard_map/ppermute | solution.py:93
  10.9 1.6 %collective-permute-start.9 = (bf16[2,3,128,128]{3,2,1,0:T(8,128)(2,1)}, bf16[2,3,128,128]{3,2,1,0:T(8,128)(2,1)S(1)}, u32[]{:S(2)}, u32[]{:S(2)}) collective-permute-start(bf16[2,3,128,128]{3,2,1,0:T(8,128)(2,1)} %refs_0_.9), channel_id=1, source_target_pairs={{0,8},{8,0},{16,24},{24,16},{1,9},{9,1},{17,25},{25,17},{2,10},{10... | collective-permute-start | bytes 589832 | tf_op jit(solution)/shard_map/ppermute | solution.py:96
  12.5 1.6 %collective-permute-done.11.refs_4_ = bf16[2,3,128,128]{3,2,1,0:T(8,128)(2,1)S(1)} collective-permute-done((bf16[2,3,128,128]{3,2,1,0:T(8,128)(2,1)}, bf16[2,3,128,128]{3,2,1,0:T(8,128)(2,1)S(1)}, u32[]{:S(2)}, u32[]{:S(2)}) %collective-permute-start.11) | collective-permute-done | bytes 196640 | tf_op jit(solution)/shard_map/ppermute | solution.py:96
  14.1 0.8 %collective-permute-start.13 = (bf16[2,3,128,128]{3,2,1,0:T(8,128)(2,1)S(1)}, bf16[2,3,128,128]{3,2,1,0:T(8,128)(2,1)S(1)}, u32[]{:S(2)}, u32[]{:S(2)}) collective-permute-start(bf16[2,3,128,128]{3,2,1,0:T(8,128)(2,1)S(1)} %collective-permute-done.11.refs_4_), channel_id=1, source_target_pairs={{0,8},{8,0},{16,24},{24,16},{1,9},{9,1},{17,25},{25,17},{2,10},{10... | collective-permute-start | bytes 589832 | tf_op jit(solution)/shard_map/ppermute | solution.py:96
  14.9 0.4 collective-permute-done.7.refs_0_
  15.3 0.0 collective-permute-start.8
  15.3 5.0 %collective-permute-done.5.refs_0_ = bf16[2,3,128,128]{3,2,1,0:T(8,128)(2,1)S(1)} collective-permute-done((bf16[2,3,128,128]{3,2,1,0:T(8,128)(2,1)}, bf16[2,3,128,128]{3,2,1,0:T(8,128)(2,1)S(1)}, u32[]{:S(2)}, u32[]{:S(2)}) %collective-permute-start.5) | collective-permute-done | bytes 196640 | tf_op jit(solution)/shard_map/ppermute | solution.py:93
  20.4 0.5 %collective-permute-start.4 = (bf16[2,3,128,128]{3,2,1,0:T(8,128)(2,1)S(1)}, bf16[2,3,128,128]{3,2,1,0:T(8,128)(2,1)S(1)}, u32[]{:S(2)}, u32[]{:S(2)}) collective-permute-start(bf16[2,3,128,128]{3,2,1,0:T(8,128)(2,1)S(1)} %collective-permute-done.3.refs_0_), channel_id=1, source_target_pairs={{0,1},{1,0},{2,3},{3,2},{4,5},{5,4},{6,7},{7,6},{8,9},{9,8},{10,11... | collective-permute-start | bytes 589832 | tf_op jit(solution)/shard_map/ppermute | solution.py:93
  20.9 0.1 collective-permute-start.12
  20.9 1.5 %collective-permute-done.13.refs_6_ = bf16[2,3,128,128]{3,2,1,0:T(8,128)(2,1)S(1)} collective-permute-done((bf16[2,3,128,128]{3,2,1,0:T(8,128)(2,1)S(1)}, bf16[2,3,128,128]{3,2,1,0:T(8,128)(2,1)S(1)}, u32[]{:S(2)}, u32[]{:S(2)}) %collective-permute-start.13) | collective-permute-done | bytes 196640 | tf_op jit(solution)/shard_map/ppermute | solution.py:96
  22.5 0.0 collective-permute-start.10
  22.5 0.0 collective-permute-done.8.refs_1_
  22.5 0.5 %collective-permute-start.14 = (bf16[2,3,128,128]{3,2,1,0:T(8,128)(2,1)S(1)}, bf16[2,3,128,128]{3,2,1,0:T(8,128)(2,1)S(1)}, u32[]{:S(2)}, u32[]{:S(2)}) collective-permute-start(bf16[2,3,128,128]{3,2,1,0:T(8,128)(2,1)S(1)} %collective-permute-done.13.refs_6_), channel_id=1, source_target_pairs={{0,1},{1,0},{2,3},{3,2},{4,5},{5,4},{6,7},{7,6},{8,9},{9,8},{10,11... | collective-permute-start | bytes 589832 | tf_op jit(solution)/shard_map/ppermute | solution.py:93
  23.0 0.7 %fold_left.4.refs_2_ = bf16[16,4,128,128]{3,2,1,0:T(8,128)(2,1)S(1)} custom-call(s32[258]{0:T(512)S(1)} %concatenate.3.info, bf16[2,3,128,128]{3,2,1,0:T(8,128)(2,1)S(1)} %collective-permute-done.7.refs_0_, bf16[2,3,128,128]{3,2,1,0:T(8,128)(2,1)S(1)} %collective-permute-done.8.refs_1_), custom_call_target="tpu_custom_call" | custom-call | bytes 1048576 | tf_op jit(solution)/shard_map/fold_left/pallas_call | solution.py:130
  23.7 0.7 %fold_left.5.refs_2_ = bf16[16,4,128,128]{3,2,1,0:T(8,128)(2,1)S(1)} custom-call(s32[258]{0:T(512)S(1)} %concatenate.3.info, bf16[2,3,128,128]{3,2,1,0:T(8,128)(2,1)S(1)} %collective-permute-done.5.refs_0_, bf16[2,3,128,128]{3,2,1,0:T(8,128)(2,1)S(1)} %collective-permute-done.6.refs_1_, ...), custom_call_target="tpu_custom_call", output_to_operand_aliasing={{}: (3, {})} | custom-call | bytes 1048576 | tf_op jit(solution)/shard_map/fold_left/pallas_call | solution.py:130
  24.4 0.0 copy-start.1
  24.5 0.7 %fold_left.6.refs_2_ = bf16[16,4,128,128]{3,2,1,0:T(8,128)(2,1)S(1)} custom-call(s32[258]{0:T(512)S(1)} %concatenate.3.info, bf16[2,3,128,128]{3,2,1,0:T(8,128)(2,1)S(1)} %collective-permute-done.3.refs_0_, bf16[2,3,128,128]{3,2,1,0:T(8,128)(2,1)S(1)} %collective-permute-done.4.refs_1_, ...), custom_call_target="tpu_custom_call", output_to_operand_aliasing={{}: (3, {})} | custom-call | bytes 1048576 | tf_op jit(solution)/shard_map/fold_left/pallas_call | solution.py:130
  25.2 0.2 copy-done.1
  25.4 0.7 %fold_left.7.left = bf16[16,4,128,128]{3,2,1,0:T(8,128)(2,1)S(1)} custom-call(s32[258]{0:T(512)S(1)} %concatenate.3.info, bf16[2,3,128,128]{3,2,1,0:T(8,128)(2,1)S(1)} %copy-done.1, bf16[2,3,128,128]{3,2,1,0:T(8,128)(2,1)S(1)} %collective-permute-done.1.refs_1_, bf16[16,4,128,128]{3,2,1,0:T(8,128)(2,1)S(1)} %fold_left.6.refs_2_), custom_call_target="tpu_custom_call", output_to_operand_aliasing={{}: (3, {})} | custom-call | bytes 1048576 | tf_op jit(solution)/shard_map/fold_left/pallas_call | solution.py:130
  26.1 0.5 %copy-done = bf16[1,1,4,8,128,128]{5,4,3,2,1,0:T(8,128)(2,1)S(1)} copy-done((bf16[1,1,4,8,128,128]{5,4,3,2,1,0:T(8,128)(2,1)S(1)}, bf16[1,1,4,8,128,128]{5,4,3,2,1,0:T(8,128)(2,1)}, u32[]{:S(2)}) %copy-start) | copy-done | bytes 1048600
  26.6 1.8 %section.5 = bf16[2,4,128,128]{3,2,1,0:T(8,128)(2,1)S(1)} custom-call(s32[258]{0:T(512)S(1)} %concatenate.3.info, bf16[4,8,128,128]{3,2,1,0:T(8,128)(2,1)S(1)} %bitcast.7, bf16[4,8,128,128]{3,2,1,0:T(8,128)(2,1)S(1)} %collective-permute-done.2.other_a, bf16[16,4,128,128]{3,2,1,0:T(8,128)(2,1)S(1)} %fold_left.7.left, bf16[2,3,128,128]{3,2,1,0:T(8,128)(2,1)S(1)} %copy-done.1, ...), custom_call_target="tpu_custom_call" | custom-call | flops 536870912 | bytes 4194304 | tf_op jit(solution)/shard_map/section/pallas_call | solution.py:149
  28.4 2.6 %collective-permute-start.15 = (bf16[2,4,128,128]{3,2,1,0:T(8,128)(2,1)S(1)}, bf16[2,4,128,128]{3,2,1,0:T(8,128)(2,1)S(1)}, u32[]{:S(2)}, u32[]{:S(2)}) collective-permute-start(bf16[2,4,128,128]{3,2,1,0:T(8,128)(2,1)S(1)} %section.5), channel_id=1, source_target_pairs={{0,6},{1,7},{2,4},{3,5},{4,2},{5,3},{6,0},{7,1},{8,14},{9,15},{10,... | collective-permute-start | bytes 786440 | tf_op jit(solution)/shard_map/ppermute | solution.py:93
  30.9 1.8 %section.6 = bf16[2,4,128,128]{3,2,1,0:T(8,128)(2,1)S(1)} custom-call(s32[258]{0:T(512)S(1)} %concatenate.3.info, bf16[4,8,128,128]{3,2,1,0:T(8,128)(2,1)S(1)} %bitcast.8, bf16[4,8,128,128]{3,2,1,0:T(8,128)(2,1)S(1)} %collective-permute-done.2.other_a, bf16[16,4,128,128]{3,2,1,0:T(8,128)(2,1)S(1)} %fold_left.7.left, bf16[2,3,128,128]{3,2,1,0:T(8,128)(2,1)S(1)} %copy-done.1, ...), custom_call_target="tpu_custom_call" | custom-call | flops 536870912 | bytes 4194304 | tf_op jit(solution)/shard_map/section/pallas_call | solution.py:149
  32.7 0.6 %collective-permute-start.16 = (bf16[2,4,128,128]{3,2,1,0:T(8,128)(2,1)S(1)}, bf16[2,4,128,128]{3,2,1,0:T(8,128)(2,1)S(1)}, u32[]{:S(2)}, u32[]{:S(2)}) collective-permute-start(bf16[2,4,128,128]{3,2,1,0:T(8,128)(2,1)S(1)} %section.6), channel_id=1, source_target_pairs={{0,4},{1,5},{2,6},{3,7},{4,0},{5,1},{6,2},{7,3},{8,12},{9,13},{10,... | collective-permute-start | bytes 786440 | tf_op jit(solution)/shard_map/ppermute | solution.py:93
  33.3 1.8 %section.7 = bf16[2,4,128,128]{3,2,1,0:T(8,128)(2,1)S(1)} custom-call(s32[258]{0:T(512)S(1)} %concatenate.3.info, bf16[4,8,128,128]{3,2,1,0:T(8,128)(2,1)S(1)} %bitcast.9, bf16[4,8,128,128]{3,2,1,0:T(8,128)(2,1)S(1)} %collective-permute-done.2.other_a, bf16[16,4,128,128]{3,2,1,0:T(8,128)(2,1)S(1)} %fold_left.7.left, bf16[2,3,128,128]{3,2,1,0:T(8,128)(2,1)S(1)} %copy-done.1, ...), custom_call_target="tpu_custom_call" | custom-call | flops 536870912 | bytes 4194304 | tf_op jit(solution)/shard_map/section/pallas_call | solution.py:149
  35.0 0.5 %collective-permute-start.17 = (bf16[2,4,128,128]{3,2,1,0:T(8,128)(2,1)S(1)}, bf16[2,4,128,128]{3,2,1,0:T(8,128)(2,1)S(1)}, u32[]{:S(2)}, u32[]{:S(2)}) collective-permute-start(bf16[2,4,128,128]{3,2,1,0:T(8,128)(2,1)S(1)} %section.7), channel_id=1, source_target_pairs={{0,2},{1,3},{2,0},{3,1},{4,6},{5,7},{6,4},{7,5},{8,10},{9,11},{10,... | collective-permute-start | bytes 786440 | tf_op jit(solution)/shard_map/ppermute | solution.py:93
  35.6 1.8 %section.4 = f32[2,4,128,128]{3,2,1,0:T(8,128)S(1)} custom-call(s32[258]{0:T(512)S(1)} %concatenate.3.info, bf16[4,8,128,128]{3,2,1,0:T(8,128)(2,1)S(1)} %bitcast.10, bf16[4,8,128,128]{3,2,1,0:T(8,128)(2,1)S(1)} %collective-permute-done.2.other_a, bf16[16,4,128,128]{3,2,1,0:T(8,128)(2,1)S(1)} %fold_left.7.left, bf16[2,3,128,128]{3,2,1,0:T(8,128)(2,1)S(1)} %copy-done.1, ...), custom_call_target="tpu_custom_call" | custom-call | flops 536870912 | bytes 4194304 | tf_op jit(solution)/shard_map/section/pallas_call | solution.py:149
  37.4 0.3 collective-permute-done.15
  37.7 5.5 %collective-permute-done.16 = bf16[2,4,128,128]{3,2,1,0:T(8,128)(2,1)S(1)} collective-permute-done((bf16[2,4,128,128]{3,2,1,0:T(8,128)(2,1)S(1)}, bf16[2,4,128,128]{3,2,1,0:T(8,128)(2,1)S(1)}, u32[]{:S(2)}, u32[]{:S(2)}) %collective-permute-start.16) | collective-permute-done | bytes 262176 | tf_op jit(solution)/shard_map/ppermute | solution.py:93
  43.2 0.2 collective-permute-done.17
  43.3 0.9 %convert_add_fusion = f32[2,4,128,128]{3,2,1,0:T(8,128)} fusion(bf16[2,4,128,128]{3,2,1,0:T(8,128)(2,1)S(1)} %collective-permute-done.17, bf16[2,4,128,128]{3,2,1,0:T(8,128)(2,1)S(1)} %collective-permute-done.16, f32[2,4,128,128]{3,2,1,0:T(8,128)S(1)} %section.4, bf16[2,4,128,128]{3,2,1,0:T(8,128)(2,1)S(1)} %collective-permute-done.15), kind=kLoop, calls=%fused_computation | loop fusion | flops 786432 | bytes 1835008 | tf_op jit(solution)/shard_map/add | solution.py:173
  (10 shorter events, 0.0 us)
Async XLA Ops:
  0.0 7.3 %collective-permute-start.2 = (bf16[4,8,128,128]{3,2,1,0:T(8,128)(2,1)}, bf16[4,8,128,128]{3,2,1,0:T(8,128)(2,1)S(1)}, u32[]{:S(2)}, u32[]{:S(2)}) collective-permute-start(bf16[4,8,128,128]{3,2,1,0:T(8,128)(2,1)} %bitcast.6), channel_id=1, source_target_pairs={{0,1},{1,0},{2,3},{3,2},{4,5},{5,4},{6,7},{7,6},{8,9},{9,8},{10,11... | collective-permute-start | bytes 3145736 | tf_op jit(solution)/shard_map/ppermute | solution.py:93
  0.5 6.9 %collective-permute-start.1 = (bf16[2,3,128,128]{3,2,1,0:T(8,128)(2,1)}, bf16[2,3,128,128]{3,2,1,0:T(8,128)(2,1)S(1)}, u32[]{:S(2)}, u32[]{:S(2)}) collective-permute-start(bf16[2,3,128,128]{3,2,1,0:T(8,128)(2,1)} %refs_0_.9), channel_id=1, source_target_pairs={{0,1},{1,0},{2,3},{3,2},{4,5},{5,4},{6,7},{7,6},{8,9},{9,8},{10,11... | collective-permute-start | bytes 589832 | tf_op jit(solution)/shard_map/ppermute | solution.py:93
  0.5 13.6 %collective-permute-start.11 = (bf16[2,3,128,128]{3,2,1,0:T(8,128)(2,1)}, bf16[2,3,128,128]{3,2,1,0:T(8,128)(2,1)S(1)}, u32[]{:S(2)}, u32[]{:S(2)}) collective-permute-start(bf16[2,3,128,128]{3,2,1,0:T(8,128)(2,1)} %refs_0_.9), channel_id=1, source_target_pairs={{0,16},{8,24},{16,0},{24,8},{1,17},{9,25},{17,1},{25,9},{2,18},{10... | collective-permute-start | bytes 589832 | tf_op jit(solution)/shard_map/ppermute | solution.py:96
  5.3 1.8 %collective-permute-start = (s32[4,8]{1,0:T(4,128)S(1)}, s32[4,8]{1,0:T(4,128)S(1)}, u32[]{:S(2)}, u32[]{:S(2)}) collective-permute-start(s32[4,8]{1,0:T(4,128)S(1)} %get-tuple-element.13), channel_id=1, source_target_pairs={{0,1},{1,0},{2,3},{3,2},{4,5},{5,4},{6,7},{7,6},{8,9},{9,8},{10,11... | collective-permute-start | bytes 392 | tf_op jit(solution)/shard_map/ppermute | solution.py:93
  7.3 8.0 %collective-permute-start.7 = (bf16[2,3,128,128]{3,2,1,0:T(8,128)(2,1)}, bf16[2,3,128,128]{3,2,1,0:T(8,128)(2,1)S(1)}, u32[]{:S(2)}, u32[]{:S(2)}) collective-permute-start(bf16[2,3,128,128]{3,2,1,0:T(8,128)(2,1)} %refs_0_.9), channel_id=1, source_target_pairs={{0,2},{1,3},{2,0},{3,1},{4,6},{5,7},{6,4},{7,5},{8,10},{9,11},{10,... | collective-permute-start | bytes 589832 | tf_op jit(solution)/shard_map/ppermute | solution.py:93
  8.9 11.5 %collective-permute-start.5 = (bf16[2,3,128,128]{3,2,1,0:T(8,128)(2,1)}, bf16[2,3,128,128]{3,2,1,0:T(8,128)(2,1)S(1)}, u32[]{:S(2)}, u32[]{:S(2)}) collective-permute-start(bf16[2,3,128,128]{3,2,1,0:T(8,128)(2,1)} %refs_0_.9), channel_id=1, source_target_pairs={{0,4},{1,5},{2,6},{3,7},{4,0},{5,1},{6,2},{7,3},{8,12},{9,13},{10,... | collective-permute-start | bytes 589832 | tf_op jit(solution)/shard_map/ppermute | solution.py:93
  10.4 9.9 %collective-permute-start.3 = (bf16[2,3,128,128]{3,2,1,0:T(8,128)(2,1)}, bf16[2,3,128,128]{3,2,1,0:T(8,128)(2,1)S(1)}, u32[]{:S(2)}, u32[]{:S(2)}) collective-permute-start(bf16[2,3,128,128]{3,2,1,0:T(8,128)(2,1)} %refs_0_.9), channel_id=1, source_target_pairs={{0,6},{1,7},{2,4},{3,5},{4,2},{5,3},{6,0},{7,1},{8,14},{9,15},{10,... | collective-permute-start | bytes 589832 | tf_op jit(solution)/shard_map/ppermute | solution.py:93
  10.9 10.0 %collective-permute-start.9 = (bf16[2,3,128,128]{3,2,1,0:T(8,128)(2,1)}, bf16[2,3,128,128]{3,2,1,0:T(8,128)(2,1)S(1)}, u32[]{:S(2)}, u32[]{:S(2)}) collective-permute-start(bf16[2,3,128,128]{3,2,1,0:T(8,128)(2,1)} %refs_0_.9), channel_id=1, source_target_pairs={{0,8},{8,0},{16,24},{24,16},{1,9},{9,1},{17,25},{25,17},{2,10},{10... | collective-permute-start | bytes 589832 | tf_op jit(solution)/shard_map/ppermute | solution.py:96
  14.1 8.4 %collective-permute-start.13 = (bf16[2,3,128,128]{3,2,1,0:T(8,128)(2,1)S(1)}, bf16[2,3,128,128]{3,2,1,0:T(8,128)(2,1)S(1)}, u32[]{:S(2)}, u32[]{:S(2)}) collective-permute-start(bf16[2,3,128,128]{3,2,1,0:T(8,128)(2,1)S(1)} %collective-permute-done.11.refs_4_), channel_id=1, source_target_pairs={{0,8},{8,0},{16,24},{24,16},{1,9},{9,1},{17,25},{25,17},{2,10},{10... | collective-permute-start | bytes 589832 | tf_op jit(solution)/shard_map/ppermute | solution.py:96
  15.3 7.2 %collective-permute-start.8 = (bf16[2,3,128,128]{3,2,1,0:T(8,128)(2,1)S(1)}, bf16[2,3,128,128]{3,2,1,0:T(8,128)(2,1)S(1)}, u32[]{:S(2)}, u32[]{:S(2)}) collective-permute-start(bf16[2,3,128,128]{3,2,1,0:T(8,128)(2,1)S(1)} %collective-permute-done.7.refs_0_), channel_id=1, source_target_pairs={{0,1},{1,0},{2,3},{3,2},{4,5},{5,4},{6,7},{7,6},{8,9},{9,8},{10,11... | collective-permute-start | bytes 589832 | tf_op jit(solution)/shard_map/ppermute | solution.py:93
  20.4 3.4 %collective-permute-start.6 = (bf16[2,3,128,128]{3,2,1,0:T(8,128)(2,1)S(1)}, bf16[2,3,128,128]{3,2,1,0:T(8,128)(2,1)S(1)}, u32[]{:S(2)}, u32[]{:S(2)}) collective-permute-start(bf16[2,3,128,128]{3,2,1,0:T(8,128)(2,1)S(1)} %collective-permute-done.5.refs_0_), channel_id=1, source_target_pairs={{0,1},{1,0},{2,3},{3,2},{4,5},{5,4},{6,7},{7,6},{8,9},{9,8},{10,11... | collective-permute-start | bytes 589832 | tf_op jit(solution)/shard_map/ppermute | solution.py:93
  20.4 4.1 %collective-permute-start.4 = (bf16[2,3,128,128]{3,2,1,0:T(8,128)(2,1)S(1)}, bf16[2,3,128,128]{3,2,1,0:T(8,128)(2,1)S(1)}, u32[]{:S(2)}, u32[]{:S(2)}) collective-permute-start(bf16[2,3,128,128]{3,2,1,0:T(8,128)(2,1)S(1)} %collective-permute-done.3.refs_0_), channel_id=1, source_target_pairs={{0,1},{1,0},{2,3},{3,2},{4,5},{5,4},{6,7},{7,6},{8,9},{9,8},{10,11... | collective-permute-start | bytes 589832 | tf_op jit(solution)/shard_map/ppermute | solution.py:93
  20.9 5.2 %collective-permute-start.12 = (bf16[2,3,128,128]{3,2,1,0:T(8,128)(2,1)S(1)}, bf16[2,3,128,128]{3,2,1,0:T(8,128)(2,1)S(1)}, u32[]{:S(2)}, u32[]{:S(2)}) collective-permute-start(bf16[2,3,128,128]{3,2,1,0:T(8,128)(2,1)S(1)} %collective-permute-done.11.refs_4_), channel_id=1, source_target_pairs={{0,1},{1,0},{2,3},{3,2},{4,5},{5,4},{6,7},{7,6},{8,9},{9,8},{10,11... | collective-permute-start | bytes 589832 | tf_op jit(solution)/shard_map/ppermute | solution.py:93
  22.5 3.6 %collective-permute-start.10 = (bf16[2,3,128,128]{3,2,1,0:T(8,128)(2,1)S(1)}, bf16[2,3,128,128]{3,2,1,0:T(8,128)(2,1)S(1)}, u32[]{:S(2)}, u32[]{:S(2)}) collective-permute-start(bf16[2,3,128,128]{3,2,1,0:T(8,128)(2,1)S(1)} %collective-permute-done.9.refs_2_), channel_id=1, source_target_pairs={{0,1},{1,0},{2,3},{3,2},{4,5},{5,4},{6,7},{7,6},{8,9},{9,8},{10,11... | collective-permute-start | bytes 589832 | tf_op jit(solution)/shard_map/ppermute | solution.py:93
  22.5 3.6 %collective-permute-start.14 = (bf16[2,3,128,128]{3,2,1,0:T(8,128)(2,1)S(1)}, bf16[2,3,128,128]{3,2,1,0:T(8,128)(2,1)S(1)}, u32[]{:S(2)}, u32[]{:S(2)}) collective-permute-start(bf16[2,3,128,128]{3,2,1,0:T(8,128)(2,1)S(1)} %collective-permute-done.13.refs_6_), channel_id=1, source_target_pairs={{0,1},{1,0},{2,3},{3,2},{4,5},{5,4},{6,7},{7,6},{8,9},{9,8},{10,11... | collective-permute-start | bytes 589832 | tf_op jit(solution)/shard_map/ppermute | solution.py:93
  24.4 0.9 %copy-start.1 = (bf16[2,3,128,128]{3,2,1,0:T(8,128)(2,1)S(1)}, bf16[2,3,128,128]{3,2,1,0:T(8,128)(2,1)}, u32[]{:S(2)}) copy-start(bf16[2,3,128,128]{3,2,1,0:T(8,128)(2,1)} %refs_0_.9) | copy-start | bytes 589828
  25.4 1.2 %copy-start = (bf16[1,1,4,8,128,128]{5,4,3,2,1,0:T(8,128)(2,1)S(1)}, bf16[1,1,4,8,128,128]{5,4,3,2,1,0:T(8,128)(2,1)}, u32[]{:S(2)}) copy-start(bf16[1,1,4,8,128,128]{5,4,3,2,1,0:T(8,128)(2,1)} %param.6) | copy-start | bytes 3145732
  28.4 9.3 %collective-permute-start.15 = (bf16[2,4,128,128]{3,2,1,0:T(8,128)(2,1)S(1)}, bf16[2,4,128,128]{3,2,1,0:T(8,128)(2,1)S(1)}, u32[]{:S(2)}, u32[]{:S(2)}) collective-permute-start(bf16[2,4,128,128]{3,2,1,0:T(8,128)(2,1)S(1)} %section.5), channel_id=1, source_target_pairs={{0,6},{1,7},{2,4},{3,5},{4,2},{5,3},{6,0},{7,1},{8,14},{9,15},{10,... | collective-permute-start | bytes 786440 | tf_op jit(solution)/shard_map/ppermute | solution.py:93
  32.7 10.5 %collective-permute-start.16 = (bf16[2,4,128,128]{3,2,1,0:T(8,128)(2,1)S(1)}, bf16[2,4,128,128]{3,2,1,0:T(8,128)(2,1)S(1)}, u32[]{:S(2)}, u32[]{:S(2)}) collective-permute-start(bf16[2,4,128,128]{3,2,1,0:T(8,128)(2,1)S(1)} %section.6), channel_id=1, source_target_pairs={{0,4},{1,5},{2,6},{3,7},{4,0},{5,1},{6,2},{7,3},{8,12},{9,13},{10,... | collective-permute-start | bytes 786440 | tf_op jit(solution)/shard_map/ppermute | solution.py:93
  35.0 8.3 %collective-permute-start.17 = (bf16[2,4,128,128]{3,2,1,0:T(8,128)(2,1)S(1)}, bf16[2,4,128,128]{3,2,1,0:T(8,128)(2,1)S(1)}, u32[]{:S(2)}, u32[]{:S(2)}) collective-permute-start(bf16[2,4,128,128]{3,2,1,0:T(8,128)(2,1)S(1)} %section.7), channel_id=1, source_target_pairs={{0,2},{1,3},{2,0},{3,1},{4,6},{5,7},{6,4},{7,5},{8,10},{9,11},{10,... | collective-permute-start | bytes 786440 | tf_op jit(solution)/shard_map/ppermute | solution.py:93

commit v3 on v2

--- a/solution.py
+++ b/solution.py
@@ -102,9 +102,6 @@
         a_rows.reshape(row_count, slots) * segment + a_cols.reshape(row_count, slots),
         -1,
     )
-    right = [p_vals] + [None] * (row_count - 1)
-    for d in sorted(range(1, row_count), key=lambda d: (d.bit_count(), -d)):
-        right[d] = row_xor(right[d & (d - 1)], d & -d)
     other_codes = col_xor(codes, 1)
     info = jnp.concatenate(
         [
@@ -114,10 +111,16 @@
             p_cols.reshape(-1),
         ]
     )
-    near_p, info, other_p, other_a = lax.optimization_barrier(
-        (p_vals, info, col_xor(p_vals, 1), col_xor(own_a, 1))
-    )
+    near_p, other_a = lax.optimization_barrier((p_vals, col_xor(own_a, 1)))
     left = [p_vals] + [col_xor(near_p, 2 * e) for e in range(1, row_count)]
+    right = [p_vals] + [None] * (row_count - 1)
+    for d in sorted(range(1, row_count), key=lambda d: (d.bit_count(), -d)):
+        piece = right[d & (d - 1)]
+        if d & (d - 1):
+            piece, info = lax.optimization_barrier((piece, info))
+        right[d] = row_xor(piece, d & -d)
+    late_p, *_ = lax.optimization_barrier((p_vals, *left[1:], right[1]))
+    other_p = col_xor(late_p, 1)
     right = [half for piece in right[1:] for half in (piece, col_xor(piece, 1))]
     right = [p_vals, other_p] + right
     smem = pl.BlockSpec(memory_space=pltpu.SMEM)

time: 44.4 us -> 43.5 us (0.980)
  starting transfers between devices: 15.3 us -> 14.8 us
    ppermute x3, waiting for transfers between devices: 3.17 us -> 2.24 us  [row_xor(): return lax.ppermute(x, 'row', [(r, r ^ b) for r in range(row_count)])]
    ppermute x15, waiting for transfers between devices: 11.4 us -> 12 us  [col_xor(): return lax.ppermute(x, 'col', [(c, c ^ b) for c in range(col_count)])]
    ppermute x3, starting transfers between devices: 6.41 us -> 5.88 us  [row_xor(): return lax.ppermute(x, 'row', [(r, r ^ b) for r in range(row_count)])]
  transfers between devices with their start and end apart: 18 -> 18, of which waited for: 7 -> 7; matrix products, arithmetic and copies ran while one was open for 6% -> 6% of each run, Pallas kernels for 18% -> 19%
where the time goes in v3:
time: 43.5 us; the launch traced here: 43.3 us
  starting transfers between devices  14.8 us (34%)
  waiting for transfers between devices  14.3 us (33%)
  Pallas kernels  9.91 us (23%)
  other arithmetic  2.43 us (6%)
  local copies, waits for them, and re-layouts  1.72 us (4%)
    ppermute x15, waiting for transfers between devices, col_xor(): return lax.ppermute(x, 'col', [(c, c ^ b) for c in range(col_count)])  12 us
    ppermute x15, starting transfers between devices, col_xor(): return lax.ppermute(x, 'col', [(c, c ^ b) for c in range(col_count)])  8.9 us
    pallas_call x4, Pallas kernels, partial_of(): pl.pallas_call(functools.partial(section, sizes, hop), out_shape=jax.Shap...  7.04 us
    ppermute x3, starting transfers between devices, row_xor(): return lax.ppermute(x, 'row', [(r, r ^ b) for r in range(row_count)])  5.88 us
    pallas_call x4, Pallas kernels, local(): pl.pallas_call(functools.partial(fold_left, sizes, hop), out_shape=jax.Sh...  2.87 us
    ppermute x3, waiting for transfers between devices, row_xor(): return lax.ppermute(x, 'row', [(r, r ^ b) for r in range(row_count)])  2.24 us
    unnamed x5, local copies, waits for them, and re-layouts  1.25 us
    add x1, other arithmetic, local(): total = total + piece.astype(jnp.float32)  0.91 us
  transfers between devices with their start and end apart: 18, of which 7 were waited for; matrix products, arithmetic and copies ran while one was open for 6% of the time, Pallas kernels for 19%

profile of v3, /device:TPU:0, one launch (start us, length us, event | category | flops | bytes accessed | tf_op | source)
XLA Modules:
  0.0 43.3 jit_solution(18223334985711667674)
XLA Ops:
  0.0 0.5 %collective-permute-start.2 = (bf16[4,8,128,128]{3,2,1,0:T(8,128)(2,1)}, bf16[4,8,128,128]{3,2,1,0:T(8,128)(2,1)S(1)}, u32[]{:S(2)}, u32[]{:S(2)}) collective-permute-start(bf16[4,8,128,128]{3,2,1,0:T(8,128)(2,1)} %bitcast.6), channel_id=1, source_target_pairs={{0,1},{1,0},{2,3},{3,2},{4,5},{5,4},{6,7},{7,6},{8,9},{9,8},{10,11... | collective-permute-start | bytes 3145736 | tf_op jit(solution)/shard_map/ppermute | solution.py:93
  0.5 3.6 %collective-permute-start = (bf16[2,3,128,128]{3,2,1,0:T(8,128)(2,1)}, bf16[2,3,128,128]{3,2,1,0:T(8,128)(2,1)S(1)}, u32[]{:S(2)}, u32[]{:S(2)}) collective-permute-start(bf16[2,3,128,128]{3,2,1,0:T(8,128)(2,1)} %refs_0_.9), channel_id=1, source_target_pairs={{0,16},{8,24},{16,0},{24,8},{1,17},{9,25},{17,1},{25,9},{2,18},{10... | collective-permute-start | bytes 589832 | tf_op jit(solution)/shard_map/ppermute | solution.py:96
  4.0 1.6 %collective-permute-start.6 = (bf16[2,3,128,128]{3,2,1,0:T(8,128)(2,1)}, bf16[2,3,128,128]{3,2,1,0:T(8,128)(2,1)S(1)}, u32[]{:S(2)}, u32[]{:S(2)}) collective-permute-start(bf16[2,3,128,128]{3,2,1,0:T(8,128)(2,1)} %refs_0_.9), channel_id=1, source_target_pairs={{0,8},{8,0},{16,24},{24,16},{1,9},{9,1},{17,25},{25,17},{2,10},{10... | collective-permute-start | bytes 589832 | tf_op jit(solution)/shard_map/ppermute | solution.py:96
  5.6 0.8 %bitcast_select_fusion = (s32[4,8]{1,0:T(4,128)S(1)}, s32[1,1,4,8]{3,2,1,0:T(4,128)S(1)}) fusion(s32[4]{0:T(128)} %bitcast.11, s32[1,1,4,8]{3,2,1,0:T(4,128)} %param.8, s32[1,1,4,8]{3,2,1,0:T(4,128)} %param.7), kind=kLoop, calls=%fused_computation.1 | loop fusion | flops 128 | bytes 528 | tf_op jit(solution)/shard_map/jit(_where)/select_n | solution.py:100
  6.4 0.0 collective-permute-start.1
  6.4 0.1 add.20
  6.5 0.7 %iota_compare_fusion = pred[4,8]{1,0:T(4,128)(4,1)S(1)} fusion(s32[4]{0:T(128)} %bitcast.12), kind=kLoop, calls=%fused_computation.3 | loop fusion | flops 32 | bytes 48 | tf_op jit(solution)/shard_map/lt | solution.py:101
  7.2 0.1 lt.23
  7.3 0.0 collective-permute-done.2.other_a
  7.3 1.5 %collective-permute-start.3 = (bf16[2,3,128,128]{3,2,1,0:T(8,128)(2,1)}, bf16[2,3,128,128]{3,2,1,0:T(8,128)(2,1)S(1)}, u32[]{:S(2)}, u32[]{:S(2)}) collective-permute-start(bf16[2,3,128,128]{3,2,1,0:T(8,128)(2,1)} %refs_0_.9), channel_id=1, source_target_pairs={{0,2},{1,3},{2,0},{3,1},{4,6},{5,7},{6,4},{7,5},{8,10},{9,11},{10,... | collective-permute-start | bytes 589832 | tf_op jit(solution)/shard_map/ppermute | solution.py:93
  8.8 1.5 %collective-permute-start.4 = (bf16[2,3,128,128]{3,2,1,0:T(8,128)(2,1)}, bf16[2,3,128,128]{3,2,1,0:T(8,128)(2,1)S(1)}, u32[]{:S(2)}, u32[]{:S(2)}) collective-permute-start(bf16[2,3,128,128]{3,2,1,0:T(8,128)(2,1)} %refs_0_.9), channel_id=1, source_target_pairs={{0,4},{1,5},{2,6},{3,7},{4,0},{5,1},{6,2},{7,3},{8,12},{9,13},{10,... | collective-permute-start | bytes 589832 | tf_op jit(solution)/shard_map/ppermute | solution.py:93
  10.3 0.8 %copy.10 = s32[64,3]{1,0:T(8,128)S(1)} copy(s32[64,3]{0,1:T(4,128)} %param.11) | data formatting | bytes 1536 | tf_op args[5]
  11.1 0.1 reshape.26
  11.3 0.1 reshape.25
  11.3 0.1 concatenate.3.info
  11.4 0.5 %collective-permute-start.5 = (bf16[2,3,128,128]{3,2,1,0:T(8,128)(2,1)}, bf16[2,3,128,128]{3,2,1,0:T(8,128)(2,1)S(1)}, u32[]{:S(2)}, u32[]{:S(2)}) collective-permute-start(bf16[2,3,128,128]{3,2,1,0:T(8,128)(2,1)} %refs_0_.9), channel_id=1, source_target_pairs={{0,6},{1,7},{2,4},{3,5},{4,2},{5,3},{6,0},{7,1},{8,14},{9,15},{10,... | collective-permute-start | bytes 589832 | tf_op jit(solution)/shard_map/ppermute | solution.py:93
  11.9 2.2 %collective-permute-done.refs_4_ = bf16[2,3,128,128]{3,2,1,0:T(8,128)(2,1)S(1)} collective-permute-done((bf16[2,3,128,128]{3,2,1,0:T(8,128)(2,1)}, bf16[2,3,128,128]{3,2,1,0:T(8,128)(2,1)S(1)}, u32[]{:S(2)}, u32[]{:S(2)}) %collective-permute-start) | collective-permute-done | bytes 196640 | tf_op jit(solution)/shard_map/ppermute | solution.py:96
  14.1 0.7 %collective-permute-start.13 = (bf16[2,3,128,128]{3,2,1,0:T(8,128)(2,1)S(1)}, bf16[2,3,128,128]{3,2,1,0:T(8,128)(2,1)S(1)}, u32[]{:S(2)}, u32[]{:S(2)}) collective-permute-start(bf16[2,3,128,128]{3,2,1,0:T(8,128)(2,1)S(1)} %collective-permute-done.refs_4_), channel_id=1, source_target_pairs={{0,8},{8,0},{16,24},{24,16},{1,9},{9,1},{17,25},{25,17},{2,10},{10... | collective-permute-start | bytes 589832 | tf_op jit(solution)/shard_map/ppermute | solution.py:96
  14.9 0.4 collective-permute-done.3.refs_0_
  15.2 0.0 collective-permute-start.10
  15.2 5.0 %collective-permute-done.4.refs_0_ = bf16[2,3,128,128]{3,2,1,0:T(8,128)(2,1)S(1)} collective-permute-done((bf16[2,3,128,128]{3,2,1,0:T(8,128)(2,1)}, bf16[2,3,128,128]{3,2,1,0:T(8,128)(2,1)S(1)}, u32[]{:S(2)}, u32[]{:S(2)}) %collective-permute-start.4) | collective-permute-done | bytes 196640 | tf_op jit(solution)/shard_map/ppermute | solution.py:93
  20.3 0.5 %collective-permute-start.11 = (bf16[2,3,128,128]{3,2,1,0:T(8,128)(2,1)S(1)}, bf16[2,3,128,128]{3,2,1,0:T(8,128)(2,1)S(1)}, u32[]{:S(2)}, u32[]{:S(2)}) collective-permute-start(bf16[2,3,128,128]{3,2,1,0:T(8,128)(2,1)S(1)} %collective-permute-done.6.refs_2_), channel_id=1, source_target_pairs={{0,1},{1,0},{2,3},{3,2},{4,5},{5,4},{6,7},{7,6},{8,9},{9,8},{10,11... | collective-permute-start | bytes 589832 | tf_op jit(solution)/shard_map/ppermute | solution.py:93
  20.8 0.1 collective-permute-start.8
  20.9 0.4 %collective-permute-start.7 = (bf16[2,3,128,128]{3,2,1,0:T(8,128)(2,1)}, bf16[2,3,128,128]{3,2,1,0:T(8,128)(2,1)S(1)}, u32[]{:S(2)}, u32[]{:S(2)}) collective-permute-start(bf16[2,3,128,128]{3,2,1,0:T(8,128)(2,1)} %refs_0_.9), channel_id=1, source_target_pairs={{0,1},{1,0},{2,3},{3,2},{4,5},{5,4},{6,7},{7,6},{8,9},{9,8},{10,11... | collective-permute-start | bytes 589832 | tf_op jit(solution)/shard_map/ppermute | solution.py:93
  21.3 0.1 collective-permute-start.12
  21.4 0.3 collective-permute-done.9.refs_1_
  21.7 0.1 collective-permute-start.14
  21.9 0.7 %fold_left.4.refs_2_ = bf16[16,4,128,128]{3,2,1,0:T(8,128)(2,1)S(1)} custom-call(s32[258]{0:T(512)S(1)} %concatenate.3.info, bf16[2,3,128,128]{3,2,1,0:T(8,128)(2,1)S(1)} %collective-permute-done.3.refs_0_, bf16[2,3,128,128]{3,2,1,0:T(8,128)(2,1)S(1)} %collective-permute-done.10.refs_1_), custom_call_target="tpu_custom_call" | custom-call | bytes 1048576 | tf_op jit(solution)/shard_map/fold_left/pallas_call | solution.py:133
  22.6 0.7 %fold_left.5.refs_2_ = bf16[16,4,128,128]{3,2,1,0:T(8,128)(2,1)S(1)} custom-call(s32[258]{0:T(512)S(1)} %concatenate.3.info, bf16[2,3,128,128]{3,2,1,0:T(8,128)(2,1)S(1)} %collective-permute-done.4.refs_0_, bf16[2,3,128,128]{3,2,1,0:T(8,128)(2,1)S(1)} %collective-permute-done.9.refs_1_, ...), custom_call_target="tpu_custom_call", output_to_operand_aliasing={{}: (3, {})} | custom-call | bytes 1048576 | tf_op jit(solution)/shard_map/fold_left/pallas_call | solution.py:133
  23.3 0.0 copy-start.1
  23.3 0.0 collective-permute-done.8.refs_1_
  23.3 0.7 %fold_left.6.refs_2_ = bf16[16,4,128,128]{3,2,1,0:T(8,128)(2,1)S(1)} custom-call(s32[258]{0:T(512)S(1)} %concatenate.3.info, bf16[2,3,128,128]{3,2,1,0:T(8,128)(2,1)S(1)} %collective-permute-done.5.refs_0_, bf16[2,3,128,128]{3,2,1,0:T(8,128)(2,1)S(1)} %collective-permute-done.8.refs_1_, ...), custom_call_target="tpu_custom_call", output_to_operand_aliasing={{}: (3, {})} | custom-call | bytes 1048576 | tf_op jit(solution)/shard_map/fold_left/pallas_call | solution.py:133
  24.1 0.0 copy-start
  24.1 0.2 copy-done.1
  24.2 0.7 %fold_left.7.left = bf16[16,4,128,128]{3,2,1,0:T(8,128)(2,1)S(1)} custom-call(s32[258]{0:T(512)S(1)} %concatenate.3.info, bf16[2,3,128,128]{3,2,1,0:T(8,128)(2,1)S(1)} %copy-done.1, bf16[2,3,128,128]{3,2,1,0:T(8,128)(2,1)S(1)} %collective-permute-done.7.refs_1_, bf16[16,4,128,128]{3,2,1,0:T(8,128)(2,1)S(1)} %fold_left.6.refs_2_), custom_call_target="tpu_custom_call", output_to_operand_aliasing={{}: (3, {})} | custom-call | bytes 1048576 | tf_op jit(solution)/shard_map/fold_left/pallas_call | solution.py:133
  25.0 0.0 collective-permute-done.14.refs_7_
  25.0 0.3 copy-done
  25.3 1.8 %section.5 = bf16[2,4,128,128]{3,2,1,0:T(8,128)(2,1)S(1)} custom-call(s32[258]{0:T(512)S(1)} %concatenate.3.info, bf16[4,8,128,128]{3,2,1,0:T(8,128)(2,1)S(1)} %bitcast.7, bf16[4,8,128,128]{3,2,1,0:T(8,128)(2,1)S(1)} %collective-permute-done.2.other_a, bf16[16,4,128,128]{3,2,1,0:T(8,128)(2,1)S(1)} %fold_left.7.left, bf16[2,3,128,128]{3,2,1,0:T(8,128)(2,1)S(1)} %copy-done.1, ...), custom_call_target="tpu_custom_call" | custom-call | flops 536870912 | bytes 4194304 | tf_op jit(solution)/shard_map/section/pallas_call | solution.py:152
  27.1 1.9 %collective-permute-start.15 = (bf16[2,4,128,128]{3,2,1,0:T(8,128)(2,1)S(1)}, bf16[2,4,128,128]{3,2,1,0:T(8,128)(2,1)S(1)}, u32[]{:S(2)}, u32[]{:S(2)}) collective-permute-start(bf16[2,4,128,128]{3,2,1,0:T(8,128)(2,1)S(1)} %section.5), channel_id=1, source_target_pairs={{0,6},{1,7},{2,4},{3,5},{4,2},{5,3},{6,0},{7,1},{8,14},{9,15},{10,... | collective-permute-start | bytes 786440 | tf_op jit(solution)/shard_map/ppermute | solution.py:93
  29.0 1.8 %section.6 = bf16[2,4,128,128]{3,2,1,0:T(8,128)(2,1)S(1)} custom-call(s32[258]{0:T(512)S(1)} %concatenate.3.info, bf16[4,8,128,128]{3,2,1,0:T(8,128)(2,1)S(1)} %bitcast.8, bf16[4,8,128,128]{3,2,1,0:T(8,128)(2,1)S(1)} %collective-permute-done.2.other_a, bf16[16,4,128,128]{3,2,1,0:T(8,128)(2,1)S(1)} %fold_left.7.left, bf16[2,3,128,128]{3,2,1,0:T(8,128)(2,1)S(1)} %copy-done.1, ...), custom_call_target="tpu_custom_call" | custom-call | flops 536870912 | bytes 4194304 | tf_op jit(solution)/shard_map/section/pallas_call | solution.py:152
  30.8 0.6 %collective-permute-start.16 = (bf16[2,4,128,128]{3,2,1,0:T(8,128)(2,1)S(1)}, bf16[2,4,128,128]{3,2,1,0:T(8,128)(2,1)S(1)}, u32[]{:S(2)}, u32[]{:S(2)}) collective-permute-start(bf16[2,4,128,128]{3,2,1,0:T(8,128)(2,1)S(1)} %section.6), channel_id=1, source_target_pairs={{0,4},{1,5},{2,6},{3,7},{4,0},{5,1},{6,2},{7,3},{8,12},{9,13},{10,... | collective-permute-start | bytes 786440 | tf_op jit(solution)/shard_map/ppermute | solution.py:93
  31.3 1.8 %section.7 = bf16[2,4,128,128]{3,2,1,0:T(8,128)(2,1)S(1)} custom-call(s32[258]{0:T(512)S(1)} %concatenate.3.info, bf16[4,8,128,128]{3,2,1,0:T(8,128)(2,1)S(1)} %bitcast.9, bf16[4,8,128,128]{3,2,1,0:T(8,128)(2,1)S(1)} %collective-permute-done.2.other_a, bf16[16,4,128,128]{3,2,1,0:T(8,128)(2,1)S(1)} %fold_left.7.left, bf16[2,3,128,128]{3,2,1,0:T(8,128)(2,1)S(1)} %copy-done.1, ...), custom_call_target="tpu_custom_call" | custom-call | flops 536870912 | bytes 4194304 | tf_op jit(solution)/shard_map/section/pallas_call | solution.py:152
  33.1 1.2 %collective-permute-start.17 = (bf16[2,4,128,128]{3,2,1,0:T(8,128)(2,1)S(1)}, bf16[2,4,128,128]{3,2,1,0:T(8,128)(2,1)S(1)}, u32[]{:S(2)}, u32[]{:S(2)}) collective-permute-start(bf16[2,4,128,128]{3,2,1,0:T(8,128)(2,1)S(1)} %section.7), channel_id=1, source_target_pairs={{0,2},{1,3},{2,0},{3,1},{4,6},{5,7},{6,4},{7,5},{8,10},{9,11},{10,... | collective-permute-start | bytes 786440 | tf_op jit(solution)/shard_map/ppermute | solution.py:93
  34.3 1.8 %section.4 = f32[2,4,128,128]{3,2,1,0:T(8,128)S(1)} custom-call(s32[258]{0:T(512)S(1)} %concatenate.3.info, bf16[4,8,128,128]{3,2,1,0:T(8,128)(2,1)S(1)} %bitcast.10, bf16[4,8,128,128]{3,2,1,0:T(8,128)(2,1)S(1)} %collective-permute-done.2.other_a, bf16[16,4,128,128]{3,2,1,0:T(8,128)(2,1)S(1)} %fold_left.7.left, bf16[2,3,128,128]{3,2,1,0:T(8,128)(2,1)S(1)} %copy-done.1, ...), custom_call_target="tpu_custom_call" | custom-call | flops 536870912 | bytes 4194304 | tf_op jit(solution)/shard_map/section/pallas_call | solution.py:152
  36.1 0.6 %collective-permute-done.15 = bf16[2,4,128,128]{3,2,1,0:T(8,128)(2,1)S(1)} collective-permute-done((bf16[2,4,128,128]{3,2,1,0:T(8,128)(2,1)S(1)}, bf16[2,4,128,128]{3,2,1,0:T(8,128)(2,1)S(1)}, u32[]{:S(2)}, u32[]{:S(2)}) %collective-permute-start.15) | collective-permute-done | bytes 262176 | tf_op jit(solution)/shard_map/ppermute | solution.py:93
  36.7 5.5 %collective-permute-done.16 = bf16[2,4,128,128]{3,2,1,0:T(8,128)(2,1)S(1)} collective-permute-done((bf16[2,4,128,128]{3,2,1,0:T(8,128)(2,1)S(1)}, bf16[2,4,128,128]{3,2,1,0:T(8,128)(2,1)S(1)}, u32[]{:S(2)}, u32[]{:S(2)}) %collective-permute-start.16) | collective-permute-done | bytes 262176 | tf_op jit(solution)/shard_map/ppermute | solution.py:93
  42.2 0.1 collective-permute-done.17
  42.3 0.9 %convert_add_fusion = f32[2,4,128,128]{3,2,1,0:T(8,128)} fusion(bf16[2,4,128,128]{3,2,1,0:T(8,128)(2,1)S(1)} %collective-permute-done.17, bf16[2,4,128,128]{3,2,1,0:T(8,128)(2,1)S(1)} %collective-permute-done.16, f32[2,4,128,128]{3,2,1,0:T(8,128)S(1)} %section.4, bf16[2,4,128,128]{3,2,1,0:T(8,128)(2,1)S(1)} %collective-permute-done.15), kind=kLoop, calls=%fused_computation | loop fusion | flops 786432 | bytes 1835008 | tf_op jit(solution)/shard_map/add | solution.py:176
  (10 shorter events, 0.0 us)
Async XLA Ops:
  0.0 7.3 %collective-permute-start.2 = (bf16[4,8,128,128]{3,2,1,0:T(8,128)(2,1)}, bf16[4,8,128,128]{3,2,1,0:T(8,128)(2,1)S(1)}, u32[]{:S(2)}, u32[]{:S(2)}) collective-permute-start(bf16[4,8,128,128]{3,2,1,0:T(8,128)(2,1)} %bitcast.6), channel_id=1, source_target_pairs={{0,1},{1,0},{2,3},{3,2},{4,5},{5,4},{6,7},{7,6},{8,9},{9,8},{10,11... | collective-permute-start | bytes 3145736 | tf_op jit(solution)/shard_map/ppermute | solution.py:93
  0.5 13.7 %collective-permute-start = (bf16[2,3,128,128]{3,2,1,0:T(8,128)(2,1)}, bf16[2,3,128,128]{3,2,1,0:T(8,128)(2,1)S(1)}, u32[]{:S(2)}, u32[]{:S(2)}) collective-permute-start(bf16[2,3,128,128]{3,2,1,0:T(8,128)(2,1)} %refs_0_.9), channel_id=1, source_target_pairs={{0,16},{8,24},{16,0},{24,8},{1,17},{9,25},{17,1},{25,9},{2,18},{10... | collective-permute-start | bytes 589832 | tf_op jit(solution)/shard_map/ppermute | solution.py:96
  4.0 16.2 %collective-permute-start.6 = (bf16[2,3,128,128]{3,2,1,0:T(8,128)(2,1)}, bf16[2,3,128,128]{3,2,1,0:T(8,128)(2,1)S(1)}, u32[]{:S(2)}, u32[]{:S(2)}) collective-permute-start(bf16[2,3,128,128]{3,2,1,0:T(8,128)(2,1)} %refs_0_.9), channel_id=1, source_target_pairs={{0,8},{8,0},{16,24},{24,16},{1,9},{9,1},{17,25},{25,17},{2,10},{10... | collective-permute-start | bytes 589832 | tf_op jit(solution)/shard_map/ppermute | solution.py:96
  6.4 4.8 %collective-permute-start.1 = (s32[4,8]{1,0:T(4,128)S(1)}, s32[4,8]{1,0:T(4,128)S(1)}, u32[]{:S(2)}, u32[]{:S(2)}) collective-permute-start(s32[4,8]{1,0:T(4,128)S(1)} %get-tuple-element.15), channel_id=1, source_target_pairs={{0,1},{1,0},{2,3},{3,2},{4,5},{5,4},{6,7},{7,6},{8,9},{9,8},{10,11... | collective-permute-start | bytes 392 | tf_op jit(solution)/shard_map/ppermute | solution.py:93
  7.3 7.9 %collective-permute-start.3 = (bf16[2,3,128,128]{3,2,1,0:T(8,128)(2,1)}, bf16[2,3,128,128]{3,2,1,0:T(8,128)(2,1)S(1)}, u32[]{:S(2)}, u32[]{:S(2)}) collective-permute-start(bf16[2,3,128,128]{3,2,1,0:T(8,128)(2,1)} %refs_0_.9), channel_id=1, source_target_pairs={{0,2},{1,3},{2,0},{3,1},{4,6},{5,7},{6,4},{7,5},{8,10},{9,11},{10,... | collective-permute-start | bytes 589832 | tf_op jit(solution)/shard_map/ppermute | solution.py:93
  8.8 11.5 %collective-permute-start.4 = (bf16[2,3,128,128]{3,2,1,0:T(8,128)(2,1)}, bf16[2,3,128,128]{3,2,1,0:T(8,128)(2,1)S(1)}, u32[]{:S(2)}, u32[]{:S(2)}) collective-permute-start(bf16[2,3,128,128]{3,2,1,0:T(8,128)(2,1)} %refs_0_.9), channel_id=1, source_target_pairs={{0,4},{1,5},{2,6},{3,7},{4,0},{5,1},{6,2},{7,3},{8,12},{9,13},{10,... | collective-permute-start | bytes 589832 | tf_op jit(solution)/shard_map/ppermute | solution.py:93
  11.4 9.4 %collective-permute-start.5 = (bf16[2,3,128,128]{3,2,1,0:T(8,128)(2,1)}, bf16[2,3,128,128]{3,2,1,0:T(8,128)(2,1)S(1)}, u32[]{:S(2)}, u32[]{:S(2)}) collective-permute-start(bf16[2,3,128,128]{3,2,1,0:T(8,128)(2,1)} %refs_0_.9), channel_id=1, source_target_pairs={{0,6},{1,7},{2,4},{3,5},{4,2},{5,3},{6,0},{7,1},{8,14},{9,15},{10,... | collective-permute-start | bytes 589832 | tf_op jit(solution)/shard_map/ppermute | solution.py:93
  14.1 6.7 %collective-permute-start.13 = (bf16[2,3,128,128]{3,2,1,0:T(8,128)(2,1)S(1)}, bf16[2,3,128,128]{3,2,1,0:T(8,128)(2,1)S(1)}, u32[]{:S(2)}, u32[]{:S(2)}) collective-permute-start(bf16[2,3,128,128]{3,2,1,0:T(8,128)(2,1)S(1)} %collective-permute-done.refs_4_), channel_id=1, source_target_pairs={{0,8},{8,0},{16,24},{24,16},{1,9},{9,1},{17,25},{25,17},{2,10},{10... | collective-permute-start | bytes 589832 | tf_op jit(solution)/shard_map/ppermute | solution.py:96
  15.2 6.1 %collective-permute-start.10 = (bf16[2,3,128,128]{3,2,1,0:T(8,128)(2,1)S(1)}, bf16[2,3,128,128]{3,2,1,0:T(8,128)(2,1)S(1)}, u32[]{:S(2)}, u32[]{:S(2)}) collective-permute-start(bf16[2,3,128,128]{3,2,1,0:T(8,128)(2,1)S(1)} %collective-permute-done.3.refs_0_), channel_id=1, source_target_pairs={{0,1},{1,0},{2,3},{3,2},{4,5},{5,4},{6,7},{7,6},{8,9},{9,8},{10,11... | collective-permute-start | bytes 589832 | tf_op jit(solution)/shard_map/ppermute | solution.py:93
  20.3 1.4 %collective-permute-start.9 = (bf16[2,3,128,128]{3,2,1,0:T(8,128)(2,1)S(1)}, bf16[2,3,128,128]{3,2,1,0:T(8,128)(2,1)S(1)}, u32[]{:S(2)}, u32[]{:S(2)}) collective-permute-start(bf16[2,3,128,128]{3,2,1,0:T(8,128)(2,1)S(1)} %collective-permute-done.4.refs_0_), channel_id=1, source_target_pairs={{0,1},{1,0},{2,3},{3,2},{4,5},{5,4},{6,7},{7,6},{8,9},{9,8},{10,11... | collective-permute-start | bytes 589832 | tf_op jit(solution)/shard_map/ppermute | solution.py:93
  20.3 4.7 %collective-permute-start.11 = (bf16[2,3,128,128]{3,2,1,0:T(8,128)(2,1)S(1)}, bf16[2,3,128,128]{3,2,1,0:T(8,128)(2,1)S(1)}, u32[]{:S(2)}, u32[]{:S(2)}) collective-permute-start(bf16[2,3,128,128]{3,2,1,0:T(8,128)(2,1)S(1)} %collective-permute-done.6.refs_2_), channel_id=1, source_target_pairs={{0,1},{1,0},{2,3},{3,2},{4,5},{5,4},{6,7},{7,6},{8,9},{9,8},{10,11... | collective-permute-start | bytes 589832 | tf_op jit(solution)/shard_map/ppermute | solution.py:93
  20.8 2.5 %collective-permute-start.8 = (bf16[2,3,128,128]{3,2,1,0:T(8,128)(2,1)S(1)}, bf16[2,3,128,128]{3,2,1,0:T(8,128)(2,1)S(1)}, u32[]{:S(2)}, u32[]{:S(2)}) collective-permute-start(bf16[2,3,128,128]{3,2,1,0:T(8,128)(2,1)S(1)} %collective-permute-done.5.refs_0_), channel_id=1, source_target_pairs={{0,1},{1,0},{2,3},{3,2},{4,5},{5,4},{6,7},{7,6},{8,9},{9,8},{10,11... | collective-permute-start | bytes 589832 | tf_op jit(solution)/shard_map/ppermute | solution.py:93
  20.9 3.2 %collective-permute-start.7 = (bf16[2,3,128,128]{3,2,1,0:T(8,128)(2,1)}, bf16[2,3,128,128]{3,2,1,0:T(8,128)(2,1)S(1)}, u32[]{:S(2)}, u32[]{:S(2)}) collective-permute-start(bf16[2,3,128,128]{3,2,1,0:T(8,128)(2,1)} %refs_0_.9), channel_id=1, source_target_pairs={{0,1},{1,0},{2,3},{3,2},{4,5},{5,4},{6,7},{7,6},{8,9},{9,8},{10,11... | collective-permute-start | bytes 589832 | tf_op jit(solution)/shard_map/ppermute | solution.py:93
  21.3 3.7 %collective-permute-start.12 = (bf16[2,3,128,128]{3,2,1,0:T(8,128)(2,1)S(1)}, bf16[2,3,128,128]{3,2,1,0:T(8,128)(2,1)S(1)}, u32[]{:S(2)}, u32[]{:S(2)}) collective-permute-start(bf16[2,3,128,128]{3,2,1,0:T(8,128)(2,1)S(1)} %collective-permute-done.refs_4_), channel_id=1, source_target_pairs={{0,1},{1,0},{2,3},{3,2},{4,5},{5,4},{6,7},{7,6},{8,9},{9,8},{10,11... | collective-permute-start | bytes 589832 | tf_op jit(solution)/shard_map/ppermute | solution.py:93
  21.7 3.3 %collective-permute-start.14 = (bf16[2,3,128,128]{3,2,1,0:T(8,128)(2,1)S(1)}, bf16[2,3,128,128]{3,2,1,0:T(8,128)(2,1)S(1)}, u32[]{:S(2)}, u32[]{:S(2)}) collective-permute-start(bf16[2,3,128,128]{3,2,1,0:T(8,128)(2,1)S(1)} %collective-permute-done.13.refs_6_), channel_id=1, source_target_pairs={{0,1},{1,0},{2,3},{3,2},{4,5},{5,4},{6,7},{7,6},{8,9},{9,8},{10,11... | collective-permute-start | bytes 589832 | tf_op jit(solution)/shard_map/ppermute | solution.py:93
  23.3 0.9 %copy-start.1 = (bf16[2,3,128,128]{3,2,1,0:T(8,128)(2,1)S(1)}, bf16[2,3,128,128]{3,2,1,0:T(8,128)(2,1)}, u32[]{:S(2)}) copy-start(bf16[2,3,128,128]{3,2,1,0:T(8,128)(2,1)} %refs_0_.9) | copy-start | bytes 589828
  24.1 1.3 %copy-start = (bf16[1,1,4,8,128,128]{5,4,3,2,1,0:T(8,128)(2,1)S(1)}, bf16[1,1,4,8,128,128]{5,4,3,2,1,0:T(8,128)(2,1)}, u32[]{:S(2)}) copy-start(bf16[1,1,4,8,128,128]{5,4,3,2,1,0:T(8,128)(2,1)} %param.6) | copy-start | bytes 3145732
  27.1 9.6 %collective-permute-start.15 = (bf16[2,4,128,128]{3,2,1,0:T(8,128)(2,1)S(1)}, bf16[2,4,128,128]{3,2,1,0:T(8,128)(2,1)S(1)}, u32[]{:S(2)}, u32[]{:S(2)}) collective-permute-start(bf16[2,4,128,128]{3,2,1,0:T(8,128)(2,1)S(1)} %section.5), channel_id=1, source_target_pairs={{0,6},{1,7},{2,4},{3,5},{4,2},{5,3},{6,0},{7,1},{8,14},{9,15},{10,... | collective-permute-start | bytes 786440 | tf_op jit(solution)/shard_map/ppermute | solution.py:93
  30.8 11.5 %collective-permute-start.16 = (bf16[2,4,128,128]{3,2,1,0:T(8,128)(2,1)S(1)}, bf16[2,4,128,128]{3,2,1,0:T(8,128)(2,1)S(1)}, u32[]{:S(2)}, u32[]{:S(2)}) collective-permute-start(bf16[2,4,128,128]{3,2,1,0:T(8,128)(2,1)S(1)} %section.6), channel_id=1, source_target_pairs={{0,4},{1,5},{2,6},{3,7},{4,0},{5,1},{6,2},{7,3},{8,12},{9,13},{10,... | collective-permute-start | bytes 786440 | tf_op jit(solution)/shard_map/ppermute | solution.py:93
  33.1 9.2 %collective-permute-start.17 = (bf16[2,4,128,128]{3,2,1,0:T(8,128)(2,1)S(1)}, bf16[2,4,128,128]{3,2,1,0:T(8,128)(2,1)S(1)}, u32[]{:S(2)}, u32[]{:S(2)}) collective-permute-start(bf16[2,4,128,128]{3,2,1,0:T(8,128)(2,1)S(1)} %section.7), channel_id=1, source_target_pairs={{0,2},{1,3},{2,0},{3,1},{4,6},{5,7},{6,4},{7,5},{8,10},{9,11},{10,... | collective-permute-start | bytes 786440 | tf_op jit(solution)/shard_map/ppermute | solution.py:93

commit v4 on v3

--- a/solution.py
+++ b/solution.py
@@ -11,14 +11,14 @@
 HALF = 2
 
 
-def fold_left(sizes, hop, info, *refs):
-    pieces, out = refs[:2], refs[-1]
+def fold_left(sizes, hops, info, *refs):
+    pieces, out = refs[: 2 * len(hops)], refs[-1]
     slots, segment, per_row, block = sizes
     table = 2 + slots * out.shape[0] // segment
     grid_row, grid_col = info[0], info[1]
-    for u, piece in enumerate(pieces):
+    for b, piece in enumerate(pieces):
         for seg in range(segment):
-            i = lax.bitwise_xor(grid_col, 2 * hop + u) * segment + seg
+            i = lax.bitwise_xor(grid_col, 2 * hops[b // 2] + b % 2) * segment + seg
             base = table + (grid_row * out.shape[0] + i) * per_row
             used = 0
             for q in range(per_row):
@@ -97,10 +97,12 @@
 
     own_a = a_vals.reshape(row_count, slots, block, block)
     position = lax.iota(jnp.int32, slots)[None, :]
-    codes = jnp.where(
-        position < a_live.reshape(row_count, 1),
-        a_rows.reshape(row_count, slots) * segment + a_cols.reshape(row_count, slots),
-        -1,
+    codes = lax.optimization_barrier(
+        jnp.where(
+            position < a_live.reshape(row_count, 1),
+            a_rows.reshape(row_count, slots) * segment + a_cols.reshape(row_count, slots),
+            -1,
+        )
     )
     other_codes = col_xor(codes, 1)
     info = jnp.concatenate(
@@ -127,23 +129,27 @@
     vmem = pl.BlockSpec(memory_space=pltpu.VMEM)
     hbm = pl.BlockSpec(memory_space=pl.ANY)
     folded_left = ()
-    for hop in [*range(1, row_count), 0]:
-        pair = (left[hop], col_xor(left[hop], 1) if hop else other_p)
+    for hops in (range(1, row_count), range(1)):
+        halves = [
+            half
+            for hop in hops
+            for half in (left[hop], col_xor(left[hop], 1) if hop else other_p)
+        ]
         folded_left = (
             pl.pallas_call(
-                functools.partial(fold_left, sizes, hop),
+                functools.partial(fold_left, sizes, hops),
                 out_shape=jax.ShapeDtypeStruct(
                     (segment * col_count, CROW, block, block), jnp.bfloat16
                 ),
-                in_specs=[smem, vmem, vmem] + [hbm] * len(folded_left),
+                in_specs=[smem] + [vmem] * len(halves) + [hbm] * len(folded_left),
                 out_specs=vmem,
-                input_output_aliases={3: 0} if folded_left else {},
-                compiler_params=pltpu.CompilerParams(vmem_limit_bytes=8 << 20),
+                input_output_aliases={1 + len(halves): 0} if folded_left else {},
+                compiler_params=pltpu.CompilerParams(vmem_limit_bytes=16 << 20),
                 cost_estimate=pl.CostEstimate(
                     flops=0, bytes_accessed=1 << 20, transcendentals=0
                 ),
                 name="fold_left",
-            )(info, *pair, *folded_left),
+            )(info, *halves, *folded_left),
         )
     (folded_left,) = folded_left
     depth = 2 * slots * block
@@ -169,7 +175,7 @@
         )(info, own_a, other_a, folded_left, *right)
 
     arrived = []
-    for hop in range(row_count - 1, 0, -1):
+    for hop in range(1, row_count):
         arrived.append(col_xor(partial_of(hop, jnp.bfloat16), 2 * hop))
     total = partial_of(0, jnp.float32)
     for piece in arrived:

time: 43.5 us -> 41.6 us (0.956)
  Pallas kernels: 9.91 us -> 8.68 us
  other arithmetic: 2.43 us -> 1.68 us
  waiting for transfers between devices: 14.3 us -> 14.9 us
    ppermute x3, waiting for transfers between devices: 2.24 us -> 4.57 us  [row_xor(): return lax.ppermute(x, 'row', [(r, r ^ b) for r in range(row_count)])]
    ppermute x15, waiting for transfers between devices: 12 us -> 10.4 us  [col_xor(): return lax.ppermute(x, 'col', [(c, c ^ b) for c in range(col_count)])]
    pallas_call x4 -> x2, Pallas kernels: 2.87 us -> 1.64 us  [local(): pl.pallas_call(functools.partial(fold_left, sizes, hops), out_shape=jax.S...]
    lt x1 -> x0, other arithmetic: 0.73 us -> none  [local(): position < a_live.reshape(row_count, 1)]
  transfers between devices with their start and end apart: 18 -> 18, of which waited for: 7 -> 7; matrix products, arithmetic and copies ran while one was open for 6% -> 5% of each run, Pallas kernels for 19% -> 17%
where the time goes in v4:
time: 41.6 us; the launch traced here: 41.4 us
  waiting for transfers between devices  14.9 us (36%)
  starting transfers between devices  14.7 us (35%)
  Pallas kernels  8.68 us (21%)
  other arithmetic  1.68 us (4%)
  local copies, waits for them, and re-layouts  1.29 us (3%)
    ppermute x15, waiting for transfers between devices, col_xor(): return lax.ppermute(x, 'col', [(c, c ^ b) for c in range(col_count)])  10.4 us
    ppermute x15, starting transfers between devices, col_xor(): return lax.ppermute(x, 'col', [(c, c ^ b) for c in range(col_count)])  8.8 us
    pallas_call x4, Pallas kernels, partial_of(): pl.pallas_call(functools.partial(section, sizes, hop), out_shape=jax.Shap...  7.04 us
    ppermute x3, starting transfers between devices, row_xor(): return lax.ppermute(x, 'row', [(r, r ^ b) for r in range(row_count)])  5.94 us
    ppermute x3, waiting for transfers between devices, row_xor(): return lax.ppermute(x, 'row', [(r, r ^ b) for r in range(row_count)])  4.57 us
    pallas_call x2, Pallas kernels, local(): pl.pallas_call(functools.partial(fold_left, sizes, hops), out_shape=jax.S...  1.64 us
    unnamed x5, local copies, waits for them, and re-layouts  0.91 us
    add x1, other arithmetic, local(): total = total + piece.astype(jnp.float32)  0.91 us
  transfers between devices with their start and end apart: 18, of which 7 were waited for; matrix products, arithmetic and copies ran while one was open for 5% of the time, Pallas kernels for 17%

profile of v4, /device:TPU:0, one launch (start us, length us, event | category | flops | bytes accessed | tf_op | source)
XLA Modules:
  0.0 41.4 jit_solution(9982238489627049572)
XLA Ops:
  0.0 0.5 %collective-permute-start.2 = (bf16[4,8,128,128]{3,2,1,0:T(8,128)(2,1)}, bf16[4,8,128,128]{3,2,1,0:T(8,128)(2,1)S(1)}, u32[]{:S(2)}, u32[]{:S(2)}) collective-permute-start(bf16[4,8,128,128]{3,2,1,0:T(8,128)(2,1)} %bitcast.6), channel_id=1, source_target_pairs={{0,1},{1,0},{2,3},{3,2},{4,5},{5,4},{6,7},{7,6},{8,9},{9,8},{10,11... | collective-permute-start | bytes 3145736 | tf_op jit(solution)/shard_map/ppermute | solution.py:93
  0.5 3.6 %collective-permute-start = (bf16[2,3,128,128]{3,2,1,0:T(8,128)(2,1)}, bf16[2,3,128,128]{3,2,1,0:T(8,128)(2,1)S(1)}, u32[]{:S(2)}, u32[]{:S(2)}) collective-permute-start(bf16[2,3,128,128]{3,2,1,0:T(8,128)(2,1)} %refs_0_.9), channel_id=1, source_target_pairs={{0,16},{8,24},{16,0},{24,8},{1,17},{9,25},{17,1},{25,9},{2,18},{10... | collective-permute-start | bytes 589832 | tf_op jit(solution)/shard_map/ppermute | solution.py:96
  4.1 1.6 %collective-permute-start.6 = (bf16[2,3,128,128]{3,2,1,0:T(8,128)(2,1)}, bf16[2,3,128,128]{3,2,1,0:T(8,128)(2,1)S(1)}, u32[]{:S(2)}, u32[]{:S(2)}) collective-permute-start(bf16[2,3,128,128]{3,2,1,0:T(8,128)(2,1)} %refs_0_.9), channel_id=1, source_target_pairs={{0,8},{8,0},{16,24},{24,16},{1,9},{9,1},{17,25},{25,17},{2,10},{10... | collective-permute-start | bytes 589832 | tf_op jit(solution)/shard_map/ppermute | solution.py:96
  5.7 0.0 collective-permute-done.2.other_a
  5.7 1.5 %collective-permute-start.3 = (bf16[2,3,128,128]{3,2,1,0:T(8,128)(2,1)}, bf16[2,3,128,128]{3,2,1,0:T(8,128)(2,1)S(1)}, u32[]{:S(2)}, u32[]{:S(2)}) collective-permute-start(bf16[2,3,128,128]{3,2,1,0:T(8,128)(2,1)} %refs_0_.9), channel_id=1, source_target_pairs={{0,2},{1,3},{2,0},{3,1},{4,6},{5,7},{6,4},{7,5},{8,10},{9,11},{10,... | collective-permute-start | bytes 589832 | tf_op jit(solution)/shard_map/ppermute | solution.py:93
  7.2 1.5 %collective-permute-start.4 = (bf16[2,3,128,128]{3,2,1,0:T(8,128)(2,1)}, bf16[2,3,128,128]{3,2,1,0:T(8,128)(2,1)S(1)}, u32[]{:S(2)}, u32[]{:S(2)}) collective-permute-start(bf16[2,3,128,128]{3,2,1,0:T(8,128)(2,1)} %refs_0_.9), channel_id=1, source_target_pairs={{0,4},{1,5},{2,6},{3,7},{4,0},{5,1},{6,2},{7,3},{8,12},{9,13},{10,... | collective-permute-start | bytes 589832 | tf_op jit(solution)/shard_map/ppermute | solution.py:93
  8.7 0.8 %bitcast_select_fusion = s32[4,8]{1,0:T(4,128)S(1)} fusion(s32[1,1,4,8]{3,2,1,0:T(4,128)} %param.8, s32[1,1,4,8]{3,2,1,0:T(4,128)} %param.7, s32[4]{0:T(128)} %bitcast.11), kind=kLoop, calls=%fused_computation.1 | loop fusion | flops 128 | bytes 400 | tf_op jit(solution)/shard_map/jit(_where)/select_n | solution.py:101
  9.5 0.0 collective-permute-start.1
  9.5 0.1 reshape.19
  9.6 0.8 %copy.8 = s32[64,3]{1,0:T(8,128)S(1)} copy(s32[64,3]{0,1:T(4,128)} %param.11) | data formatting | bytes 1536 | tf_op args[5]
  10.3 0.1 reshape.21
  10.5 0.2 collective-permute-done.1
  10.6 0.1 reshape.20
  10.7 0.1 concatenate.3.info
  10.8 0.5 %collective-permute-start.5 = (bf16[2,3,128,128]{3,2,1,0:T(8,128)(2,1)}, bf16[2,3,128,128]{3,2,1,0:T(8,128)(2,1)S(1)}, u32[]{:S(2)}, u32[]{:S(2)}) collective-permute-start(bf16[2,3,128,128]{3,2,1,0:T(8,128)(2,1)} %refs_0_.9), channel_id=1, source_target_pairs={{0,6},{1,7},{2,4},{3,5},{4,2},{5,3},{6,0},{7,1},{8,14},{9,15},{10,... | collective-permute-start | bytes 589832 | tf_op jit(solution)/shard_map/ppermute | solution.py:93
  11.3 2.9 %collective-permute-done.refs_4_ = bf16[2,3,128,128]{3,2,1,0:T(8,128)(2,1)S(1)} collective-permute-done((bf16[2,3,128,128]{3,2,1,0:T(8,128)(2,1)}, bf16[2,3,128,128]{3,2,1,0:T(8,128)(2,1)S(1)}, u32[]{:S(2)}, u32[]{:S(2)}) %collective-permute-start) | collective-permute-done | bytes 196640 | tf_op jit(solution)/shard_map/ppermute | solution.py:96
  14.1 0.7 %collective-permute-start.13 = (bf16[2,3,128,128]{3,2,1,0:T(8,128)(2,1)S(1)}, bf16[2,3,128,128]{3,2,1,0:T(8,128)(2,1)S(1)}, u32[]{:S(2)}, u32[]{:S(2)}) collective-permute-start(bf16[2,3,128,128]{3,2,1,0:T(8,128)(2,1)S(1)} %collective-permute-done.refs_4_), channel_id=1, source_target_pairs={{0,8},{8,0},{16,24},{24,16},{1,9},{9,1},{17,25},{25,17},{2,10},{10... | collective-permute-start | bytes 589832 | tf_op jit(solution)/shard_map/ppermute | solution.py:96
  14.9 0.0 collective-permute-done.3.refs_0_
  14.9 0.0 collective-permute-done.4.refs_2_
  14.9 0.5 %collective-permute-start.9 = (bf16[2,3,128,128]{3,2,1,0:T(8,128)(2,1)S(1)}, bf16[2,3,128,128]{3,2,1,0:T(8,128)(2,1)S(1)}, u32[]{:S(2)}, u32[]{:S(2)}) collective-permute-start(bf16[2,3,128,128]{3,2,1,0:T(8,128)(2,1)S(1)} %collective-permute-done.4.refs_2_), channel_id=1, source_target_pairs={{0,1},{1,0},{2,3},{3,2},{4,5},{5,4},{6,7},{7,6},{8,9},{9,8},{10,11... | collective-permute-start | bytes 589832 | tf_op jit(solution)/shard_map/ppermute | solution.py:93
  15.4 0.1 collective-permute-start.11
  15.5 3.6 %collective-permute-done.5.refs_4_ = bf16[2,3,128,128]{3,2,1,0:T(8,128)(2,1)S(1)} collective-permute-done((bf16[2,3,128,128]{3,2,1,0:T(8,128)(2,1)}, bf16[2,3,128,128]{3,2,1,0:T(8,128)(2,1)S(1)}, u32[]{:S(2)}, u32[]{:S(2)}) %collective-permute-start.5) | collective-permute-done | bytes 196640 | tf_op jit(solution)/shard_map/ppermute | solution.py:93
  19.1 0.0 collective-permute-start.10
  19.1 1.7 %collective-permute-done.13.refs_6_ = bf16[2,3,128,128]{3,2,1,0:T(8,128)(2,1)S(1)} collective-permute-done((bf16[2,3,128,128]{3,2,1,0:T(8,128)(2,1)S(1)}, bf16[2,3,128,128]{3,2,1,0:T(8,128)(2,1)S(1)}, u32[]{:S(2)}, u32[]{:S(2)}) %collective-permute-start.13) | collective-permute-done | bytes 196640 | tf_op jit(solution)/shard_map/ppermute | solution.py:96
  20.8 0.0 collective-permute-start.7
  20.8 0.0 collective-permute-done.8.refs_1_
  20.8 0.5 %collective-permute-start.12 = (bf16[2,3,128,128]{3,2,1,0:T(8,128)(2,1)S(1)}, bf16[2,3,128,128]{3,2,1,0:T(8,128)(2,1)S(1)}, u32[]{:S(2)}, u32[]{:S(2)}) collective-permute-start(bf16[2,3,128,128]{3,2,1,0:T(8,128)(2,1)S(1)} %collective-permute-done.refs_4_), channel_id=1, source_target_pairs={{0,1},{1,0},{2,3},{3,2},{4,5},{5,4},{6,7},{7,6},{8,9},{9,8},{10,11... | collective-permute-start | bytes 589832 | tf_op jit(solution)/shard_map/ppermute | solution.py:93
  21.3 0.0 collective-permute-done.9.refs_3_
  21.3 0.1 collective-permute-start.14
  21.3 0.0 collective-permute-done.10.refs_5_
  21.3 0.9 %fold_left.2.refs_2_ = bf16[16,4,128,128]{3,2,1,0:T(8,128)(2,1)S(1)} custom-call(s32[258]{0:T(512)S(1)} %concatenate.3.info, bf16[2,3,128,128]{3,2,1,0:T(8,128)(2,1)S(1)} %collective-permute-done.3.refs_0_, bf16[2,3,128,128]{3,2,1,0:T(8,128)(2,1)S(1)} %collective-permute-done.8.refs_1_, bf16[2,3,128,128]{3,2,1,0:T(8,128)(2,1)S(1)} %collective-permute-done.4.refs_2_, ...), custom_call_target="tpu_custom_call" | custom-call | bytes 1048576 | tf_op jit(solution)/shard_map/fold_left/pallas_call | solution.py:139
  22.3 0.0 copy-start
  22.3 0.3 collective-permute-done.7.refs_1_
  22.6 0.7 %fold_left.3.left = bf16[16,4,128,128]{3,2,1,0:T(8,128)(2,1)S(1)} custom-call(s32[258]{0:T(512)S(1)} %concatenate.3.info, bf16[2,3,128,128]{3,2,1,0:T(8,128)(2,1)S(1)} %copy-done.1, bf16[2,3,128,128]{3,2,1,0:T(8,128)(2,1)S(1)} %collective-permute-done.7.refs_1_, bf16[16,4,128,128]{3,2,1,0:T(8,128)(2,1)S(1)} %fold_left.2.refs_2_), custom_call_target="tpu_custom_call", output_to_operand_aliasing={{}: (3, {})} | custom-call | bytes 1048576 | tf_op jit(solution)/shard_map/fold_left/pallas_call | solution.py:139
  23.3 0.0 collective-permute-done.11.refs_3_
  23.3 0.0 collective-permute-done.12.refs_5_
  23.4 0.1 copy-done
  23.5 1.8 %section.7 = bf16[2,4,128,128]{3,2,1,0:T(8,128)(2,1)S(1)} custom-call(s32[258]{0:T(512)S(1)} %concatenate.3.info, bf16[4,8,128,128]{3,2,1,0:T(8,128)(2,1)S(1)} %bitcast.7, bf16[4,8,128,128]{3,2,1,0:T(8,128)(2,1)S(1)} %collective-permute-done.2.other_a, bf16[16,4,128,128]{3,2,1,0:T(8,128)(2,1)S(1)} %fold_left.3.left, bf16[2,3,128,128]{3,2,1,0:T(8,128)(2,1)S(1)} %copy-done.1, ...), custom_call_target="tpu_custom_call" | custom-call | flops 536870912 | bytes 4194304 | tf_op jit(solution)/shard_map/section/pallas_call | solution.py:158
  25.3 2.4 %collective-permute-start.17 = (bf16[2,4,128,128]{3,2,1,0:T(8,128)(2,1)S(1)}, bf16[2,4,128,128]{3,2,1,0:T(8,128)(2,1)S(1)}, u32[]{:S(2)}, u32[]{:S(2)}) collective-permute-start(bf16[2,4,128,128]{3,2,1,0:T(8,128)(2,1)S(1)} %section.7), channel_id=1, source_target_pairs={{0,6},{1,7},{2,4},{3,5},{4,2},{5,3},{6,0},{7,1},{8,14},{9,15},{10,... | collective-permute-start | bytes 786440 | tf_op jit(solution)/shard_map/ppermute | solution.py:93
  27.6 1.8 %section.6 = bf16[2,4,128,128]{3,2,1,0:T(8,128)(2,1)S(1)} custom-call(s32[258]{0:T(512)S(1)} %concatenate.3.info, bf16[4,8,128,128]{3,2,1,0:T(8,128)(2,1)S(1)} %bitcast.8, bf16[4,8,128,128]{3,2,1,0:T(8,128)(2,1)S(1)} %collective-permute-done.2.other_a, bf16[16,4,128,128]{3,2,1,0:T(8,128)(2,1)S(1)} %fold_left.3.left, bf16[2,3,128,128]{3,2,1,0:T(8,128)(2,1)S(1)} %copy-done.1, ...), custom_call_target="tpu_custom_call" | custom-call | flops 536870912 | bytes 4194304 | tf_op jit(solution)/shard_map/section/pallas_call | solution.py:158
  29.4 0.6 %collective-permute-start.16 = (bf16[2,4,128,128]{3,2,1,0:T(8,128)(2,1)S(1)}, bf16[2,4,128,128]{3,2,1,0:T(8,128)(2,1)S(1)}, u32[]{:S(2)}, u32[]{:S(2)}) collective-permute-start(bf16[2,4,128,128]{3,2,1,0:T(8,128)(2,1)S(1)} %section.6), channel_id=1, source_target_pairs={{0,4},{1,5},{2,6},{3,7},{4,0},{5,1},{6,2},{7,3},{8,12},{9,13},{10,... | collective-permute-start | bytes 786440 | tf_op jit(solution)/shard_map/ppermute | solution.py:93
  30.0 1.8 %section.5 = bf16[2,4,128,128]{3,2,1,0:T(8,128)(2,1)S(1)} custom-call(s32[258]{0:T(512)S(1)} %concatenate.3.info, bf16[4,8,128,128]{3,2,1,0:T(8,128)(2,1)S(1)} %bitcast.9, bf16[4,8,128,128]{3,2,1,0:T(8,128)(2,1)S(1)} %collective-permute-done.2.other_a, bf16[16,4,128,128]{3,2,1,0:T(8,128)(2,1)S(1)} %fold_left.3.left, bf16[2,3,128,128]{3,2,1,0:T(8,128)(2,1)S(1)} %copy-done.1, ...), custom_call_target="tpu_custom_call" | custom-call | flops 536870912 | bytes 4194304 | tf_op jit(solution)/shard_map/section/pallas_call | solution.py:158
  31.7 0.8 %collective-permute-start.15 = (bf16[2,4,128,128]{3,2,1,0:T(8,128)(2,1)S(1)}, bf16[2,4,128,128]{3,2,1,0:T(8,128)(2,1)S(1)}, u32[]{:S(2)}, u32[]{:S(2)}) collective-permute-start(bf16[2,4,128,128]{3,2,1,0:T(8,128)(2,1)S(1)} %section.5), channel_id=1, source_target_pairs={{0,2},{1,3},{2,0},{3,1},{4,6},{5,7},{6,4},{7,5},{8,10},{9,11},{10,... | collective-permute-start | bytes 786440 | tf_op jit(solution)/shard_map/ppermute | solution.py:93
  32.5 1.8 %section.4 = f32[2,4,128,128]{3,2,1,0:T(8,128)S(1)} custom-call(s32[258]{0:T(512)S(1)} %concatenate.3.info, bf16[4,8,128,128]{3,2,1,0:T(8,128)(2,1)S(1)} %bitcast.10, bf16[4,8,128,128]{3,2,1,0:T(8,128)(2,1)S(1)} %collective-permute-done.2.other_a, bf16[16,4,128,128]{3,2,1,0:T(8,128)(2,1)S(1)} %fold_left.3.left, bf16[2,3,128,128]{3,2,1,0:T(8,128)(2,1)S(1)} %copy-done.1, ...), custom_call_target="tpu_custom_call" | custom-call | flops 536870912 | bytes 4194304 | tf_op jit(solution)/shard_map/section/pallas_call | solution.py:158
  34.3 0.7 %collective-permute-done.17 = bf16[2,4,128,128]{3,2,1,0:T(8,128)(2,1)S(1)} collective-permute-done((bf16[2,4,128,128]{3,2,1,0:T(8,128)(2,1)S(1)}, bf16[2,4,128,128]{3,2,1,0:T(8,128)(2,1)S(1)}, u32[]{:S(2)}, u32[]{:S(2)}) %collective-permute-start.17) | collective-permute-done | bytes 262176 | tf_op jit(solution)/shard_map/ppermute | solution.py:93
  35.0 5.5 %collective-permute-done.16 = bf16[2,4,128,128]{3,2,1,0:T(8,128)(2,1)S(1)} collective-permute-done((bf16[2,4,128,128]{3,2,1,0:T(8,128)(2,1)S(1)}, bf16[2,4,128,128]{3,2,1,0:T(8,128)(2,1)S(1)}, u32[]{:S(2)}, u32[]{:S(2)}) %collective-permute-start.16) | collective-permute-done | bytes 262176 | tf_op jit(solution)/shard_map/ppermute | solution.py:93
  40.5 0.0 collective-permute-done.15
  40.5 0.9 %convert_add_fusion = f32[2,4,128,128]{3,2,1,0:T(8,128)} fusion(bf16[2,4,128,128]{3,2,1,0:T(8,128)(2,1)S(1)} %collective-permute-done.17, bf16[2,4,128,128]{3,2,1,0:T(8,128)(2,1)S(1)} %collective-permute-done.16, f32[2,4,128,128]{3,2,1,0:T(8,128)S(1)} %section.4, bf16[2,4,128,128]{3,2,1,0:T(8,128)(2,1)S(1)} %collective-permute-done.15), kind=kLoop, calls=%fused_computation | loop fusion | flops 786432 | bytes 1835008 | tf_op jit(solution)/shard_map/add | solution.py:182
  (5 shorter events, 0.0 us)
Async XLA Ops:
  0.0 22.6 %copy-start.1 = (bf16[2,3,128,128]{3,2,1,0:T(8,128)(2,1)S(1)}, bf16[2,3,128,128]{3,2,1,0:T(8,128)(2,1)}, u32[]{:S(2)}) copy-start(bf16[2,3,128,128]{3,2,1,0:T(8,128)(2,1)} %refs_0_.9) | copy-start | bytes 589828
  0.0 5.7 %collective-permute-start.2 = (bf16[4,8,128,128]{3,2,1,0:T(8,128)(2,1)}, bf16[4,8,128,128]{3,2,1,0:T(8,128)(2,1)S(1)}, u32[]{:S(2)}, u32[]{:S(2)}) collective-permute-start(bf16[4,8,128,128]{3,2,1,0:T(8,128)(2,1)} %bitcast.6), channel_id=1, source_target_pairs={{0,1},{1,0},{2,3},{3,2},{4,5},{5,4},{6,7},{7,6},{8,9},{9,8},{10,11... | collective-permute-start | bytes 3145736 | tf_op jit(solution)/shard_map/ppermute | solution.py:93
  0.5 13.7 %collective-permute-start = (bf16[2,3,128,128]{3,2,1,0:T(8,128)(2,1)}, bf16[2,3,128,128]{3,2,1,0:T(8,128)(2,1)S(1)}, u32[]{:S(2)}, u32[]{:S(2)}) collective-permute-start(bf16[2,3,128,128]{3,2,1,0:T(8,128)(2,1)} %refs_0_.9), channel_id=1, source_target_pairs={{0,16},{8,24},{16,0},{24,8},{1,17},{9,25},{17,1},{25,9},{2,18},{10... | collective-permute-start | bytes 589832 | tf_op jit(solution)/shard_map/ppermute | solution.py:96
  4.1 11.3 %collective-permute-start.6 = (bf16[2,3,128,128]{3,2,1,0:T(8,128)(2,1)}, bf16[2,3,128,128]{3,2,1,0:T(8,128)(2,1)S(1)}, u32[]{:S(2)}, u32[]{:S(2)}) collective-permute-start(bf16[2,3,128,128]{3,2,1,0:T(8,128)(2,1)} %refs_0_.9), channel_id=1, source_target_pairs={{0,8},{8,0},{16,24},{24,16},{1,9},{9,1},{17,25},{25,17},{2,10},{10... | collective-permute-start | bytes 589832 | tf_op jit(solution)/shard_map/ppermute | solution.py:96
  5.7 9.2 %collective-permute-start.3 = (bf16[2,3,128,128]{3,2,1,0:T(8,128)(2,1)}, bf16[2,3,128,128]{3,2,1,0:T(8,128)(2,1)S(1)}, u32[]{:S(2)}, u32[]{:S(2)}) collective-permute-start(bf16[2,3,128,128]{3,2,1,0:T(8,128)(2,1)} %refs_0_.9), channel_id=1, source_target_pairs={{0,2},{1,3},{2,0},{3,1},{4,6},{5,7},{6,4},{7,5},{8,10},{9,11},{10,... | collective-permute-start | bytes 589832 | tf_op jit(solution)/shard_map/ppermute | solution.py:93
  7.2 7.7 %collective-permute-start.4 = (bf16[2,3,128,128]{3,2,1,0:T(8,128)(2,1)}, bf16[2,3,128,128]{3,2,1,0:T(8,128)(2,1)S(1)}, u32[]{:S(2)}, u32[]{:S(2)}) collective-permute-start(bf16[2,3,128,128]{3,2,1,0:T(8,128)(2,1)} %refs_0_.9), channel_id=1, source_target_pairs={{0,4},{1,5},{2,6},{3,7},{4,0},{5,1},{6,2},{7,3},{8,12},{9,13},{10,... | collective-permute-start | bytes 589832 | tf_op jit(solution)/shard_map/ppermute | solution.py:93
  9.5 1.2 %collective-permute-start.1 = (s32[4,8]{1,0:T(4,128)S(1)}, s32[4,8]{1,0:T(4,128)S(1)}, u32[]{:S(2)}, u32[]{:S(2)}) collective-permute-start(s32[4,8]{1,0:T(4,128)S(1)} %bitcast_select_fusion), channel_id=1, source_target_pairs={{0,1},{1,0},{2,3},{3,2},{4,5},{5,4},{6,7},{7,6},{8,9},{9,8},{10,11... | collective-permute-start | bytes 392 | tf_op jit(solution)/shard_map/ppermute | solution.py:93
  10.8 8.3 %collective-permute-start.5 = (bf16[2,3,128,128]{3,2,1,0:T(8,128)(2,1)}, bf16[2,3,128,128]{3,2,1,0:T(8,128)(2,1)S(1)}, u32[]{:S(2)}, u32[]{:S(2)}) collective-permute-start(bf16[2,3,128,128]{3,2,1,0:T(8,128)(2,1)} %refs_0_.9), channel_id=1, source_target_pairs={{0,6},{1,7},{2,4},{3,5},{4,2},{5,3},{6,0},{7,1},{8,14},{9,15},{10,... | collective-permute-start | bytes 589832 | tf_op jit(solution)/shard_map/ppermute | solution.py:93
  14.1 6.6 %collective-permute-start.13 = (bf16[2,3,128,128]{3,2,1,0:T(8,128)(2,1)S(1)}, bf16[2,3,128,128]{3,2,1,0:T(8,128)(2,1)S(1)}, u32[]{:S(2)}, u32[]{:S(2)}) collective-permute-start(bf16[2,3,128,128]{3,2,1,0:T(8,128)(2,1)S(1)} %collective-permute-done.refs_4_), channel_id=1, source_target_pairs={{0,8},{8,0},{16,24},{24,16},{1,9},{9,1},{17,25},{25,17},{2,10},{10... | collective-permute-start | bytes 589832 | tf_op jit(solution)/shard_map/ppermute | solution.py:96
  14.9 5.9 %collective-permute-start.8 = (bf16[2,3,128,128]{3,2,1,0:T(8,128)(2,1)S(1)}, bf16[2,3,128,128]{3,2,1,0:T(8,128)(2,1)S(1)}, u32[]{:S(2)}, u32[]{:S(2)}) collective-permute-start(bf16[2,3,128,128]{3,2,1,0:T(8,128)(2,1)S(1)} %collective-permute-done.3.refs_0_), channel_id=1, source_target_pairs={{0,1},{1,0},{2,3},{3,2},{4,5},{5,4},{6,7},{7,6},{8,9},{9,8},{10,11... | collective-permute-start | bytes 589832 | tf_op jit(solution)/shard_map/ppermute | solution.py:93
  14.9 6.4 %collective-permute-start.9 = (bf16[2,3,128,128]{3,2,1,0:T(8,128)(2,1)S(1)}, bf16[2,3,128,128]{3,2,1,0:T(8,128)(2,1)S(1)}, u32[]{:S(2)}, u32[]{:S(2)}) collective-permute-start(bf16[2,3,128,128]{3,2,1,0:T(8,128)(2,1)S(1)} %collective-permute-done.4.refs_2_), channel_id=1, source_target_pairs={{0,1},{1,0},{2,3},{3,2},{4,5},{5,4},{6,7},{7,6},{8,9},{9,8},{10,11... | collective-permute-start | bytes 589832 | tf_op jit(solution)/shard_map/ppermute | solution.py:93
  15.4 8.0 %collective-permute-start.11 = (bf16[2,3,128,128]{3,2,1,0:T(8,128)(2,1)S(1)}, bf16[2,3,128,128]{3,2,1,0:T(8,128)(2,1)S(1)}, u32[]{:S(2)}, u32[]{:S(2)}) collective-permute-start(bf16[2,3,128,128]{3,2,1,0:T(8,128)(2,1)S(1)} %collective-permute-done.6.refs_2_), channel_id=1, source_target_pairs={{0,1},{1,0},{2,3},{3,2},{4,5},{5,4},{6,7},{7,6},{8,9},{9,8},{10,11... | collective-permute-start | bytes 589832 | tf_op jit(solution)/shard_map/ppermute | solution.py:93
  19.1 2.3 %collective-permute-start.10 = (bf16[2,3,128,128]{3,2,1,0:T(8,128)(2,1)S(1)}, bf16[2,3,128,128]{3,2,1,0:T(8,128)(2,1)S(1)}, u32[]{:S(2)}, u32[]{:S(2)}) collective-permute-start(bf16[2,3,128,128]{3,2,1,0:T(8,128)(2,1)S(1)} %collective-permute-done.5.refs_4_), channel_id=1, source_target_pairs={{0,1},{1,0},{2,3},{3,2},{4,5},{5,4},{6,7},{7,6},{8,9},{9,8},{10,11... | collective-permute-start | bytes 589832 | tf_op jit(solution)/shard_map/ppermute | solution.py:93
  20.8 1.9 %collective-permute-start.7 = (bf16[2,3,128,128]{3,2,1,0:T(8,128)(2,1)}, bf16[2,3,128,128]{3,2,1,0:T(8,128)(2,1)S(1)}, u32[]{:S(2)}, u32[]{:S(2)}) collective-permute-start(bf16[2,3,128,128]{3,2,1,0:T(8,128)(2,1)} %refs_0_.9), channel_id=1, source_target_pairs={{0,1},{1,0},{2,3},{3,2},{4,5},{5,4},{6,7},{7,6},{8,9},{9,8},{10,11... | collective-permute-start | bytes 589832 | tf_op jit(solution)/shard_map/ppermute | solution.py:93
  20.8 2.6 %collective-permute-start.12 = (bf16[2,3,128,128]{3,2,1,0:T(8,128)(2,1)S(1)}, bf16[2,3,128,128]{3,2,1,0:T(8,128)(2,1)S(1)}, u32[]{:S(2)}, u32[]{:S(2)}) collective-permute-start(bf16[2,3,128,128]{3,2,1,0:T(8,128)(2,1)S(1)} %collective-permute-done.refs_4_), channel_id=1, source_target_pairs={{0,1},{1,0},{2,3},{3,2},{4,5},{5,4},{6,7},{7,6},{8,9},{9,8},{10,11... | collective-permute-start | bytes 589832 | tf_op jit(solution)/shard_map/ppermute | solution.py:93
  21.3 2.1 %collective-permute-start.14 = (bf16[2,3,128,128]{3,2,1,0:T(8,128)(2,1)S(1)}, bf16[2,3,128,128]{3,2,1,0:T(8,128)(2,1)S(1)}, u32[]{:S(2)}, u32[]{:S(2)}) collective-permute-start(bf16[2,3,128,128]{3,2,1,0:T(8,128)(2,1)S(1)} %collective-permute-done.13.refs_6_), channel_id=1, source_target_pairs={{0,1},{1,0},{2,3},{3,2},{4,5},{5,4},{6,7},{7,6},{8,9},{9,8},{10,11... | collective-permute-start | bytes 589832 | tf_op jit(solution)/shard_map/ppermute | solution.py:93
  22.3 1.2 %copy-start = (bf16[1,1,4,8,128,128]{5,4,3,2,1,0:T(8,128)(2,1)S(1)}, bf16[1,1,4,8,128,128]{5,4,3,2,1,0:T(8,128)(2,1)}, u32[]{:S(2)}) copy-start(bf16[1,1,4,8,128,128]{5,4,3,2,1,0:T(8,128)(2,1)} %param.6) | copy-start | bytes 3145732
  25.3 9.7 %collective-permute-start.17 = (bf16[2,4,128,128]{3,2,1,0:T(8,128)(2,1)S(1)}, bf16[2,4,128,128]{3,2,1,0:T(8,128)(2,1)S(1)}, u32[]{:S(2)}, u32[]{:S(2)}) collective-permute-start(bf16[2,4,128,128]{3,2,1,0:T(8,128)(2,1)S(1)} %section.7), channel_id=1, source_target_pairs={{0,6},{1,7},{2,4},{3,5},{4,2},{5,3},{6,0},{7,1},{8,14},{9,15},{10,... | collective-permute-start | bytes 786440 | tf_op jit(solution)/shard_map/ppermute | solution.py:93
  29.4 11.1 %collective-permute-start.16 = (bf16[2,4,128,128]{3,2,1,0:T(8,128)(2,1)S(1)}, bf16[2,4,128,128]{3,2,1,0:T(8,128)(2,1)S(1)}, u32[]{:S(2)}, u32[]{:S(2)}) collective-permute-start(bf16[2,4,128,128]{3,2,1,0:T(8,128)(2,1)S(1)} %section.6), channel_id=1, source_target_pairs={{0,4},{1,5},{2,6},{3,7},{4,0},{5,1},{6,2},{7,3},{8,12},{9,13},{10,... | collective-permute-start | bytes 786440 | tf_op jit(solution)/shard_map/ppermute | solution.py:93
  31.7 8.8 %collective-permute-start.15 = (bf16[2,4,128,128]{3,2,1,0:T(8,128)(2,1)S(1)}, bf16[2,4,128,128]{3,2,1,0:T(8,128)(2,1)S(1)}, u32[]{:S(2)}, u32[]{:S(2)}) collective-permute-start(bf16[2,4,128,128]{3,2,1,0:T(8,128)(2,1)S(1)} %section.5), channel_id=1, source_target_pairs={{0,2},{1,3},{2,0},{3,1},{4,6},{5,7},{6,4},{7,5},{8,10},{9,11},{10,... | collective-permute-start | bytes 786440 | tf_op jit(solution)/shard_map/ppermute | solution.py:93

commit v5 on v4

--- a/solution.py
+++ b/solution.py
@@ -114,7 +114,7 @@
         ]
     )
     near_p, other_a = lax.optimization_barrier((p_vals, col_xor(own_a, 1)))
-    left = [p_vals] + [col_xor(near_p, 2 * e) for e in range(1, row_count)]
+    left = [p_vals] + [col_xor(near_p if e > 1 else p_vals, 2 * e) for e in range(1, row_count)]
     right = [p_vals] + [None] * (row_count - 1)
     for d in sorted(range(1, row_count), key=lambda d: (d.bit_count(), -d)):
         piece = right[d & (d - 1)]

time: 41.6 us -> 41.1 us (0.988)
  waiting for transfers between devices: 14.9 us -> 14.1 us
    ppermute x15, waiting for transfers between devices: 10.4 us -> 9.53 us  [col_xor(): return lax.ppermute(x, 'col', [(c, c ^ b) for c in range(col_count)])]
where the time goes in v5:
time: 41.1 us; the launch traced here: 40.9 us
  starting transfers between devices  14.7 us (36%)
  waiting for transfers between devices  14.1 us (34%)
  Pallas kernels  8.69 us (21%)
  other arithmetic  1.68 us (4%)
  local copies, waits for them, and re-layouts  1.59 us (4%)
    ppermute x15, waiting for transfers between devices, col_xor(): return lax.ppermute(x, 'col', [(c, c ^ b) for c in range(col_count)])  9.53 us
    ppermute x15, starting transfers between devices, col_xor(): return lax.ppermute(x, 'col', [(c, c ^ b) for c in range(col_count)])  8.72 us
    pallas_call x4, Pallas kernels, partial_of(): pl.pallas_call(functools.partial(section, sizes, hop), out_shape=jax.Shap...  7.05 us
    ppermute x3, starting transfers between devices, row_xor(): return lax.ppermute(x, 'row', [(r, r ^ b) for r in range(row_count)])  5.99 us
    ppermute x3, waiting for transfers between devices, row_xor(): return lax.ppermute(x, 'row', [(r, r ^ b) for r in range(row_count)])  4.59 us
    pallas_call x2, Pallas kernels, local(): pl.pallas_call(functools.partial(fold_left, sizes, hops), out_shape=jax.S...  1.64 us
    unnamed x5, local copies, waits for them, and re-layouts  1.22 us
    add x1, other arithmetic, local(): total = total + piece.astype(jnp.float32)  0.91 us
  transfers between devices with their start and end apart: 18, of which 7 were waited for; matrix products, arithmetic and copies ran while one was open for 5% of the time, Pallas kernels for 17%

profile of v5, /device:TPU:0, one launch (start us, length us, event | category | flops | bytes accessed | tf_op | source)
XLA Modules:
  0.0 40.9 jit_solution(2822090811294345321)
XLA Ops:
  0.0 0.5 %collective-permute-start.2 = (bf16[4,8,128,128]{3,2,1,0:T(8,128)(2,1)}, bf16[4,8,128,128]{3,2,1,0:T(8,128)(2,1)S(1)}, u32[]{:S(2)}, u32[]{:S(2)}) collective-permute-start(bf16[4,8,128,128]{3,2,1,0:T(8,128)(2,1)} %bitcast.6), channel_id=1, source_target_pairs={{0,1},{1,0},{2,3},{3,2},{4,5},{5,4},{6,7},{7,6},{8,9},{9,8},{10,11... | collective-permute-start | bytes 3145736 | tf_op jit(solution)/shard_map/ppermute | solution.py:93
  0.5 3.6 %collective-permute-start = (bf16[2,3,128,128]{3,2,1,0:T(8,128)(2,1)}, bf16[2,3,128,128]{3,2,1,0:T(8,128)(2,1)S(1)}, u32[]{:S(2)}, u32[]{:S(2)}) collective-permute-start(bf16[2,3,128,128]{3,2,1,0:T(8,128)(2,1)} %refs_0_.9), channel_id=1, source_target_pairs={{0,16},{8,24},{16,0},{24,8},{1,17},{9,25},{17,1},{25,9},{2,18},{10... | collective-permute-start | bytes 589832 | tf_op jit(solution)/shard_map/ppermute | solution.py:96
  4.1 1.5 %collective-permute-start.3 = (bf16[2,3,128,128]{3,2,1,0:T(8,128)(2,1)}, bf16[2,3,128,128]{3,2,1,0:T(8,128)(2,1)S(1)}, u32[]{:S(2)}, u32[]{:S(2)}) collective-permute-start(bf16[2,3,128,128]{3,2,1,0:T(8,128)(2,1)} %refs_0_.9), channel_id=1, source_target_pairs={{0,2},{1,3},{2,0},{3,1},{4,6},{5,7},{6,4},{7,5},{8,10},{9,11},{10,... | collective-permute-start | bytes 589832 | tf_op jit(solution)/shard_map/ppermute | solution.py:93
  5.6 1.6 %collective-permute-start.6 = (bf16[2,3,128,128]{3,2,1,0:T(8,128)(2,1)}, bf16[2,3,128,128]{3,2,1,0:T(8,128)(2,1)S(1)}, u32[]{:S(2)}, u32[]{:S(2)}) collective-permute-start(bf16[2,3,128,128]{3,2,1,0:T(8,128)(2,1)} %refs_0_.9), channel_id=1, source_target_pairs={{0,8},{8,0},{16,24},{24,16},{1,9},{9,1},{17,25},{25,17},{2,10},{10... | collective-permute-start | bytes 589832 | tf_op jit(solution)/shard_map/ppermute | solution.py:96
  7.2 0.0 collective-permute-done.2.other_a
  7.2 1.5 %collective-permute-start.4 = (bf16[2,3,128,128]{3,2,1,0:T(8,128)(2,1)}, bf16[2,3,128,128]{3,2,1,0:T(8,128)(2,1)S(1)}, u32[]{:S(2)}, u32[]{:S(2)}) collective-permute-start(bf16[2,3,128,128]{3,2,1,0:T(8,128)(2,1)} %refs_0_.9), channel_id=1, source_target_pairs={{0,4},{1,5},{2,6},{3,7},{4,0},{5,1},{6,2},{7,3},{8,12},{9,13},{10,... | collective-permute-start | bytes 589832 | tf_op jit(solution)/shard_map/ppermute | solution.py:93
  8.7 0.8 %bitcast_select_fusion = s32[4,8]{1,0:T(4,128)S(1)} fusion(s32[1,1,4,8]{3,2,1,0:T(4,128)} %param.8, s32[1,1,4,8]{3,2,1,0:T(4,128)} %param.7, s32[4]{0:T(128)} %bitcast.11), kind=kLoop, calls=%fused_computation.1 | loop fusion | flops 128 | bytes 400 | tf_op jit(solution)/shard_map/jit(_where)/select_n | solution.py:101
  9.5 0.0 collective-permute-start.1
  9.5 0.1 reshape.19
  9.6 0.8 %copy.8 = s32[64,3]{1,0:T(8,128)S(1)} copy(s32[64,3]{0,1:T(4,128)} %param.11) | data formatting | bytes 1536 | tf_op args[5]
  10.3 0.1 reshape.21
  10.5 0.2 collective-permute-done.1
  10.6 0.1 reshape.20
  10.7 0.1 concatenate.3.info
  10.8 0.5 %collective-permute-start.5 = (bf16[2,3,128,128]{3,2,1,0:T(8,128)(2,1)}, bf16[2,3,128,128]{3,2,1,0:T(8,128)(2,1)S(1)}, u32[]{:S(2)}, u32[]{:S(2)}) collective-permute-start(bf16[2,3,128,128]{3,2,1,0:T(8,128)(2,1)} %refs_0_.9), channel_id=1, source_target_pairs={{0,6},{1,7},{2,4},{3,5},{4,2},{5,3},{6,0},{7,1},{8,14},{9,15},{10,... | collective-permute-start | bytes 589832 | tf_op jit(solution)/shard_map/ppermute | solution.py:93
  11.3 0.0 collective-permute-done.3.refs_0_
  11.3 0.1 collective-permute-start.8
  11.3 2.8 %collective-permute-done.refs_4_ = bf16[2,3,128,128]{3,2,1,0:T(8,128)(2,1)S(1)} collective-permute-done((bf16[2,3,128,128]{3,2,1,0:T(8,128)(2,1)}, bf16[2,3,128,128]{3,2,1,0:T(8,128)(2,1)S(1)}, u32[]{:S(2)}, u32[]{:S(2)}) %collective-permute-start) | collective-permute-done | bytes 196640 | tf_op jit(solution)/shard_map/ppermute | solution.py:96
  14.1 0.8 %collective-permute-start.13 = (bf16[2,3,128,128]{3,2,1,0:T(8,128)(2,1)S(1)}, bf16[2,3,128,128]{3,2,1,0:T(8,128)(2,1)S(1)}, u32[]{:S(2)}, u32[]{:S(2)}) collective-permute-start(bf16[2,3,128,128]{3,2,1,0:T(8,128)(2,1)S(1)} %collective-permute-done.refs_4_), channel_id=1, source_target_pairs={{0,8},{8,0},{16,24},{24,16},{1,9},{9,1},{17,25},{25,17},{2,10},{10... | collective-permute-start | bytes 589832 | tf_op jit(solution)/shard_map/ppermute | solution.py:96
  14.9 0.0 collective-permute-done.4.refs_2_
  14.9 0.0 collective-permute-start.9
  14.9 0.6 %collective-permute-done.6.refs_2_ = bf16[2,3,128,128]{3,2,1,0:T(8,128)(2,1)S(1)} collective-permute-done((bf16[2,3,128,128]{3,2,1,0:T(8,128)(2,1)}, bf16[2,3,128,128]{3,2,1,0:T(8,128)(2,1)S(1)}, u32[]{:S(2)}, u32[]{:S(2)}) %collective-permute-start.6) | collective-permute-done | bytes 196640 | tf_op jit(solution)/shard_map/ppermute | solution.py:96
  15.5 0.0 collective-permute-start.11
  15.5 3.5 %collective-permute-done.5.refs_4_ = bf16[2,3,128,128]{3,2,1,0:T(8,128)(2,1)S(1)} collective-permute-done((bf16[2,3,128,128]{3,2,1,0:T(8,128)(2,1)}, bf16[2,3,128,128]{3,2,1,0:T(8,128)(2,1)S(1)}, u32[]{:S(2)}, u32[]{:S(2)}) %collective-permute-start.5) | collective-permute-done | bytes 196640 | tf_op jit(solution)/shard_map/ppermute | solution.py:93
  19.1 0.0 collective-permute-start.10
  19.1 0.0 collective-permute-done.8.refs_1_
  19.1 0.5 %collective-permute-start.7 = (bf16[2,3,128,128]{3,2,1,0:T(8,128)(2,1)}, bf16[2,3,128,128]{3,2,1,0:T(8,128)(2,1)S(1)}, u32[]{:S(2)}, u32[]{:S(2)}) collective-permute-start(bf16[2,3,128,128]{3,2,1,0:T(8,128)(2,1)} %refs_0_.9), channel_id=1, source_target_pairs={{0,1},{1,0},{2,3},{3,2},{4,5},{5,4},{6,7},{7,6},{8,9},{9,8},{10,11... | collective-permute-start | bytes 589832 | tf_op jit(solution)/shard_map/ppermute | solution.py:93
  19.6 1.2 %collective-permute-done.13.refs_6_ = bf16[2,3,128,128]{3,2,1,0:T(8,128)(2,1)S(1)} collective-permute-done((bf16[2,3,128,128]{3,2,1,0:T(8,128)(2,1)S(1)}, bf16[2,3,128,128]{3,2,1,0:T(8,128)(2,1)S(1)}, u32[]{:S(2)}, u32[]{:S(2)}) %collective-permute-start.13) | collective-permute-done | bytes 196640 | tf_op jit(solution)/shard_map/ppermute | solution.py:96
  20.8 0.0 collective-permute-start.12
  20.8 0.0 collective-permute-done.9.refs_3_
  20.8 0.5 %collective-permute-start.14 = (bf16[2,3,128,128]{3,2,1,0:T(8,128)(2,1)S(1)}, bf16[2,3,128,128]{3,2,1,0:T(8,128)(2,1)S(1)}, u32[]{:S(2)}, u32[]{:S(2)}) collective-permute-start(bf16[2,3,128,128]{3,2,1,0:T(8,128)(2,1)S(1)} %collective-permute-done.13.refs_6_), channel_id=1, source_target_pairs={{0,1},{1,0},{2,3},{3,2},{4,5},{5,4},{6,7},{7,6},{8,9},{9,8},{10,11... | collective-permute-start | bytes 589832 | tf_op jit(solution)/shard_map/ppermute | solution.py:93
  21.3 0.9 %fold_left.2.refs_2_ = bf16[16,4,128,128]{3,2,1,0:T(8,128)(2,1)S(1)} custom-call(s32[258]{0:T(512)S(1)} %concatenate.3.info, bf16[2,3,128,128]{3,2,1,0:T(8,128)(2,1)S(1)} %collective-permute-done.3.refs_0_, bf16[2,3,128,128]{3,2,1,0:T(8,128)(2,1)S(1)} %collective-permute-done.8.refs_1_, bf16[2,3,128,128]{3,2,1,0:T(8,128)(2,1)S(1)} %collective-permute-done.4.refs_2_, ...), custom_call_target="tpu_custom_call" | custom-call | bytes 1048576 | tf_op jit(solution)/shard_map/fold_left/pallas_call | solution.py:139
  22.2 0.0 copy-start
  22.2 0.0 collective-permute-done.7.refs_1_
  22.2 0.7 %fold_left.3.left = bf16[16,4,128,128]{3,2,1,0:T(8,128)(2,1)S(1)} custom-call(s32[258]{0:T(512)S(1)} %concatenate.3.info, bf16[2,3,128,128]{3,2,1,0:T(8,128)(2,1)S(1)} %copy-done.1, bf16[2,3,128,128]{3,2,1,0:T(8,128)(2,1)S(1)} %collective-permute-done.7.refs_1_, bf16[16,4,128,128]{3,2,1,0:T(8,128)(2,1)S(1)} %fold_left.2.refs_2_), custom_call_target="tpu_custom_call", output_to_operand_aliasing={{}: (3, {})} | custom-call | bytes 1048576 | tf_op jit(solution)/shard_map/fold_left/pallas_call | solution.py:139
  23.0 0.0 collective-permute-done.11.refs_3_
  23.0 0.4 %copy-done = bf16[1,1,4,8,128,128]{5,4,3,2,1,0:T(8,128)(2,1)S(1)} copy-done((bf16[1,1,4,8,128,128]{5,4,3,2,1,0:T(8,128)(2,1)S(1)}, bf16[1,1,4,8,128,128]{5,4,3,2,1,0:T(8,128)(2,1)}, u32[]{:S(2)}) %copy-start) | copy-done | bytes 1048600
  23.4 1.8 %section.7 = bf16[2,4,128,128]{3,2,1,0:T(8,128)(2,1)S(1)} custom-call(s32[258]{0:T(512)S(1)} %concatenate.3.info, bf16[4,8,128,128]{3,2,1,0:T(8,128)(2,1)S(1)} %bitcast.7, bf16[4,8,128,128]{3,2,1,0:T(8,128)(2,1)S(1)} %collective-permute-done.2.other_a, bf16[16,4,128,128]{3,2,1,0:T(8,128)(2,1)S(1)} %fold_left.3.left, bf16[2,3,128,128]{3,2,1,0:T(8,128)(2,1)S(1)} %copy-done.1, ...), custom_call_target="tpu_custom_call" | custom-call | flops 536870912 | bytes 4194304 | tf_op jit(solution)/shard_map/section/pallas_call | solution.py:158
  25.2 2.4 %collective-permute-start.17 = (bf16[2,4,128,128]{3,2,1,0:T(8,128)(2,1)S(1)}, bf16[2,4,128,128]{3,2,1,0:T(8,128)(2,1)S(1)}, u32[]{:S(2)}, u32[]{:S(2)}) collective-permute-start(bf16[2,4,128,128]{3,2,1,0:T(8,128)(2,1)S(1)} %section.7), channel_id=1, source_target_pairs={{0,6},{1,7},{2,4},{3,5},{4,2},{5,3},{6,0},{7,1},{8,14},{9,15},{10,... | collective-permute-start | bytes 786440 | tf_op jit(solution)/shard_map/ppermute | solution.py:93
  27.6 1.8 %section.6 = bf16[2,4,128,128]{3,2,1,0:T(8,128)(2,1)S(1)} custom-call(s32[258]{0:T(512)S(1)} %concatenate.3.info, bf16[4,8,128,128]{3,2,1,0:T(8,128)(2,1)S(1)} %bitcast.8, bf16[4,8,128,128]{3,2,1,0:T(8,128)(2,1)S(1)} %collective-permute-done.2.other_a, bf16[16,4,128,128]{3,2,1,0:T(8,128)(2,1)S(1)} %fold_left.3.left, bf16[2,3,128,128]{3,2,1,0:T(8,128)(2,1)S(1)} %copy-done.1, ...), custom_call_target="tpu_custom_call" | custom-call | flops 536870912 | bytes 4194304 | tf_op jit(solution)/shard_map/section/pallas_call | solution.py:158
  29.3 0.6 %collective-permute-start.16 = (bf16[2,4,128,128]{3,2,1,0:T(8,128)(2,1)S(1)}, bf16[2,4,128,128]{3,2,1,0:T(8,128)(2,1)S(1)}, u32[]{:S(2)}, u32[]{:S(2)}) collective-permute-start(bf16[2,4,128,128]{3,2,1,0:T(8,128)(2,1)S(1)} %section.6), channel_id=1, source_target_pairs={{0,4},{1,5},{2,6},{3,7},{4,0},{5,1},{6,2},{7,3},{8,12},{9,13},{10,... | collective-permute-start | bytes 786440 | tf_op jit(solution)/shard_map/ppermute | solution.py:93
  29.9 1.8 %section.5 = bf16[2,4,128,128]{3,2,1,0:T(8,128)(2,1)S(1)} custom-call(s32[258]{0:T(512)S(1)} %concatenate.3.info, bf16[4,8,128,128]{3,2,1,0:T(8,128)(2,1)S(1)} %bitcast.9, bf16[4,8,128,128]{3,2,1,0:T(8,128)(2,1)S(1)} %collective-permute-done.2.other_a, bf16[16,4,128,128]{3,2,1,0:T(8,128)(2,1)S(1)} %fold_left.3.left, bf16[2,3,128,128]{3,2,1,0:T(8,128)(2,1)S(1)} %copy-done.1, ...), custom_call_target="tpu_custom_call" | custom-call | flops 536870912 | bytes 4194304 | tf_op jit(solution)/shard_map/section/pallas_call | solution.py:158
  31.7 0.7 %collective-permute-start.15 = (bf16[2,4,128,128]{3,2,1,0:T(8,128)(2,1)S(1)}, bf16[2,4,128,128]{3,2,1,0:T(8,128)(2,1)S(1)}, u32[]{:S(2)}, u32[]{:S(2)}) collective-permute-start(bf16[2,4,128,128]{3,2,1,0:T(8,128)(2,1)S(1)} %section.5), channel_id=1, source_target_pairs={{0,2},{1,3},{2,0},{3,1},{4,6},{5,7},{6,4},{7,5},{8,10},{9,11},{10,... | collective-permute-start | bytes 786440 | tf_op jit(solution)/shard_map/ppermute | solution.py:93
  32.4 1.8 %section.4 = f32[2,4,128,128]{3,2,1,0:T(8,128)S(1)} custom-call(s32[258]{0:T(512)S(1)} %concatenate.3.info, bf16[4,8,128,128]{3,2,1,0:T(8,128)(2,1)S(1)} %bitcast.10, bf16[4,8,128,128]{3,2,1,0:T(8,128)(2,1)S(1)} %collective-permute-done.2.other_a, bf16[16,4,128,128]{3,2,1,0:T(8,128)(2,1)S(1)} %fold_left.3.left, bf16[2,3,128,128]{3,2,1,0:T(8,128)(2,1)S(1)} %copy-done.1, ...), custom_call_target="tpu_custom_call" | custom-call | flops 536870912 | bytes 4194304 | tf_op jit(solution)/shard_map/section/pallas_call | solution.py:158
  34.2 0.3 collective-permute-done.17
  34.5 5.5 %collective-permute-done.16 = bf16[2,4,128,128]{3,2,1,0:T(8,128)(2,1)S(1)} collective-permute-done((bf16[2,4,128,128]{3,2,1,0:T(8,128)(2,1)S(1)}, bf16[2,4,128,128]{3,2,1,0:T(8,128)(2,1)S(1)}, u32[]{:S(2)}, u32[]{:S(2)}) %collective-permute-start.16) | collective-permute-done | bytes 262176 | tf_op jit(solution)/shard_map/ppermute | solution.py:93
  40.0 0.0 collective-permute-done.15
  40.0 0.9 %convert_add_fusion = f32[2,4,128,128]{3,2,1,0:T(8,128)} fusion(bf16[2,4,128,128]{3,2,1,0:T(8,128)(2,1)S(1)} %collective-permute-done.17, bf16[2,4,128,128]{3,2,1,0:T(8,128)(2,1)S(1)} %collective-permute-done.16, f32[2,4,128,128]{3,2,1,0:T(8,128)S(1)} %section.4, bf16[2,4,128,128]{3,2,1,0:T(8,128)(2,1)S(1)} %collective-permute-done.15), kind=kLoop, calls=%fused_computation | loop fusion | flops 786432 | bytes 1835008 | tf_op jit(solution)/shard_map/add | solution.py:182
  (5 shorter events, 0.0 us)
Async XLA Ops:
  0.0 22.2 %copy-start.1 = (bf16[2,3,128,128]{3,2,1,0:T(8,128)(2,1)S(1)}, bf16[2,3,128,128]{3,2,1,0:T(8,128)(2,1)}, u32[]{:S(2)}) copy-start(bf16[2,3,128,128]{3,2,1,0:T(8,128)(2,1)} %refs_0_.9) | copy-start | bytes 589828
  0.0 7.2 %collective-permute-start.2 = (bf16[4,8,128,128]{3,2,1,0:T(8,128)(2,1)}, bf16[4,8,128,128]{3,2,1,0:T(8,128)(2,1)S(1)}, u32[]{:S(2)}, u32[]{:S(2)}) collective-permute-start(bf16[4,8,128,128]{3,2,1,0:T(8,128)(2,1)} %bitcast.6), channel_id=1, source_target_pairs={{0,1},{1,0},{2,3},{3,2},{4,5},{5,4},{6,7},{7,6},{8,9},{9,8},{10,11... | collective-permute-start | bytes 3145736 | tf_op jit(solution)/shard_map/ppermute | solution.py:93
  0.5 13.7 %collective-permute-start = (bf16[2,3,128,128]{3,2,1,0:T(8,128)(2,1)}, bf16[2,3,128,128]{3,2,1,0:T(8,128)(2,1)S(1)}, u32[]{:S(2)}, u32[]{:S(2)}) collective-permute-start(bf16[2,3,128,128]{3,2,1,0:T(8,128)(2,1)} %refs_0_.9), channel_id=1, source_target_pairs={{0,16},{8,24},{16,0},{24,8},{1,17},{9,25},{17,1},{25,9},{2,18},{10... | collective-permute-start | bytes 589832 | tf_op jit(solution)/shard_map/ppermute | solution.py:96
  4.1 7.2 %collective-permute-start.3 = (bf16[2,3,128,128]{3,2,1,0:T(8,128)(2,1)}, bf16[2,3,128,128]{3,2,1,0:T(8,128)(2,1)S(1)}, u32[]{:S(2)}, u32[]{:S(2)}) collective-permute-start(bf16[2,3,128,128]{3,2,1,0:T(8,128)(2,1)} %refs_0_.9), channel_id=1, source_target_pairs={{0,2},{1,3},{2,0},{3,1},{4,6},{5,7},{6,4},{7,5},{8,10},{9,11},{10,... | collective-permute-start | bytes 589832 | tf_op jit(solution)/shard_map/ppermute | solution.py:93
  5.6 9.9 %collective-permute-start.6 = (bf16[2,3,128,128]{3,2,1,0:T(8,128)(2,1)}, bf16[2,3,128,128]{3,2,1,0:T(8,128)(2,1)S(1)}, u32[]{:S(2)}, u32[]{:S(2)}) collective-permute-start(bf16[2,3,128,128]{3,2,1,0:T(8,128)(2,1)} %refs_0_.9), channel_id=1, source_target_pairs={{0,8},{8,0},{16,24},{24,16},{1,9},{9,1},{17,25},{25,17},{2,10},{10... | collective-permute-start | bytes 589832 | tf_op jit(solution)/shard_map/ppermute | solution.py:96
  7.2 7.7 %collective-permute-start.4 = (bf16[2,3,128,128]{3,2,1,0:T(8,128)(2,1)}, bf16[2,3,128,128]{3,2,1,0:T(8,128)(2,1)S(1)}, u32[]{:S(2)}, u32[]{:S(2)}) collective-permute-start(bf16[2,3,128,128]{3,2,1,0:T(8,128)(2,1)} %refs_0_.9), channel_id=1, source_target_pairs={{0,4},{1,5},{2,6},{3,7},{4,0},{5,1},{6,2},{7,3},{8,12},{9,13},{10,... | collective-permute-start | bytes 589832 | tf_op jit(solution)/shard_map/ppermute | solution.py:93
  9.5 1.2 %collective-permute-start.1 = (s32[4,8]{1,0:T(4,128)S(1)}, s32[4,8]{1,0:T(4,128)S(1)}, u32[]{:S(2)}, u32[]{:S(2)}) collective-permute-start(s32[4,8]{1,0:T(4,128)S(1)} %bitcast_select_fusion), channel_id=1, source_target_pairs={{0,1},{1,0},{2,3},{3,2},{4,5},{5,4},{6,7},{7,6},{8,9},{9,8},{10,11... | collective-permute-start | bytes 392 | tf_op jit(solution)/shard_map/ppermute | solution.py:93
  10.8 8.3 %collective-permute-start.5 = (bf16[2,3,128,128]{3,2,1,0:T(8,128)(2,1)}, bf16[2,3,128,128]{3,2,1,0:T(8,128)(2,1)S(1)}, u32[]{:S(2)}, u32[]{:S(2)}) collective-permute-start(bf16[2,3,128,128]{3,2,1,0:T(8,128)(2,1)} %refs_0_.9), channel_id=1, source_target_pairs={{0,6},{1,7},{2,4},{3,5},{4,2},{5,3},{6,0},{7,1},{8,14},{9,15},{10,... | collective-permute-start | bytes 589832 | tf_op jit(solution)/shard_map/ppermute | solution.py:93
  11.3 7.8 %collective-permute-start.8 = (bf16[2,3,128,128]{3,2,1,0:T(8,128)(2,1)S(1)}, bf16[2,3,128,128]{3,2,1,0:T(8,128)(2,1)S(1)}, u32[]{:S(2)}, u32[]{:S(2)}) collective-permute-start(bf16[2,3,128,128]{3,2,1,0:T(8,128)(2,1)S(1)} %collective-permute-done.3.refs_0_), channel_id=1, source_target_pairs={{0,1},{1,0},{2,3},{3,2},{4,5},{5,4},{6,7},{7,6},{8,9},{9,8},{10,11... | collective-permute-start | bytes 589832 | tf_op jit(solution)/shard_map/ppermute | solution.py:93
  14.1 6.6 %collective-permute-start.13 = (bf16[2,3,128,128]{3,2,1,0:T(8,128)(2,1)S(1)}, bf16[2,3,128,128]{3,2,1,0:T(8,128)(2,1)S(1)}, u32[]{:S(2)}, u32[]{:S(2)}) collective-permute-start(bf16[2,3,128,128]{3,2,1,0:T(8,128)(2,1)S(1)} %collective-permute-done.refs_4_), channel_id=1, source_target_pairs={{0,8},{8,0},{16,24},{24,16},{1,9},{9,1},{17,25},{25,17},{2,10},{10... | collective-permute-start | bytes 589832 | tf_op jit(solution)/shard_map/ppermute | solution.py:96
  14.9 5.8 %collective-permute-start.9 = (bf16[2,3,128,128]{3,2,1,0:T(8,128)(2,1)S(1)}, bf16[2,3,128,128]{3,2,1,0:T(8,128)(2,1)S(1)}, u32[]{:S(2)}, u32[]{:S(2)}) collective-permute-start(bf16[2,3,128,128]{3,2,1,0:T(8,128)(2,1)S(1)} %collective-permute-done.4.refs_2_), channel_id=1, source_target_pairs={{0,1},{1,0},{2,3},{3,2},{4,5},{5,4},{6,7},{7,6},{8,9},{9,8},{10,11... | collective-permute-start | bytes 589832 | tf_op jit(solution)/shard_map/ppermute | solution.py:93
  15.5 7.4 %collective-permute-start.11 = (bf16[2,3,128,128]{3,2,1,0:T(8,128)(2,1)S(1)}, bf16[2,3,128,128]{3,2,1,0:T(8,128)(2,1)S(1)}, u32[]{:S(2)}, u32[]{:S(2)}) collective-permute-start(bf16[2,3,128,128]{3,2,1,0:T(8,128)(2,1)S(1)} %collective-permute-done.6.refs_2_), channel_id=1, source_target_pairs={{0,1},{1,0},{2,3},{3,2},{4,5},{5,4},{6,7},{7,6},{8,9},{9,8},{10,11... | collective-permute-start | bytes 589832 | tf_op jit(solution)/shard_map/ppermute | solution.py:93
  19.1 2.2 %collective-permute-start.10 = (bf16[2,3,128,128]{3,2,1,0:T(8,128)(2,1)S(1)}, bf16[2,3,128,128]{3,2,1,0:T(8,128)(2,1)S(1)}, u32[]{:S(2)}, u32[]{:S(2)}) collective-permute-start(bf16[2,3,128,128]{3,2,1,0:T(8,128)(2,1)S(1)} %collective-permute-done.5.refs_4_), channel_id=1, source_target_pairs={{0,1},{1,0},{2,3},{3,2},{4,5},{5,4},{6,7},{7,6},{8,9},{9,8},{10,11... | collective-permute-start | bytes 589832 | tf_op jit(solution)/shard_map/ppermute | solution.py:93
  19.1 3.1 %collective-permute-start.7 = (bf16[2,3,128,128]{3,2,1,0:T(8,128)(2,1)}, bf16[2,3,128,128]{3,2,1,0:T(8,128)(2,1)S(1)}, u32[]{:S(2)}, u32[]{:S(2)}) collective-permute-start(bf16[2,3,128,128]{3,2,1,0:T(8,128)(2,1)} %refs_0_.9), channel_id=1, source_target_pairs={{0,1},{1,0},{2,3},{3,2},{4,5},{5,4},{6,7},{7,6},{8,9},{9,8},{10,11... | collective-permute-start | bytes 589832 | tf_op jit(solution)/shard_map/ppermute | solution.py:93
  20.8 2.2 %collective-permute-start.12 = (bf16[2,3,128,128]{3,2,1,0:T(8,128)(2,1)S(1)}, bf16[2,3,128,128]{3,2,1,0:T(8,128)(2,1)S(1)}, u32[]{:S(2)}, u32[]{:S(2)}) collective-permute-start(bf16[2,3,128,128]{3,2,1,0:T(8,128)(2,1)S(1)} %collective-permute-done.refs_4_), channel_id=1, source_target_pairs={{0,1},{1,0},{2,3},{3,2},{4,5},{5,4},{6,7},{7,6},{8,9},{9,8},{10,11... | collective-permute-start | bytes 589832 | tf_op jit(solution)/shard_map/ppermute | solution.py:93
  20.8 2.2 %collective-permute-start.14 = (bf16[2,3,128,128]{3,2,1,0:T(8,128)(2,1)S(1)}, bf16[2,3,128,128]{3,2,1,0:T(8,128)(2,1)S(1)}, u32[]{:S(2)}, u32[]{:S(2)}) collective-permute-start(bf16[2,3,128,128]{3,2,1,0:T(8,128)(2,1)S(1)} %collective-permute-done.13.refs_6_), channel_id=1, source_target_pairs={{0,1},{1,0},{2,3},{3,2},{4,5},{5,4},{6,7},{7,6},{8,9},{9,8},{10,11... | collective-permute-start | bytes 589832 | tf_op jit(solution)/shard_map/ppermute | solution.py:93
  22.2 1.2 %copy-start = (bf16[1,1,4,8,128,128]{5,4,3,2,1,0:T(8,128)(2,1)S(1)}, bf16[1,1,4,8,128,128]{5,4,3,2,1,0:T(8,128)(2,1)}, u32[]{:S(2)}) copy-start(bf16[1,1,4,8,128,128]{5,4,3,2,1,0:T(8,128)(2,1)} %param.6) | copy-start | bytes 3145732
  25.2 9.3 %collective-permute-start.17 = (bf16[2,4,128,128]{3,2,1,0:T(8,128)(2,1)S(1)}, bf16[2,4,128,128]{3,2,1,0:T(8,128)(2,1)S(1)}, u32[]{:S(2)}, u32[]{:S(2)}) collective-permute-start(bf16[2,4,128,128]{3,2,1,0:T(8,128)(2,1)S(1)} %section.7), channel_id=1, source_target_pairs={{0,6},{1,7},{2,4},{3,5},{4,2},{5,3},{6,0},{7,1},{8,14},{9,15},{10,... | collective-permute-start | bytes 786440 | tf_op jit(solution)/shard_map/ppermute | solution.py:93
  29.3 10.7 %collective-permute-start.16 = (bf16[2,4,128,128]{3,2,1,0:T(8,128)(2,1)S(1)}, bf16[2,4,128,128]{3,2,1,0:T(8,128)(2,1)S(1)}, u32[]{:S(2)}, u32[]{:S(2)}) collective-permute-start(bf16[2,4,128,128]{3,2,1,0:T(8,128)(2,1)S(1)} %section.6), channel_id=1, source_target_pairs={{0,4},{1,5},{2,6},{3,7},{4,0},{5,1},{6,2},{7,3},{8,12},{9,13},{10,... | collective-permute-start | bytes 786440 | tf_op jit(solution)/shard_map/ppermute | solution.py:93
  31.7 8.3 %collective-permute-start.15 = (bf16[2,4,128,128]{3,2,1,0:T(8,128)(2,1)S(1)}, bf16[2,4,128,128]{3,2,1,0:T(8,128)(2,1)S(1)}, u32[]{:S(2)}, u32[]{:S(2)}) collective-permute-start(bf16[2,4,128,128]{3,2,1,0:T(8,128)(2,1)S(1)} %section.5), channel_id=1, source_target_pairs={{0,2},{1,3},{2,0},{3,1},{4,6},{5,7},{6,4},{7,5},{8,10},{9,11},{10,... | collective-permute-start | bytes 786440 | tf_op jit(solution)/shard_map/ppermute | solution.py:93

commit v6 on v5

--- a/solution.py
+++ b/solution.py
@@ -114,7 +114,7 @@
         ]
     )
     near_p, other_a = lax.optimization_barrier((p_vals, col_xor(own_a, 1)))
-    left = [p_vals] + [col_xor(near_p if e > 1 else p_vals, 2 * e) for e in range(1, row_count)]
+    left = [p_vals] + [col_xor(near_p if e < row_count - 1 else p_vals, 2 * e) for e in range(1, row_count)]
     right = [p_vals] + [None] * (row_count - 1)
     for d in sorted(range(1, row_count), key=lambda d: (d.bit_count(), -d)):
         piece = right[d & (d - 1)]

time: 41.1 us -> 41.1 us (level)
    ppermute x3, waiting for transfers between devices: 4.59 us -> 3.32 us  [row_xor(): return lax.ppermute(x, 'row', [(r, r ^ b) for r in range(row_count)])]
    ppermute x15, waiting for transfers between devices: 9.53 us -> 10.4 us  [col_xor(): return lax.ppermute(x, 'col', [(c, c ^ b) for c in range(col_count)])]
    ppermute x15, starting transfers between devices: 8.72 us -> 9.14 us  [col_xor(): return lax.ppermute(x, 'col', [(c, c ^ b) for c in range(col_count)])]
  transfers between devices with their start and end apart: 18 -> 18, of which waited for: 7 -> 8; matrix products, arithmetic and copies ran while one was open for 5% -> 5% of each run, Pallas kernels for 17% -> 17%
where the time goes in v6:
time: 41.1 us; the launch traced here: 40.9 us
  starting transfers between devices  15.1 us (37%)
  waiting for transfers between devices  13.7 us (33%)
  Pallas kernels  8.68 us (21%)
  other arithmetic  1.68 us (4%)
  local copies, waits for them, and re-layouts  1.59 us (4%)
    ppermute x15, waiting for transfers between devices, col_xor(): return lax.ppermute(x, 'col', [(c, c ^ b) for c in range(col_count)])  10.4 us
    ppermute x15, starting transfers between devices, col_xor(): return lax.ppermute(x, 'col', [(c, c ^ b) for c in range(col_count)])  9.14 us
    pallas_call x4, Pallas kernels, partial_of(): pl.pallas_call(functools.partial(section, sizes, hop), out_shape=jax.Shap...  7.04 us
    ppermute x3, starting transfers between devices, row_xor(): return lax.ppermute(x, 'row', [(r, r ^ b) for r in range(row_count)])  5.99 us
    ppermute x3, waiting for transfers between devices, row_xor(): return lax.ppermute(x, 'row', [(r, r ^ b) for r in range(row_count)])  3.32 us
    pallas_call x2, Pallas kernels, local(): pl.pallas_call(functools.partial(fold_left, sizes, hops), out_shape=jax.S...  1.64 us
    unnamed x5, local copies, waits for them, and re-layouts  1.22 us
    add x1, other arithmetic, local(): total = total + piece.astype(jnp.float32)  0.91 us
  transfers between devices with their start and end apart: 18, of which 8 were waited for; matrix products, arithmetic and copies ran while one was open for 5% of the time, Pallas kernels for 17%

profile of v6, /device:TPU:0, one launch (start us, length us, event | category | flops | bytes accessed | tf_op | source)
XLA Modules:
  0.0 40.9 jit_solution(12927592895712344821)
XLA Ops:
  0.0 0.5 %collective-permute-start.2 = (bf16[4,8,128,128]{3,2,1,0:T(8,128)(2,1)}, bf16[4,8,128,128]{3,2,1,0:T(8,128)(2,1)S(1)}, u32[]{:S(2)}, u32[]{:S(2)}) collective-permute-start(bf16[4,8,128,128]{3,2,1,0:T(8,128)(2,1)} %bitcast.6), channel_id=1, source_target_pairs={{0,1},{1,0},{2,3},{3,2},{4,5},{5,4},{6,7},{7,6},{8,9},{9,8},{10,11... | collective-permute-start | bytes 3145736 | tf_op jit(solution)/shard_map/ppermute | solution.py:93
  0.5 3.6 %collective-permute-start = (bf16[2,3,128,128]{3,2,1,0:T(8,128)(2,1)}, bf16[2,3,128,128]{3,2,1,0:T(8,128)(2,1)S(1)}, u32[]{:S(2)}, u32[]{:S(2)}) collective-permute-start(bf16[2,3,128,128]{3,2,1,0:T(8,128)(2,1)} %refs_0_.9), channel_id=1, source_target_pairs={{0,16},{8,24},{16,0},{24,8},{1,17},{9,25},{17,1},{25,9},{2,18},{10... | collective-permute-start | bytes 589832 | tf_op jit(solution)/shard_map/ppermute | solution.py:96
  4.1 2.4 %collective-permute-start.5 = (bf16[2,3,128,128]{3,2,1,0:T(8,128)(2,1)}, bf16[2,3,128,128]{3,2,1,0:T(8,128)(2,1)S(1)}, u32[]{:S(2)}, u32[]{:S(2)}) collective-permute-start(bf16[2,3,128,128]{3,2,1,0:T(8,128)(2,1)} %refs_0_.9), channel_id=1, source_target_pairs={{0,6},{1,7},{2,4},{3,5},{4,2},{5,3},{6,0},{7,1},{8,14},{9,15},{10,... | collective-permute-start | bytes 589832 | tf_op jit(solution)/shard_map/ppermute | solution.py:93
  6.6 1.6 %collective-permute-start.6 = (bf16[2,3,128,128]{3,2,1,0:T(8,128)(2,1)}, bf16[2,3,128,128]{3,2,1,0:T(8,128)(2,1)S(1)}, u32[]{:S(2)}, u32[]{:S(2)}) collective-permute-start(bf16[2,3,128,128]{3,2,1,0:T(8,128)(2,1)} %refs_0_.9), channel_id=1, source_target_pairs={{0,8},{8,0},{16,24},{24,16},{1,9},{9,1},{17,25},{25,17},{2,10},{10... | collective-permute-start | bytes 589832 | tf_op jit(solution)/shard_map/ppermute | solution.py:96
  8.1 0.0 collective-permute-done.2.other_a
  8.1 0.5 %collective-permute-start.3 = (bf16[2,3,128,128]{3,2,1,0:T(8,128)(2,1)}, bf16[2,3,128,128]{3,2,1,0:T(8,128)(2,1)S(1)}, u32[]{:S(2)}, u32[]{:S(2)}) collective-permute-start(bf16[2,3,128,128]{3,2,1,0:T(8,128)(2,1)} %refs_0_.9), channel_id=1, source_target_pairs={{0,2},{1,3},{2,0},{3,1},{4,6},{5,7},{6,4},{7,5},{8,10},{9,11},{10,... | collective-permute-start | bytes 589832 | tf_op jit(solution)/shard_map/ppermute | solution.py:93
  8.7 0.8 %bitcast_select_fusion = s32[4,8]{1,0:T(4,128)S(1)} fusion(s32[1,1,4,8]{3,2,1,0:T(4,128)} %param.8, s32[1,1,4,8]{3,2,1,0:T(4,128)} %param.7, s32[4]{0:T(128)} %bitcast.11), kind=kLoop, calls=%fused_computation.1 | loop fusion | flops 128 | bytes 400 | tf_op jit(solution)/shard_map/jit(_where)/select_n | solution.py:101
  9.4 0.0 collective-permute-start.1
  9.4 0.1 reshape.19
  9.5 0.8 %copy.8 = s32[64,3]{1,0:T(8,128)S(1)} copy(s32[64,3]{0,1:T(4,128)} %param.11) | data formatting | bytes 1536 | tf_op args[5]
  10.3 0.1 reshape.21
  10.4 0.2 collective-permute-done.1
  10.6 0.1 reshape.20
  10.7 0.1 concatenate.3.info
  10.8 0.5 %collective-permute-start.4 = (bf16[2,3,128,128]{3,2,1,0:T(8,128)(2,1)}, bf16[2,3,128,128]{3,2,1,0:T(8,128)(2,1)S(1)}, u32[]{:S(2)}, u32[]{:S(2)}) collective-permute-start(bf16[2,3,128,128]{3,2,1,0:T(8,128)(2,1)} %refs_0_.9), channel_id=1, source_target_pairs={{0,4},{1,5},{2,6},{3,7},{4,0},{5,1},{6,2},{7,3},{8,12},{9,13},{10,... | collective-permute-start | bytes 589832 | tf_op jit(solution)/shard_map/ppermute | solution.py:93
  11.3 1.7 %collective-permute-done.5.refs_4_ = bf16[2,3,128,128]{3,2,1,0:T(8,128)(2,1)S(1)} collective-permute-done((bf16[2,3,128,128]{3,2,1,0:T(8,128)(2,1)}, bf16[2,3,128,128]{3,2,1,0:T(8,128)(2,1)S(1)}, u32[]{:S(2)}, u32[]{:S(2)}) %collective-permute-start.5) | collective-permute-done | bytes 196640 | tf_op jit(solution)/shard_map/ppermute | solution.py:93
  13.0 0.0 collective-permute-start.10
  13.0 1.2 %collective-permute-done.refs_4_ = bf16[2,3,128,128]{3,2,1,0:T(8,128)(2,1)S(1)} collective-permute-done((bf16[2,3,128,128]{3,2,1,0:T(8,128)(2,1)}, bf16[2,3,128,128]{3,2,1,0:T(8,128)(2,1)S(1)}, u32[]{:S(2)}, u32[]{:S(2)}) %collective-permute-start) | collective-permute-done | bytes 196640 | tf_op jit(solution)/shard_map/ppermute | solution.py:96
  14.1 0.8 %collective-permute-start.13 = (bf16[2,3,128,128]{3,2,1,0:T(8,128)(2,1)S(1)}, bf16[2,3,128,128]{3,2,1,0:T(8,128)(2,1)S(1)}, u32[]{:S(2)}, u32[]{:S(2)}) collective-permute-start(bf16[2,3,128,128]{3,2,1,0:T(8,128)(2,1)S(1)} %collective-permute-done.refs_4_), channel_id=1, source_target_pairs={{0,8},{8,0},{16,24},{24,16},{1,9},{9,1},{17,25},{25,17},{2,10},{10... | collective-permute-start | bytes 589832 | tf_op jit(solution)/shard_map/ppermute | solution.py:96
  14.9 1.5 %collective-permute-done.3.refs_0_ = bf16[2,3,128,128]{3,2,1,0:T(8,128)(2,1)S(1)} collective-permute-done((bf16[2,3,128,128]{3,2,1,0:T(8,128)(2,1)}, bf16[2,3,128,128]{3,2,1,0:T(8,128)(2,1)S(1)}, u32[]{:S(2)}, u32[]{:S(2)}) %collective-permute-start.3) | collective-permute-done | bytes 196640 | tf_op jit(solution)/shard_map/ppermute | solution.py:93
  16.5 0.0 collective-permute-start.8
  16.5 0.0 collective-permute-done.6.refs_2_
  16.5 0.5 %collective-permute-start.11 = (bf16[2,3,128,128]{3,2,1,0:T(8,128)(2,1)S(1)}, bf16[2,3,128,128]{3,2,1,0:T(8,128)(2,1)S(1)}, u32[]{:S(2)}, u32[]{:S(2)}) collective-permute-start(bf16[2,3,128,128]{3,2,1,0:T(8,128)(2,1)S(1)} %collective-permute-done.6.refs_2_), channel_id=1, source_target_pairs={{0,1},{1,0},{2,3},{3,2},{4,5},{5,4},{6,7},{7,6},{8,9},{9,8},{10,11... | collective-permute-start | bytes 589832 | tf_op jit(solution)/shard_map/ppermute | solution.py:93
  17.0 1.2 %collective-permute-done.4.refs_2_ = bf16[2,3,128,128]{3,2,1,0:T(8,128)(2,1)S(1)} collective-permute-done((bf16[2,3,128,128]{3,2,1,0:T(8,128)(2,1)}, bf16[2,3,128,128]{3,2,1,0:T(8,128)(2,1)S(1)}, u32[]{:S(2)}, u32[]{:S(2)}) %collective-permute-start.4) | collective-permute-done | bytes 196640 | tf_op jit(solution)/shard_map/ppermute | solution.py:93
  18.1 0.0 collective-permute-start.9
  18.1 0.0 collective-permute-done.10.refs_5_
  18.1 0.5 %collective-permute-start.7 = (bf16[2,3,128,128]{3,2,1,0:T(8,128)(2,1)}, bf16[2,3,128,128]{3,2,1,0:T(8,128)(2,1)S(1)}, u32[]{:S(2)}, u32[]{:S(2)}) collective-permute-start(bf16[2,3,128,128]{3,2,1,0:T(8,128)(2,1)} %refs_0_.9), channel_id=1, source_target_pairs={{0,1},{1,0},{2,3},{3,2},{4,5},{5,4},{6,7},{7,6},{8,9},{9,8},{10,11... | collective-permute-start | bytes 589832 | tf_op jit(solution)/shard_map/ppermute | solution.py:93
  18.7 2.1 %collective-permute-done.13.refs_6_ = bf16[2,3,128,128]{3,2,1,0:T(8,128)(2,1)S(1)} collective-permute-done((bf16[2,3,128,128]{3,2,1,0:T(8,128)(2,1)S(1)}, bf16[2,3,128,128]{3,2,1,0:T(8,128)(2,1)S(1)}, u32[]{:S(2)}, u32[]{:S(2)}) %collective-permute-start.13) | collective-permute-done | bytes 196640 | tf_op jit(solution)/shard_map/ppermute | solution.py:96
  20.8 0.0 collective-permute-start.12
  20.8 0.0 collective-permute-done.8.refs_1_
  20.8 0.5 %collective-permute-start.14 = (bf16[2,3,128,128]{3,2,1,0:T(8,128)(2,1)S(1)}, bf16[2,3,128,128]{3,2,1,0:T(8,128)(2,1)S(1)}, u32[]{:S(2)}, u32[]{:S(2)}) collective-permute-start(bf16[2,3,128,128]{3,2,1,0:T(8,128)(2,1)S(1)} %collective-permute-done.13.refs_6_), channel_id=1, source_target_pairs={{0,1},{1,0},{2,3},{3,2},{4,5},{5,4},{6,7},{7,6},{8,9},{9,8},{10,11... | collective-permute-start | bytes 589832 | tf_op jit(solution)/shard_map/ppermute | solution.py:93
  21.3 0.9 %fold_left.2.refs_2_ = bf16[16,4,128,128]{3,2,1,0:T(8,128)(2,1)S(1)} custom-call(s32[258]{0:T(512)S(1)} %concatenate.3.info, bf16[2,3,128,128]{3,2,1,0:T(8,128)(2,1)S(1)} %collective-permute-done.3.refs_0_, bf16[2,3,128,128]{3,2,1,0:T(8,128)(2,1)S(1)} %collective-permute-done.8.refs_1_, bf16[2,3,128,128]{3,2,1,0:T(8,128)(2,1)S(1)} %collective-permute-done.4.refs_2_, ...), custom_call_target="tpu_custom_call" | custom-call | bytes 1048576 | tf_op jit(solution)/shard_map/fold_left/pallas_call | solution.py:139
  22.2 0.0 copy-start
  22.2 0.7 %fold_left.3.left = bf16[16,4,128,128]{3,2,1,0:T(8,128)(2,1)S(1)} custom-call(s32[258]{0:T(512)S(1)} %concatenate.3.info, bf16[2,3,128,128]{3,2,1,0:T(8,128)(2,1)S(1)} %copy-done.1, bf16[2,3,128,128]{3,2,1,0:T(8,128)(2,1)S(1)} %collective-permute-done.7.refs_1_, bf16[16,4,128,128]{3,2,1,0:T(8,128)(2,1)S(1)} %fold_left.2.refs_2_), custom_call_target="tpu_custom_call", output_to_operand_aliasing={{}: (3, {})} | custom-call | bytes 1048576 | tf_op jit(solution)/shard_map/fold_left/pallas_call | solution.py:139
  23.0 0.0 collective-permute-done.11.refs_3_
  23.0 0.0 collective-permute-done.12.refs_5_
  23.0 0.4 %copy-done = bf16[1,1,4,8,128,128]{5,4,3,2,1,0:T(8,128)(2,1)S(1)} copy-done((bf16[1,1,4,8,128,128]{5,4,3,2,1,0:T(8,128)(2,1)S(1)}, bf16[1,1,4,8,128,128]{5,4,3,2,1,0:T(8,128)(2,1)}, u32[]{:S(2)}) %copy-start) | copy-done | bytes 1048600
  23.4 1.8 %section.7 = bf16[2,4,128,128]{3,2,1,0:T(8,128)(2,1)S(1)} custom-call(s32[258]{0:T(512)S(1)} %concatenate.3.info, bf16[4,8,128,128]{3,2,1,0:T(8,128)(2,1)S(1)} %bitcast.7, bf16[4,8,128,128]{3,2,1,0:T(8,128)(2,1)S(1)} %collective-permute-done.2.other_a, bf16[16,4,128,128]{3,2,1,0:T(8,128)(2,1)S(1)} %fold_left.3.left, bf16[2,3,128,128]{3,2,1,0:T(8,128)(2,1)S(1)} %copy-done.1, ...), custom_call_target="tpu_custom_call" | custom-call | flops 536870912 | bytes 4194304 | tf_op jit(solution)/shard_map/section/pallas_call | solution.py:158
  25.2 2.4 %collective-permute-start.17 = (bf16[2,4,128,128]{3,2,1,0:T(8,128)(2,1)S(1)}, bf16[2,4,128,128]{3,2,1,0:T(8,128)(2,1)S(1)}, u32[]{:S(2)}, u32[]{:S(2)}) collective-permute-start(bf16[2,4,128,128]{3,2,1,0:T(8,128)(2,1)S(1)} %section.7), channel_id=1, source_target_pairs={{0,6},{1,7},{2,4},{3,5},{4,2},{5,3},{6,0},{7,1},{8,14},{9,15},{10,... | collective-permute-start | bytes 786440 | tf_op jit(solution)/shard_map/ppermute | solution.py:93
  27.6 1.8 %section.6 = bf16[2,4,128,128]{3,2,1,0:T(8,128)(2,1)S(1)} custom-call(s32[258]{0:T(512)S(1)} %concatenate.3.info, bf16[4,8,128,128]{3,2,1,0:T(8,128)(2,1)S(1)} %bitcast.8, bf16[4,8,128,128]{3,2,1,0:T(8,128)(2,1)S(1)} %collective-permute-done.2.other_a, bf16[16,4,128,128]{3,2,1,0:T(8,128)(2,1)S(1)} %fold_left.3.left, bf16[2,3,128,128]{3,2,1,0:T(8,128)(2,1)S(1)} %copy-done.1, ...), custom_call_target="tpu_custom_call" | custom-call | flops 536870912 | bytes 4194304 | tf_op jit(solution)/shard_map/section/pallas_call | solution.py:158
  29.3 0.6 %collective-permute-start.16 = (bf16[2,4,128,128]{3,2,1,0:T(8,128)(2,1)S(1)}, bf16[2,4,128,128]{3,2,1,0:T(8,128)(2,1)S(1)}, u32[]{:S(2)}, u32[]{:S(2)}) collective-permute-start(bf16[2,4,128,128]{3,2,1,0:T(8,128)(2,1)S(1)} %section.6), channel_id=1, source_target_pairs={{0,4},{1,5},{2,6},{3,7},{4,0},{5,1},{6,2},{7,3},{8,12},{9,13},{10,... | collective-permute-start | bytes 786440 | tf_op jit(solution)/shard_map/ppermute | solution.py:93
  29.9 1.8 %section.5 = bf16[2,4,128,128]{3,2,1,0:T(8,128)(2,1)S(1)} custom-call(s32[258]{0:T(512)S(1)} %concatenate.3.info, bf16[4,8,128,128]{3,2,1,0:T(8,128)(2,1)S(1)} %bitcast.9, bf16[4,8,128,128]{3,2,1,0:T(8,128)(2,1)S(1)} %collective-permute-done.2.other_a, bf16[16,4,128,128]{3,2,1,0:T(8,128)(2,1)S(1)} %fold_left.3.left, bf16[2,3,128,128]{3,2,1,0:T(8,128)(2,1)S(1)} %copy-done.1, ...), custom_call_target="tpu_custom_call" | custom-call | flops 536870912 | bytes 4194304 | tf_op jit(solution)/shard_map/section/pallas_call | solution.py:158
  31.7 0.7 %collective-permute-start.15 = (bf16[2,4,128,128]{3,2,1,0:T(8,128)(2,1)S(1)}, bf16[2,4,128,128]{3,2,1,0:T(8,128)(2,1)S(1)}, u32[]{:S(2)}, u32[]{:S(2)}) collective-permute-start(bf16[2,4,128,128]{3,2,1,0:T(8,128)(2,1)S(1)} %section.5), channel_id=1, source_target_pairs={{0,2},{1,3},{2,0},{3,1},{4,6},{5,7},{6,4},{7,5},{8,10},{9,11},{10,... | collective-permute-start | bytes 786440 | tf_op jit(solution)/shard_map/ppermute | solution.py:93
  32.4 1.8 %section.4 = f32[2,4,128,128]{3,2,1,0:T(8,128)S(1)} custom-call(s32[258]{0:T(512)S(1)} %concatenate.3.info, bf16[4,8,128,128]{3,2,1,0:T(8,128)(2,1)S(1)} %bitcast.10, bf16[4,8,128,128]{3,2,1,0:T(8,128)(2,1)S(1)} %collective-permute-done.2.other_a, bf16[16,4,128,128]{3,2,1,0:T(8,128)(2,1)S(1)} %fold_left.3.left, bf16[2,3,128,128]{3,2,1,0:T(8,128)(2,1)S(1)} %copy-done.1, ...), custom_call_target="tpu_custom_call" | custom-call | flops 536870912 | bytes 4194304 | tf_op jit(solution)/shard_map/section/pallas_call | solution.py:158
  34.2 0.3 collective-permute-done.17
  34.5 5.5 %collective-permute-done.16 = bf16[2,4,128,128]{3,2,1,0:T(8,128)(2,1)S(1)} collective-permute-done((bf16[2,4,128,128]{3,2,1,0:T(8,128)(2,1)S(1)}, bf16[2,4,128,128]{3,2,1,0:T(8,128)(2,1)S(1)}, u32[]{:S(2)}, u32[]{:S(2)}) %collective-permute-start.16) | collective-permute-done | bytes 262176 | tf_op jit(solution)/shard_map/ppermute | solution.py:93
  40.0 0.0 collective-permute-done.15
  40.0 0.9 %convert_add_fusion = f32[2,4,128,128]{3,2,1,0:T(8,128)} fusion(bf16[2,4,128,128]{3,2,1,0:T(8,128)(2,1)S(1)} %collective-permute-done.17, bf16[2,4,128,128]{3,2,1,0:T(8,128)(2,1)S(1)} %collective-permute-done.16, f32[2,4,128,128]{3,2,1,0:T(8,128)S(1)} %section.4, bf16[2,4,128,128]{3,2,1,0:T(8,128)(2,1)S(1)} %collective-permute-done.15), kind=kLoop, calls=%fused_computation | loop fusion | flops 786432 | bytes 1835008 | tf_op jit(solution)/shard_map/add | solution.py:182
  (5 shorter events, 0.0 us)
Async XLA Ops:
  0.0 22.2 %copy-start.1 = (bf16[2,3,128,128]{3,2,1,0:T(8,128)(2,1)S(1)}, bf16[2,3,128,128]{3,2,1,0:T(8,128)(2,1)}, u32[]{:S(2)}) copy-start(bf16[2,3,128,128]{3,2,1,0:T(8,128)(2,1)} %refs_0_.9) | copy-start | bytes 589828
  0.0 8.1 %collective-permute-start.2 = (bf16[4,8,128,128]{3,2,1,0:T(8,128)(2,1)}, bf16[4,8,128,128]{3,2,1,0:T(8,128)(2,1)S(1)}, u32[]{:S(2)}, u32[]{:S(2)}) collective-permute-start(bf16[4,8,128,128]{3,2,1,0:T(8,128)(2,1)} %bitcast.6), channel_id=1, source_target_pairs={{0,1},{1,0},{2,3},{3,2},{4,5},{5,4},{6,7},{7,6},{8,9},{9,8},{10,11... | collective-permute-start | bytes 3145736 | tf_op jit(solution)/shard_map/ppermute | solution.py:93
  0.5 13.7 %collective-permute-start = (bf16[2,3,128,128]{3,2,1,0:T(8,128)(2,1)}, bf16[2,3,128,128]{3,2,1,0:T(8,128)(2,1)S(1)}, u32[]{:S(2)}, u32[]{:S(2)}) collective-permute-start(bf16[2,3,128,128]{3,2,1,0:T(8,128)(2,1)} %refs_0_.9), channel_id=1, source_target_pairs={{0,16},{8,24},{16,0},{24,8},{1,17},{9,25},{17,1},{25,9},{2,18},{10... | collective-permute-start | bytes 589832 | tf_op jit(solution)/shard_map/ppermute | solution.py:96
  4.1 8.9 %collective-permute-start.5 = (bf16[2,3,128,128]{3,2,1,0:T(8,128)(2,1)}, bf16[2,3,128,128]{3,2,1,0:T(8,128)(2,1)S(1)}, u32[]{:S(2)}, u32[]{:S(2)}) collective-permute-start(bf16[2,3,128,128]{3,2,1,0:T(8,128)(2,1)} %refs_0_.9), channel_id=1, source_target_pairs={{0,6},{1,7},{2,4},{3,5},{4,2},{5,3},{6,0},{7,1},{8,14},{9,15},{10,... | collective-permute-start | bytes 589832 | tf_op jit(solution)/shard_map/ppermute | solution.py:93
  6.6 9.9 %collective-permute-start.6 = (bf16[2,3,128,128]{3,2,1,0:T(8,128)(2,1)}, bf16[2,3,128,128]{3,2,1,0:T(8,128)(2,1)S(1)}, u32[]{:S(2)}, u32[]{:S(2)}) collective-permute-start(bf16[2,3,128,128]{3,2,1,0:T(8,128)(2,1)} %refs_0_.9), channel_id=1, source_target_pairs={{0,8},{8,0},{16,24},{24,16},{1,9},{9,1},{17,25},{25,17},{2,10},{10... | collective-permute-start | bytes 589832 | tf_op jit(solution)/shard_map/ppermute | solution.py:96
  8.1 8.3 %collective-permute-start.3 = (bf16[2,3,128,128]{3,2,1,0:T(8,128)(2,1)}, bf16[2,3,128,128]{3,2,1,0:T(8,128)(2,1)S(1)}, u32[]{:S(2)}, u32[]{:S(2)}) collective-permute-start(bf16[2,3,128,128]{3,2,1,0:T(8,128)(2,1)} %refs_0_.9), channel_id=1, source_target_pairs={{0,2},{1,3},{2,0},{3,1},{4,6},{5,7},{6,4},{7,5},{8,10},{9,11},{10,... | collective-permute-start | bytes 589832 | tf_op jit(solution)/shard_map/ppermute | solution.py:93
  9.4 1.2 %collective-permute-start.1 = (s32[4,8]{1,0:T(4,128)S(1)}, s32[4,8]{1,0:T(4,128)S(1)}, u32[]{:S(2)}, u32[]{:S(2)}) collective-permute-start(s32[4,8]{1,0:T(4,128)S(1)} %bitcast_select_fusion), channel_id=1, source_target_pairs={{0,1},{1,0},{2,3},{3,2},{4,5},{5,4},{6,7},{7,6},{8,9},{9,8},{10,11... | collective-permute-start | bytes 392 | tf_op jit(solution)/shard_map/ppermute | solution.py:93
  10.8 7.4 %collective-permute-start.4 = (bf16[2,3,128,128]{3,2,1,0:T(8,128)(2,1)}, bf16[2,3,128,128]{3,2,1,0:T(8,128)(2,1)S(1)}, u32[]{:S(2)}, u32[]{:S(2)}) collective-permute-start(bf16[2,3,128,128]{3,2,1,0:T(8,128)(2,1)} %refs_0_.9), channel_id=1, source_target_pairs={{0,4},{1,5},{2,6},{3,7},{4,0},{5,1},{6,2},{7,3},{8,12},{9,13},{10,... | collective-permute-start | bytes 589832 | tf_op jit(solution)/shard_map/ppermute | solution.py:93
  13.0 5.2 %collective-permute-start.10 = (bf16[2,3,128,128]{3,2,1,0:T(8,128)(2,1)S(1)}, bf16[2,3,128,128]{3,2,1,0:T(8,128)(2,1)S(1)}, u32[]{:S(2)}, u32[]{:S(2)}) collective-permute-start(bf16[2,3,128,128]{3,2,1,0:T(8,128)(2,1)S(1)} %collective-permute-done.5.refs_4_), channel_id=1, source_target_pairs={{0,1},{1,0},{2,3},{3,2},{4,5},{5,4},{6,7},{7,6},{8,9},{9,8},{10,11... | collective-permute-start | bytes 589832 | tf_op jit(solution)/shard_map/ppermute | solution.py:93
  14.1 6.6 %collective-permute-start.13 = (bf16[2,3,128,128]{3,2,1,0:T(8,128)(2,1)S(1)}, bf16[2,3,128,128]{3,2,1,0:T(8,128)(2,1)S(1)}, u32[]{:S(2)}, u32[]{:S(2)}) collective-permute-start(bf16[2,3,128,128]{3,2,1,0:T(8,128)(2,1)S(1)} %collective-permute-done.refs_4_), channel_id=1, source_target_pairs={{0,8},{8,0},{16,24},{24,16},{1,9},{9,1},{17,25},{25,17},{2,10},{10... | collective-permute-start | bytes 589832 | tf_op jit(solution)/shard_map/ppermute | solution.py:96
  16.5 4.3 %collective-permute-start.8 = (bf16[2,3,128,128]{3,2,1,0:T(8,128)(2,1)S(1)}, bf16[2,3,128,128]{3,2,1,0:T(8,128)(2,1)S(1)}, u32[]{:S(2)}, u32[]{:S(2)}) collective-permute-start(bf16[2,3,128,128]{3,2,1,0:T(8,128)(2,1)S(1)} %collective-permute-done.3.refs_0_), channel_id=1, source_target_pairs={{0,1},{1,0},{2,3},{3,2},{4,5},{5,4},{6,7},{7,6},{8,9},{9,8},{10,11... | collective-permute-start | bytes 589832 | tf_op jit(solution)/shard_map/ppermute | solution.py:93
  16.5 6.5 %collective-permute-start.11 = (bf16[2,3,128,128]{3,2,1,0:T(8,128)(2,1)S(1)}, bf16[2,3,128,128]{3,2,1,0:T(8,128)(2,1)S(1)}, u32[]{:S(2)}, u32[]{:S(2)}) collective-permute-start(bf16[2,3,128,128]{3,2,1,0:T(8,128)(2,1)S(1)} %collective-permute-done.6.refs_2_), channel_id=1, source_target_pairs={{0,1},{1,0},{2,3},{3,2},{4,5},{5,4},{6,7},{7,6},{8,9},{9,8},{10,11... | collective-permute-start | bytes 589832 | tf_op jit(solution)/shard_map/ppermute | solution.py:93
  18.1 3.1 %collective-permute-start.9 = (bf16[2,3,128,128]{3,2,1,0:T(8,128)(2,1)S(1)}, bf16[2,3,128,128]{3,2,1,0:T(8,128)(2,1)S(1)}, u32[]{:S(2)}, u32[]{:S(2)}) collective-permute-start(bf16[2,3,128,128]{3,2,1,0:T(8,128)(2,1)S(1)} %collective-permute-done.4.refs_2_), channel_id=1, source_target_pairs={{0,1},{1,0},{2,3},{3,2},{4,5},{5,4},{6,7},{7,6},{8,9},{9,8},{10,11... | collective-permute-start | bytes 589832 | tf_op jit(solution)/shard_map/ppermute | solution.py:93
  18.1 4.1 %collective-permute-start.7 = (bf16[2,3,128,128]{3,2,1,0:T(8,128)(2,1)}, bf16[2,3,128,128]{3,2,1,0:T(8,128)(2,1)S(1)}, u32[]{:S(2)}, u32[]{:S(2)}) collective-permute-start(bf16[2,3,128,128]{3,2,1,0:T(8,128)(2,1)} %refs_0_.9), channel_id=1, source_target_pairs={{0,1},{1,0},{2,3},{3,2},{4,5},{5,4},{6,7},{7,6},{8,9},{9,8},{10,11... | collective-permute-start | bytes 589832 | tf_op jit(solution)/shard_map/ppermute | solution.py:93
  20.8 2.2 %collective-permute-start.12 = (bf16[2,3,128,128]{3,2,1,0:T(8,128)(2,1)S(1)}, bf16[2,3,128,128]{3,2,1,0:T(8,128)(2,1)S(1)}, u32[]{:S(2)}, u32[]{:S(2)}) collective-permute-start(bf16[2,3,128,128]{3,2,1,0:T(8,128)(2,1)S(1)} %collective-permute-done.refs_4_), channel_id=1, source_target_pairs={{0,1},{1,0},{2,3},{3,2},{4,5},{5,4},{6,7},{7,6},{8,9},{9,8},{10,11... | collective-permute-start | bytes 589832 | tf_op jit(solution)/shard_map/ppermute | solution.py:93
  20.8 2.2 %collective-permute-start.14 = (bf16[2,3,128,128]{3,2,1,0:T(8,128)(2,1)S(1)}, bf16[2,3,128,128]{3,2,1,0:T(8,128)(2,1)S(1)}, u32[]{:S(2)}, u32[]{:S(2)}) collective-permute-start(bf16[2,3,128,128]{3,2,1,0:T(8,128)(2,1)S(1)} %collective-permute-done.13.refs_6_), channel_id=1, source_target_pairs={{0,1},{1,0},{2,3},{3,2},{4,5},{5,4},{6,7},{7,6},{8,9},{9,8},{10,11... | collective-permute-start | bytes 589832 | tf_op jit(solution)/shard_map/ppermute | solution.py:93
  22.2 1.2 %copy-start = (bf16[1,1,4,8,128,128]{5,4,3,2,1,0:T(8,128)(2,1)S(1)}, bf16[1,1,4,8,128,128]{5,4,3,2,1,0:T(8,128)(2,1)}, u32[]{:S(2)}) copy-start(bf16[1,1,4,8,128,128]{5,4,3,2,1,0:T(8,128)(2,1)} %param.6) | copy-start | bytes 3145732
  25.2 9.3 %collective-permute-start.17 = (bf16[2,4,128,128]{3,2,1,0:T(8,128)(2,1)S(1)}, bf16[2,4,128,128]{3,2,1,0:T(8,128)(2,1)S(1)}, u32[]{:S(2)}, u32[]{:S(2)}) collective-permute-start(bf16[2,4,128,128]{3,2,1,0:T(8,128)(2,1)S(1)} %section.7), channel_id=1, source_target_pairs={{0,6},{1,7},{2,4},{3,5},{4,2},{5,3},{6,0},{7,1},{8,14},{9,15},{10,... | collective-permute-start | bytes 786440 | tf_op jit(solution)/shard_map/ppermute | solution.py:93
  29.3 10.7 %collective-permute-start.16 = (bf16[2,4,128,128]{3,2,1,0:T(8,128)(2,1)S(1)}, bf16[2,4,128,128]{3,2,1,0:T(8,128)(2,1)S(1)}, u32[]{:S(2)}, u32[]{:S(2)}) collective-permute-start(bf16[2,4,128,128]{3,2,1,0:T(8,128)(2,1)S(1)} %section.6), channel_id=1, source_target_pairs={{0,4},{1,5},{2,6},{3,7},{4,0},{5,1},{6,2},{7,3},{8,12},{9,13},{10,... | collective-permute-start | bytes 786440 | tf_op jit(solution)/shard_map/ppermute | solution.py:93
  31.7 8.3 %collective-permute-start.15 = (bf16[2,4,128,128]{3,2,1,0:T(8,128)(2,1)S(1)}, bf16[2,4,128,128]{3,2,1,0:T(8,128)(2,1)S(1)}, u32[]{:S(2)}, u32[]{:S(2)}) collective-permute-start(bf16[2,4,128,128]{3,2,1,0:T(8,128)(2,1)S(1)} %section.5), channel_id=1, source_target_pairs={{0,2},{1,3},{2,0},{3,1},{4,6},{5,7},{6,4},{7,5},{8,10},{9,11},{10,... | collective-permute-start | bytes 786440 | tf_op jit(solution)/shard_map/ppermute | solution.py:93
